TPU v7x, 32 devices: a whole 2x2x4 slice. The times are simulated.
32 devices in a mesh: dp: 8 (over z, x), mp: 4 (over y, core).
Axes of the slice: x: 2, y: 2, z: 4, core: 2. Of those that a mesh axis runs over, the one named last changes fastest.
Arguments:
- latent: bfloat16 [65536, 512], P('dp'), may hold values from -6 to 6
- actions: bfloat16 [6, 65536], P(None, 'dp'), may hold values from -1 to 1
- task_ids: int32 [65536], P('dp'), may hold values from 0 to 79
- action_masks: int32 [80, 6], replicated, may hold values 0 or 1
- next_latent: bfloat16 [65536, 512], P('dp', 'mp'), may hold values from 0 to 0.25
- reward_bins: int32 [65536], P('dp'), may hold values from 0 to 99
- reward_frac: float32 [65536], P('dp'), may hold values from 0 to 1
- task_embed: bfloat16 [80, 96], replicated, may hold values from -6 to 6
- dyn_w1: bfloat16 [614, 1024], P(None, 'mp'), may hold values from -0.25 to 0.25
- dyn_b1: float32 [1024], P('mp'), may hold values from -3 to 3
- dyn_gain: float32 [1024], P('mp'), may hold values from 0.5 to 1.5
- dyn_shift: float32 [1024], P('mp'), may hold values from -2 to 2
- rew_w1: bfloat16 [614, 1024], P(None, 'mp'), may hold values from -0.25 to 0.25
- rew_b1: float32 [1024], P('mp'), may hold values from -3 to 3
- rew_gain: float32 [1024], P('mp'), may hold values from 0.5 to 1.5
- rew_shift: float32 [1024], P('mp'), may hold values from -2 to 2
- dyn_w2: bfloat16 [1024, 512], P('mp'), may hold values from -0.375 to 0.375
- dyn_b2: float32 [512], replicated, may hold values from -2 to 2
- rew_w2: bfloat16 [1024, 101], P('mp'), may hold values from -0.375 to 0.375
- rew_b2: float32 [101], replicated, may hold values from -2 to 2
Outputs:
- latents: bfloat16 [65536, 512], P('dp', 'mp')
- latent_grad: bfloat16 [65536, 512], P('dp', 'mp')
- losses: float32 [2], replicated
- grad_task_embed: float32 [80, 96], replicated
- grad_dyn_w1: float32 [614, 1024], P(None, 'mp')
- grad_dyn_b1: float32 [1024], P('mp')
- grad_dyn_gain: float32 [1024], P('mp')
- grad_dyn_shift: float32 [1024], P('mp')
- grad_rew_w1: float32 [614, 1024], P(None, 'mp')
- grad_rew_b1: float32 [1024], P('mp')
- grad_rew_gain: float32 [1024], P('mp')
- grad_rew_shift: float32 [1024], P('mp')
- grad_dyn_w2: float32 [1024, 512], P('mp')
- grad_dyn_b2: float32 [512], replicated
- grad_rew_w2: float32 [1024, 101], P('mp')
- grad_rew_b2: float32 [101], replicated
Inputs may be any that keep to these rules, and one draw needn't show every extreme that they name: The upper bin reward_bins + 1 is a valid bin.
All inputs are finite; a program needn't handle non-finite values.
Results may differ from a plain program's by a relative error of at most 0.024.
Values may be sent and summed in bfloat16 or wider, within the bound.
A program may use at most 192 MiB of HBM per device.

v0:
```python
import jax
import jax.numpy as jnp
from jax import lax
from jax.sharding import PartitionSpec as P

HID = 1024
GROUP = 8


CONS_COEF = 20.0
REW_COEF = 0.1


def mish_act(values):
    return values * jnp.tanh(jax.nn.softplus(values))


def contract(left, right, left_dim, right_dim):
    return lax.dot_general(
        left, right, (((left_dim,), (right_dim,)), ((), ())), preferred_element_type=jnp.float32
    )


def on_device(
    latent,
    actions,
    task_ids,
    action_masks,
    next_latent,
    reward_bins,
    reward_frac,
    task_embed,
    dyn_w1,
    dyn_b1,
    dyn_gain,
    dyn_shift,
    rew_w1,
    rew_b1,
    rew_gain,
    rew_shift,
    dyn_w2,
    dyn_b2,
    rew_w2,
    rew_b2,
):
    tok_rows = latent.shape[0]
    shard_width = dyn_w1.shape[1]
    share_width = next_latent.shape[1]
    n_model = lax.axis_size("mp")
    total_rows = tok_rows * lax.axis_size("dp")
    mp_index = lax.axis_index("mp")
    lat_width = latent.shape[1]
    act_width = actions.shape[0]
    onehot = (
        task_ids[:, None] == jnp.arange(task_embed.shape[0], dtype=jnp.int32)[None, :]
    ).astype(jnp.bfloat16)
    embedded = jnp.dot(onehot, task_embed, preferred_element_type=jnp.float32).astype(jnp.bfloat16)
    mask_cols = contract(action_masks.astype(jnp.bfloat16), onehot, 0, 1)
    masked = (actions.astype(jnp.float32) * mask_cols).astype(jnp.bfloat16)
    w_first = jnp.concatenate([dyn_w1, rew_w1], axis=1)
    w_lat = w_first[:lat_width]
    w_act = w_first[lat_width : lat_width + act_width]
    w_task = w_first[lat_width + act_width :]
    bias_pair = jnp.concatenate([dyn_b1, rew_b1])
    pre_act = (
        jnp.dot(latent, w_lat, preferred_element_type=jnp.float32)
        + contract(masked, w_act, 0, 0)
        + jnp.dot(embedded, w_task, preferred_element_type=jnp.float32)
        + bias_pair
    )
    pre_act = pre_act.reshape(tok_rows, 2, shard_width)
    first_sum, second_sum = lax.psum(
        (jnp.sum(pre_act, axis=2).T, jnp.sum(pre_act * pre_act, axis=2).T), "mp"
    )
    average = first_sum / HID
    variance = second_sum / HID - average * average
    inv_std = lax.rsqrt(variance + 1e-05).T[:, :, None]
    normalized = (pre_act - average.T[:, :, None]) * inv_std
    gain_pair = jnp.stack([dyn_gain, rew_gain])
    shift_pair = jnp.stack([dyn_shift, rew_shift])
    normed = normalized * gain_pair + shift_pair
    hidden = mish_act(normed).astype(jnp.bfloat16)
    hidden_dyn = hidden[:, 0]
    hidden_rew = hidden[:, 1]
    lat_part = jnp.dot(hidden_dyn, dyn_w2, preferred_element_type=jnp.float32).astype(jnp.bfloat16)
    lat_share = lax.psum_scatter(lat_part, "mp", scatter_dimension=1, tiled=True).astype(
        jnp.float32
    )
    lat_share = lat_share + lax.dynamic_slice_in_dim(dyn_b2, mp_index * share_width, share_width)
    logit_part = jnp.dot(hidden_rew, rew_w2, preferred_element_type=jnp.float32)
    logits = lax.psum(logit_part, "mp") + rew_b2
    groups = lat_share.reshape(tok_rows, share_width // GROUP, GROUP)
    simplex = jax.nn.softmax(groups, axis=-1)
    latents_out = simplex.reshape(tok_rows, share_width)
    lat_error = latents_out - next_latent.astype(jnp.float32)
    cons_part = jnp.sum(lat_error * lat_error)
    log_probs = jax.nn.log_softmax(logits, axis=-1)
    bin_iota = jnp.arange(logits.shape[1], dtype=jnp.int32)[None, :]
    target = jnp.where(bin_iota == reward_bins[:, None], 1.0 - reward_frac[:, None], 0.0)
    target = target + jnp.where(bin_iota == reward_bins[:, None] + 1, reward_frac[:, None], 0.0)
    rew_part = -jnp.sum(target * log_probs) / n_model
    d_groups = (2.0 * CONS_COEF / total_rows * lat_error).reshape(groups.shape)
    d_lat = simplex * (d_groups - jnp.sum(simplex * d_groups, axis=-1, keepdims=True))
    d_share = d_lat.reshape(tok_rows, share_width).astype(jnp.bfloat16)
    d_full = lax.all_gather(d_share, "mp", axis=1, tiled=True)
    d_logits = (REW_COEF / total_rows * (jnp.exp(log_probs) - target)).astype(jnp.bfloat16)
    grad_w2_dyn = contract(hidden_dyn, d_full, 0, 0)
    grad_b2_dyn = jnp.sum(d_full.astype(jnp.float32), axis=0)
    grad_w2_rew = contract(hidden_rew, d_logits, 0, 0)
    grad_b2_rew = jnp.sum(d_logits.astype(jnp.float32), axis=0)
    head_grads = (grad_w2_dyn, grad_b2_dyn, grad_w2_rew, grad_b2_rew)
    d_hid_dyn = contract(d_full, dyn_w2, 1, 1)
    d_hid_rew = contract(d_logits, rew_w2, 1, 1)
    d_hidden = jnp.stack([d_hid_dyn, d_hid_rew], axis=1)
    unused_value, mish_back = jax.vjp(mish_act, normed)
    d_normed = mish_back(d_hidden)[0]
    grad_gain = jnp.sum(d_normed * normalized, axis=0)
    grad_shift = jnp.sum(d_normed, axis=0)
    d_unit = d_normed * gain_pair
    back_first, back_second = lax.psum(
        (jnp.sum(d_unit, axis=2).T, jnp.sum(d_unit * normalized, axis=2).T), "mp"
    )
    d_pre = inv_std * (
        d_unit - (back_first.T / HID)[:, :, None] - normalized * (back_second.T / HID)[:, :, None]
    )
    d_pre = d_pre.reshape(tok_rows, 2 * shard_width).astype(jnp.bfloat16)
    grad_b1 = jnp.sum(d_pre.astype(jnp.float32), axis=0)
    grad_w_lat = contract(latent, d_pre, 0, 0)
    grad_w_act = jnp.dot(masked, d_pre, preferred_element_type=jnp.float32)
    task_sums = contract(onehot, d_pre, 0, 0)
    grad_w_task = jnp.dot(
        task_embed.astype(jnp.float32).T, task_sums, precision=lax.Precision.HIGHEST
    )
    embed_part = jnp.dot(task_sums, w_task.astype(jnp.float32).T, precision=lax.Precision.HIGHEST)
    grad_w1 = jnp.concatenate([grad_w_lat, grad_w_act, grad_w_task], axis=0)
    input_part = contract(d_pre, w_lat, 1, 1).astype(jnp.bfloat16)
    input_share = lax.psum_scatter(input_part, "mp", scatter_dimension=1, tiled=True).astype(
        jnp.float32
    )
    latent_grad = (input_share * total_rows).astype(jnp.bfloat16)
    cons_sum, rew_sum, grad_embed = lax.psum((cons_part, rew_part, embed_part), ("dp", "mp"))
    losses = jnp.stack([cons_sum, rew_sum]) / total_rows
    summed = lax.psum(
        (
            grad_w1,
            grad_b1,
            grad_gain,
            grad_shift,
            head_grads[0],
            head_grads[1],
            head_grads[2],
            head_grads[3],
        ),
        "dp",
    )
    grad_w1, grad_b1, grad_gain, grad_shift = (summed[0], summed[1], summed[2], summed[3])
    head_grads = (summed[4], summed[5], summed[6], summed[7])
    return (
        latents_out.astype(jnp.bfloat16),
        latent_grad,
        losses,
        grad_embed,
        grad_w1[:, :shard_width],
        grad_b1[:shard_width],
        grad_gain[0],
        grad_shift[0],
        grad_w1[:, shard_width:],
        grad_b1[shard_width:],
        grad_gain[1],
        grad_shift[1],
        head_grads[0],
        head_grads[1],
        head_grads[2],
        head_grads[3],
    )


def solution(mesh):
    return jax.shard_map(
        on_device,
        mesh=mesh,
        in_specs=(
            P("dp", None),
            P(None, "dp"),
            P("dp"),
            P(),
            P("dp", "mp"),
            P("dp"),
            P("dp"),
            P(),
            P(None, "mp"),
            P("mp"),
            P("mp"),
            P("mp"),
            P(None, "mp"),
            P("mp"),
            P("mp"),
            P("mp"),
            P("mp", None),
            P(),
            P("mp", None),
            P(),
        ),
        out_specs=(
            P("dp", "mp"),
            P("dp", "mp"),
            P(),
            P(),
            P(None, "mp"),
            P("mp"),
            P("mp"),
            P("mp"),
            P(None, "mp"),
            P("mp"),
            P("mp"),
            P("mp"),
            P("mp", None),
            P(),
            P("mp", None),
            P(),
        ),
        check_vma=False,
    )
```

profile of v0, /device:TPU:0, one launch (start us, length us, event | category | flops | bytes accessed | tf_op | source)
XLA Modules:
  0.0 630.1 jit_solution(13819635788461500749)
XLA Ops:
  10.0 11.8 %fusion.39 = f32[512,8192]{1,0:T(8,128)} fusion(bf16[8192,512]{1,0:T(8,128)(2,1)} %param.20, bf16[614,512]{1,0:T(8,128)(2,1)S(1)} %constant_dynamic-update-slice_fusion), kind=kOutput, calls=%fused_computation.95 | convolution fusion | flops 4294967296 | bytes 25690112 | tf_op jit(solution)/shard_map/dot_general | solution.py:66
  21.8 7.3 %fusion.33 = f32[8192,512]{0,1:T(8,128)} fusion(bf16[80,96]{1,0:T(8,128)(2,1)S(1)} %copy-done.21, s32[8192]{0:T(1024)S(1)} %copy-done.16, bf16[614,512]{1,0:T(8,128)(2,1)S(1)} %constant_dynamic-update-slice_fusion), kind=kOutput, calls=%fused_computation.87 | convolution fusion | flops 932577280 | bytes 16928768 | tf_op jit(solution)/shard_map/dot_general | solution.py:68
  29.7 19.8 %bitcast_reduce_fusion = (f32[8192,2]{0,1:T(2,128)}, f32[8192,2]{0,1:T(2,128)}, f32[8192,512]{0,1:T(8,128)}) fusion(f32[512]{0:T(512)S(1)} %pad_maximum_fusion.2, f32[8192,512]{0,1:T(8,128)} %fusion.33, bf16[6,8192]{1,0:T(8,128)(2,1)S(1)} %fusion.23, bf16[614,512]{1,0:T(8,128)(2,1)S(1)} %constant_dynamic-update-slice_fusion, f32[512,8192]{1,0:T(8,128)} %fusion.39), kind=kOutput, calls=%fused_computation.29 | convolution fusion | flops 75464704 | bytes 50604032 | tf_op jit(solution)/shard_map/dot_general | solution.py:19
  49.9 34.0 %all-reduce.16.cloned.1.call-done = (f32[2,8192]{1,0:T(2,128)}, f32[2,8192]{1,0:T(2,128)}) async-done(((f32[2,8192]{1,0:T(2,128)}, f32[2,8192]{1,0:T(2,128)}), (f32[2,8192]{1,0:T(2,128)}, f32[2,8192]{1,0:T(2,128)})) %all-reduce.16.cloned.1.call-update) | async-done | bytes 131088 | tf_op jit(solution)/shard_map/psum | solution.py:72
  84.9 14.7 %fusion.17 = bf16[8192,2,256]{0,2,1:T(8,128)(2,1)S(1)} fusion(f32[8192,512]{0,1:T(8,128)} %get-tuple-element.93, f32[2,256]{1,0:T(2,128)S(1)} %get-tuple-element.92, f32[2,256]{1,0:T(2,128)S(1)} %get-tuple-element.94, f32[8192,2]{0,1:T(2,128)S(1)} %get-tuple-element.82, f32[8192,2]{0,1:T(2,128)S(1)} %get-tuple-element.81), kind=kLoop, calls=%fused_computation.41 | loop fusion | flops 50331648 | bytes 25300992 | tf_op jit(solution)/shard_map/convert_element_type | solution.py:82
  99.6 3.2 copy-done.4
  102.8 5.6 convolution_convert_fusion.1
  108.4 12.1 %copy.47 = bf16[8192,512]{0,1:T(8,128)(2,1)} copy(bf16[8192,512]{1,0:T(8,128)(2,1)} %convolution_convert_fusion.1) | data formatting | bytes 16777216
  124.3 5.6 fusion.29
  130.2 62.2 %reduce-scatter.7.cloned.1.call-done = bf16[128,8192]{1,0:T(8,128)(2,1)} async-done(((bf16[512,8192]{1,0:T(8,128)(2,1)}), bf16[128,8192]{1,0:T(8,128)(2,1)}) %reduce-scatter.7.cloned.1.call-update) | async-done | bytes 2097168
  195.4 3.4 fusion.26
  198.8 7.2 %fusion.21 = bf16[8192,128]{0,1:T(8,128)(2,1)} fusion(bf16[8192,128]{0,1:T(8,128)(2,1)S(1)} %copy.45, bf16[128,8192]{1,0:T(8,128)(2,1)} %reduce-scatter.7.cloned.1.call-done, f32[8192,16]{0,1:T(8,128)S(1)} %fusion.26, f32[8192,16]{0,1:T(8,128)S(1)} %bitcast_reduce_fusion.1, f32[128]{0:T(128)} %copy-done.24), kind=kOutput, calls=%fused_computation.52 | output fusion | flops 21102600 | bytes 7340544 | tf_op jit(solution)/shard_map/sub | solution.py:103
  208.0 59.5 %all-reduce.10.cloned.1.call-done = f32[8192,101]{0,1:T(8,128)} async-done(((f32[8192,101]{0,1:T(8,128)}), f32[8192,101]{0,1:T(8,128)}) %all-reduce.10.cloned.1.call-update) | async-done | bytes 3309584 | tf_op jit(solution)/shard_map/psum | solution.py:91
  272.7 4.0 convert_reduce_fusion.2
  276.7 5.9 convolution_bitcast_fusion.1
  284.7 43.2 %all-gather.2.cloned.1.call-done = bf16[8192,512]{0,1:T(8,128)(2,1)} async-done(((bf16[8192,128]{0,1:T(8,128)(2,1)}), bf16[8192,512]{0,1:T(8,128)(2,1)}) %all-gather.2.cloned.1.call-update) | async-done | bytes 8388624 | tf_op jit(solution)/shard_map/all_gather | solution.py:105
  328.0 9.2 %convolution_bitcast_fusion = f32[8192,1,256]{0,2,1:T(8,128)} fusion(bf16[256,512]{1,0:T(8,128)(2,1)S(1)} %copy-done, bf16[8192,512]{0,1:T(8,128)(2,1)} %all-gather.2.cloned.1.call-done), kind=kOutput, calls=%fused_computation.47 | convolution fusion | flops 2147483648 | bytes 17039360 | tf_op jit(solution)/shard_map/dot_general | solution.py:19
  337.2 29.3 %pad_maximum_fusion = (f32[8192,2,256]{0,2,1:T(8,128)}, f32[8192,2,256]{0,2,1:T(8,128)}) fusion(f32[8192,1,256]{0,2,1:T(8,128)} %convolution_bitcast_fusion.1, f32[8192,1,256]{0,2,1:T(8,128)} %convolution_bitcast_fusion, f32[2,256]{1,0:T(2,128)S(1)} %get-tuple-element.92, f32[2,256]{1,0:T(2,128)S(1)} %get-tuple-element.94, ...), kind=kLoop, calls=%fused_computation.19 | loop fusion | flops 104857600 | bytes 67244032 | tf_op jit(solution)/shard_map/stack | solution.py:114
  366.5 8.7 %fusion.51 = (f32[8192,2]{0,1:T(2,128)}, f32[8192,2]{0,1:T(2,128)}) fusion(f32[8192,2,256]{0,2,1:T(8,128)} %get-tuple-element.75, f32[8192,2]{0,1:T(2,128)S(1)} %get-tuple-element.82, f32[8192,2]{0,1:T(2,128)S(1)} %get-tuple-element.81, f32[8192,512]{0,1:T(8,128)S(1)} %bitcast.218), kind=kLoop, calls=%fused_computation.119 | loop fusion | flops 20938752 | bytes 33816576 | tf_op jit(solution)/shard_map/reduce_sum | solution.py:121
  375.3 7.8 %fusion.27 = f32[256,512]{1,0:T(8,128)} fusion(bf16[8192,512]{0,1:T(8,128)(2,1)} %all-gather.2.cloned.1.call-done, bf16[8192,2,256]{0,2,1:T(8,128)(2,1)} %copy-done.4), kind=kOutput, calls=%fused_computation.71 | convolution fusion | flops 2147483648 | bytes 13107200 | tf_op jit(solution)/shard_map/dot_general | solution.py:19
  383.1 28.7 %fusion.50 = (f32[512]{0:T(512)S(1)}, f32[512]{0:T(512)S(1)}, f32[8192,512]{0,1:T(8,128)}) fusion(f32[8192,2]{0,1:T(2,128)S(1)} %get-tuple-element.82, f32[8192,512]{0,1:T(8,128)} %get-tuple-element.93, f32[8192,2]{0,1:T(2,128)S(1)} %get-tuple-element.81, f32[512]{0:T(512)S(1)} %bitcast.230, f32[512]{0:T(512)S(1)} %bitcast.228, ...), kind=kLoop, calls=%fused_computation.118 | loop fusion | flops 109050880 | bytes 50470912 | tf_op jit(solution)/shard_map/reduce_sum | solution.py:118
  413.5 12.9 %convert_reduce_fusion.1 = (f32[512]{0:T(512)S(1)}, bf16[8192,512]{0,1:T(8,128)(2,1)S(1)}) fusion(f32[8192,2]{0,1:T(2,128)S(1)} %multiply_bitcast_fusion, f32[8192,512]{0,1:T(8,128)} %get-tuple-element.93, f32[8192,2]{0,1:T(2,128)S(1)} %get-tuple-element.81, f32[8192,2]{0,1:T(2,128)S(1)} %multiply_bitcast_fusion.1, f32[8192,512]{0,1:T(8,128)} %get-tuple-element.71, ...), kind=kLoop, calls=%fused_computation.37 | loop fusion | flops 41942528 | bytes 42209280 | tf_op jit(solution)/shard_map/reduce_sum | solution.py:127
  432.4 9.7 %convolution_bitcast_fusion.3 = f32[512,512]{1,0:T(8,128)S(1)} fusion(bf16[8192,512]{0,1:T(8,128)(2,1)} %copy-done.2, bf16[8192,512]{1,0:T(8,128)(2,1)} %param.20), kind=kOutput, calls=%fused_computation.88 | convolution fusion | flops 4294967296 | bytes 17825792 | tf_op jit(solution)/shard_map/dot_general | solution.py:19
  443.7 10.3 %convolution_convert_fusion = bf16[8192,512]{1,0:T(8,128)(2,1)} fusion(bf16[8192,512]{0,1:T(8,128)(2,1)} %copy-done.2, bf16[614,512]{1,0:T(8,128)(2,1)S(1)} %copy-done.8), kind=kOutput, calls=%fused_computation.45 | convolution fusion | flops 4299161600 | bytes 17301504 | tf_op jit(solution)/shard_map/dot_general | solution.py:19
  453.9 11.8 %copy.49 = bf16[8192,512]{0,1:T(8,128)(2,1)} copy(bf16[8192,512]{1,0:T(8,128)(2,1)} %convolution_convert_fusion) | data formatting | bytes 16777216
  467.4 4.5 multiply_reduce_fusion.2
  471.9 4.1 copy.46
  476.0 4.8 convert_reduce_fusion
  481.9 41.2 %all-reduce = (f32[1]{0:T(128)}, f32[1]{0:T(128)}, f32[80,96]{1,0:T(8,128)}) all-reduce(f32[1]{0:T(128)} %bitcast.30, f32[1]{0:T(128)} %bitcast.29, f32[80,96]{1,0:T(8,128)S(1)} %fusion.41), channel_id=1, replica_groups=mesh['dp'=8,'mp'=4] {'dp','mp'}, use_global_device_ids=true, to_apply=%region_19.20 | all-reduce | flops 7682 | bytes 61456 | tf_op jit(solution)/shard_map/psum | solution.py:141
  523.1 22.9 %all-reduce.1 = (f32[512]{0:T(512)S(1)}, f32[2,256]{1,0:T(2,128)S(1)}, f32[2,256]{1,0:T(2,128)S(1)}, f32[512]{0:T(512)}, f32[101]{0:T(128)}) all-reduce(f32[512]{0:T(512)S(1)} %get-tuple-element.72, f32[2,256]{1,0:T(2,128)S(1)} %reduce_sum.142, f32[2,256]{1,0:T(2,128)S(1)} %reduce_sum.144, ...), channel_id=1, replica_groups=mesh['dp'=8,'mp'=4] {'dp'}, use_global_device_ids=true, to_apply=%region_23.24 | all-reduce | flops 2149 | bytes 17192 | tf_op jit(solution)/shard_map/psum | solution.py:143
  552.2 64.2 %reduce-scatter.9.cloned.1.call-done = bf16[128,8192]{1,0:T(8,128)(2,1)} async-done(((bf16[512,8192]{1,0:T(8,128)(2,1)}), bf16[128,8192]{1,0:T(8,128)(2,1)}) %reduce-scatter.9.cloned.1.call-update) | async-done | bytes 2097168
  616.4 3.2 copy.50
  (127 shorter events, 41.5 us)
Async XLA Ops:
  7.2 95.6 %copy-start = (bf16[256,512]{1,0:T(8,128)(2,1)S(1)}, bf16[256,512]{1,0:T(8,128)(2,1)}, u32[]{:S(2)}) copy-start(bf16[256,512]{1,0:T(8,128)(2,1)} %param.36) | copy-start | bytes 786436
  7.2 76.7 %all-reduce.16.cloned.1.call-start = ((), (), s32[]{:S(2)}) async-start(), calls=%async_computation.8 | async-start | bytes 262144 | tf_op jit(solution)/shard_map/psum | solution.py:72
  10.0 19.7 %copy-start.7 = (bf16[614,512]{1,0:T(8,128)(2,1)}, bf16[614,512]{1,0:T(8,128)(2,1)S(1)}, u32[]{:S(2)}) copy-start(bf16[614,512]{1,0:T(8,128)(2,1)S(1)} %constant_dynamic-update-slice_fusion) | copy-start | bytes 1886212
  10.0 11.8 %copy-start.16 = (s32[8192]{0:T(1024)S(1)}, s32[8192]{0:T(1024)}, u32[]{:S(2)}) copy-start(s32[8192]{0:T(1024)} %param.22) | copy-start | bytes 98308
  10.0 11.8 %copy-start.21 = (bf16[80,96]{1,0:T(8,128)(2,1)S(1)}, bf16[80,96]{1,0:T(8,128)(2,1)}, u32[]{:S(2)}) copy-start(bf16[80,96]{1,0:T(8,128)(2,1)} %param.27) | copy-start | bytes 46084
  29.6 19.9 %copy-start.11 = (bf16[6,8192]{1,0:T(8,128)(2,1)}, bf16[6,8192]{1,0:T(8,128)(2,1)S(1)}, u32[]{:S(2)}) copy-start(bf16[6,8192]{1,0:T(8,128)(2,1)S(1)} %fusion.23) | copy-start | bytes 294916
  29.6 20.2 %copy-start.26 = (f32[256]{0:T(256)S(1)}, f32[256]{0:T(256)}, u32[]{:S(2)}) copy-start(f32[256]{0:T(256)} %param.35) | copy-start | bytes 3076
  29.6 20.2 %copy-start.27 = (f32[256]{0:T(256)S(1)}, f32[256]{0:T(256)}, u32[]{:S(2)}) copy-start(f32[256]{0:T(256)} %param.31) | copy-start | bytes 3076
  29.7 20.2 %copy-start.28 = (f32[256]{0:T(256)S(1)}, f32[256]{0:T(256)}, u32[]{:S(2)}) copy-start(f32[256]{0:T(256)} %param.34) | copy-start | bytes 3076
  29.7 20.2 %copy-start.29 = (f32[256]{0:T(256)S(1)}, f32[256]{0:T(256)}, u32[]{:S(2)}) copy-start(f32[256]{0:T(256)} %param.30) | copy-start | bytes 3076
  49.6 142.8 %reduce-scatter.7.cloned.1.call-start = ((), (), s32[]{:S(2)}) async-start(), calls=%async_computation.4 | async-start | bytes 10485760
  120.5 147.0 %all-reduce.10.cloned.1.call-start = ((), (), s32[]{:S(2)}) async-start(), calls=%async_computation.3 | async-start | bytes 6815744 | tf_op jit(solution)/shard_map/psum | solution.py:91
  123.5 75.3 %copy-start.6 = (bf16[8192,128]{0,1:T(8,128)(2,1)}, bf16[8192,128]{0,1:T(8,128)(2,1)S(1)}, u32[]{:S(2)}) copy-start(bf16[8192,128]{0,1:T(8,128)(2,1)S(1)} %copy.45) | copy-start | bytes 6291460
  124.3 68.1 %copy-start.24 = (f32[128]{0:T(128)}, f32[128]{0:T(128)S(1)}, u32[]{:S(2)}) copy-start(f32[128]{0:T(128)S(1)} %dynamic_slice.3) | copy-start | bytes 1540
  129.9 198.0 %all-gather.2.cloned.1.call-start = ((), (), s32[]{:S(2)}) async-start(), calls=%async_computation.2 | async-start | bytes 10485760 | tf_op jit(solution)/shard_map/all_gather | solution.py:105
  205.9 66.8 %copy-start.18 = (f32[8192]{0:T(1024)S(1)}, f32[8192]{0:T(1024)}, u32[]{:S(2)}) copy-start(f32[8192]{0:T(1024)} %param.26) | copy-start | bytes 98308
  205.9 66.8 %copy-start.19 = (s32[8192]{0:T(1024)S(1)}, s32[8192]{0:T(1024)}, u32[]{:S(2)}) copy-start(s32[8192]{0:T(1024)} %param.25) | copy-start | bytes 98308
  205.9 66.8 %copy-start.23 = (f32[101]{0:T(128)S(1)}, f32[101]{0:T(128)}, u32[]{:S(2)}) copy-start(f32[101]{0:T(128)} %param.39) | copy-start | bytes 1216
  205.9 70.8 %copy-start.15 = (bf16[256,101]{0,1:T(8,128)(2,1)S(1)}, bf16[256,101]{0,1:T(8,128)(2,1)}, u32[]{:S(2)}) copy-start(bf16[256,101]{0,1:T(8,128)(2,1)} %param.38) | copy-start | bytes 155140
  206.0 205.8 %all-reduce.14.cloned.1.call-start = ((), (), s32[]{:S(2)}) async-start(), calls=%async_computation.7 | async-start | bytes 262144 | tf_op jit(solution)/shard_map/psum | solution.py:120
  272.7 10.0 %slice-start.4 = ((s8[8388608]{0:T(1024)(128)(4,1)}), s8[4194304]{0:T(1024)(128)(4,1)S(1)}, s32[]{:S(2)}) async-start(s8[8388608]{0:T(1024)(128)(4,1)} %bitcast.221), calls=%async_computation.13 | async-start | bytes 8388608
  328.0 38.5 %slice-start = ((s8[16777216]{0:T(1024)(128)(4,1)}), s8[4194304]{0:T(1024)(128)(4,1)S(1)}, s32[]{:S(2)}) async-start(s8[16777216]{0:T(1024)(128)(4,1)} %bitcast.217), calls=%async_computation.9 | async-start | bytes 8388608
  337.2 29.3 %slice-start.1 = ((s8[16777216]{0:T(1024)(128)(4,1)}), s8[4194304]{0:T(1024)(128)(4,1)S(1)}, s32[]{:S(2)}) async-start(s8[16777216]{0:T(1024)(128)(4,1)} %bitcast.217), calls=%async_computation.10 | async-start | bytes 8388608
  337.2 29.3 %slice-start.2 = ((s8[16777216]{0:T(1024)(128)(4,1)}), s8[4194304]{0:T(1024)(128)(4,1)S(1)}, s32[]{:S(2)}) async-start(s8[16777216]{0:T(1024)(128)(4,1)} %bitcast.217), calls=%async_computation.11 | async-start | bytes 8388608
  337.2 29.3 %slice-start.3 = ((s8[16777216]{0:T(1024)(128)(4,1)}), s8[4194304]{0:T(1024)(128)(4,1)S(1)}, s32[]{:S(2)}) async-start(s8[16777216]{0:T(1024)(128)(4,1)} %bitcast.217), calls=%async_computation.12 | async-start | bytes 8388608
  375.2 174.5 %all-reduce.12.cloned.1.call-start = ((), (), s32[]{:S(2)}) async-start(), calls=%async_computation.6 | async-start | bytes 3784704 | tf_op jit(solution)/shard_map/psum | solution.py:143
  413.5 13.0 %copy-start.12 = (bf16[6,8192]{1,0:T(8,128)(2,1)S(1)}, bf16[6,8192]{1,0:T(8,128)(2,1)}, u32[]{:S(2)}) copy-start(bf16[6,8192]{1,0:T(8,128)(2,1)} %copy-done.11) | copy-start | bytes 294916
  432.4 11.3 %copy-start.8 = (bf16[614,512]{1,0:T(8,128)(2,1)S(1)}, bf16[614,512]{1,0:T(8,128)(2,1)}, u32[]{:S(2)}) copy-start(bf16[614,512]{1,0:T(8,128)(2,1)} %copy-done.7) | copy-start | bytes 1886212
  443.6 172.8 %reduce-scatter.9.cloned.1.call-start = ((), (), s32[]{:S(2)}) async-start(), calls=%async_computation.5 | async-start | bytes 10485760
  476.0 146.8 %copy-start.1 = (bf16[256,512]{1,0:T(8,128)(2,1)S(1)}, bf16[256,512]{1,0:T(8,128)(2,1)}, u32[]{:S(2)}) copy-start(bf16[256,512]{1,0:T(8,128)(2,1)} %param.36) | copy-start | bytes 786436
  549.7 71.7 %copy-start.13 = (f32[256,512]{1,0:T(8,128)S(1)}, f32[256,512]{1,0:T(8,128)}, u32[]{:S(2)}) copy-start(f32[256,512]{1,0:T(8,128)} %get-tuple-element.108) | copy-start | bytes 1572868
  549.7 72.5 %copy-start.20 = (f32[256,101]{0,1:T(8,128)S(1)}, f32[256,101]{0,1:T(8,128)}, u32[]{:S(2)}) copy-start(f32[256,101]{0,1:T(8,128)} %get-tuple-element.110) | copy-start | bytes 310276
  (13 other events, 70.9 us)
Sparse Core Ops, SparseCore 0:
  49.7 34.1 all-reduce.15
  120.6 71.7 reduce-scatter.6
  194.8 72.6 all-reduce.9
  269.5 58.3 all-gather.1
  375.3 31.5 all-reduce.13
  443.7 98.5 all-reduce.11
  544.9 71.4 reduce-scatter.8
where the time goes:
time: 637 us; the launch traced here: 630 us
  waiting for transfers between devices  263 us (41%)
  other arithmetic  136 us (21%)
  matrix products  102 us (16%)
  blocking collectives  64.2 us (10%)
  local copies, waits for them, and re-layouts  47.8 us (8%)
  between operations  15.8 us (2%)
    unnamed x9, waiting for transfers between devices  126 us
    dot_general x9, matrix products, contract(): lax.dot_general(left, right, (((left_dim,), (right_dim,)), ((), ())), pre...  68 us
    psum x1, waiting for transfers between devices, on_device(): logits = lax.psum(logit_part, 'mp') + rew_b2  59.5 us
    all_gather x1, waiting for transfers between devices, on_device(): d_full = lax.all_gather(d_share, 'mp', axis=1, tiled=True)  43.2 us
    unnamed x86, local copies, waits for them, and re-layouts  41.7 us
    psum x1, blocking collectives, on_device(): lax.psum((cons_part, rew_part, embed_part), ('dp', 'mp'))  41.2 us
    psum x1, waiting for transfers between devices, on_device(): lax.psum((jnp.sum(pre_act, axis=2).T, jnp.sum(pre_act * pre_act, axis=2)....  34 us
    another operation x1, other arithmetic, on_device(): d_hidden = jnp.stack([d_hid_dyn, d_hid_rew], axis=1)  29.3 us
  transfers between devices with their start and end apart: 7, of which 5 were waited for; matrix products, arithmetic and copies ran while one was open for 19% of the time, Pallas kernels for 0%

commit v1 on v0

v1 whole, which is shorter than its diff:
```python
import functools

import jax
import jax.numpy as jnp
from jax import lax
from jax.experimental import pallas as pl
from jax.experimental.pallas import tpu as pltpu
from jax.sharding import PartitionSpec as P

GROUP = 8
CONS_COEF = 20.0
REW_COEF = 0.1
EPS = 1e-05
LANES = 128
TILE = 512
SUB = 64
MESH = pl.DeviceIdType.MESH
F32 = jnp.float32
BF16 = jnp.bfloat16


def dot(left, right, left_dim=1, right_dim=0):
    return lax.dot_general(
        left, right, (((left_dim,), (right_dim,)), ((), ())), preferred_element_type=F32
    )


def aligned(start, size):
    return pl.ds(pl.multiple_of(start, size), size)


def split_dot(left, right, left_dim, right_dim):
    high = left.astype(BF16)
    low = (left - high.astype(F32)).astype(BF16)
    return dot(high, right, left_dim, right_dim) + dot(low, right, left_dim, right_dim)


def main_kernel(
    sizes,
    latent_in,
    next_in,
    w1_in,
    w2t_in,
    rw2t_in,
    vecs_in,
    ids_ref,
    act_ref,
    masks_ref,
    bins_ref,
    frac_ref,
    embed_ref,
    b2_ref,
    rb2_ref,
    lat_out,
    grad_out,
    ga_ref,
    gb_ref,
    gs_ref,
    ge_ref,
    x_all,
    x_t,
    w1_raw,
    w1_c,
    w2_t,
    rw2_t,
    vecs,
    next_lat,
    dpl,
    dpl_send,
    lat_stage,
    lg_stage,
    d_rew,
    g1,
    g2t,
    rg2t,
    pre,
    dh,
    dm,
    hid,
    d_pre,
    zt,
    latt,
    dlog,
    inv_ref,
    col_acc,
    sum_acc,
    row_acc,
    b2_acc,
    load_sem,
    w_send,
    w_recv,
    n_send,
    n_recv,
    d_send,
    d_recv,
    l_local,
    l_send,
    l_recv,
    g_local,
    g_send,
    g_recv,
):
    n_mp, total_rows, hid_width = sizes
    mine = lax.axis_index("mp")
    pair = mine // 2
    half = mine % 2
    own_rows = x_all.shape[0] // 2
    lat_width = latent_in.shape[1]
    shard = w1_in.shape[2]
    share = next_in.shape[1]
    n_task = embed_ref.shape[0]
    chip_cols = 2 * share
    n_tiles = own_rows // TILE
    n_lane = hid_width // LANES

    def peer_of(flip):
        near = mine + 1 - 2 * half
        if flip == 1:
            return near
        across = 2 * (1 - pair)
        return across + half if flip == 2 else across + 1 - half

    def rows_of(device):
        return aligned(device * own_rows, own_rows)

    barrier = pltpu.get_barrier_semaphore()
    for flip in (1, 2, 3):
        pl.semaphore_signal(
            barrier, inc=1, device_id={"mp": peer_of(flip)}, device_id_type=MESH
        )
    pl.semaphore_wait(barrier, 3)

    near, across = peer_of(1), peer_of(2)

    w_pairs = []
    for net in range(2):
        cols = aligned(net * hid_width + mine * shard, shard)
        w_pairs.append((w1_in.at[net], w1_raw.at[:, cols], net))
        w_pairs.append((vecs_in.at[net], vecs.at[:, cols], net))
    block = aligned(mine * shard, shard)
    w_pairs.append((w2t_in, w2_t.at[:, block], 0))
    w_pairs.append((rw2t_in, rw2_t.at[:, block], 1))
    order = [0, 1, 4, 2, 3, 5]

    def weight_copy(index, flip):
        source, target, _ = w_pairs[index]
        return pltpu.make_async_remote_copy(
            src_ref=source,
            dst_ref=target,
            send_sem=w_send.at[flip - 1, index],
            recv_sem=w_recv.at[flip - 1, index],
            device_id={"mp": peer_of(flip)},
            device_id_type=MESH,
        )

    def next_copy(slot):
        rows = near if slot == 1 else peer_of(3)
        return pltpu.make_async_remote_copy(
            src_ref=next_in.at[rows_of(rows), :],
            dst_ref=next_lat.at[slot, half],
            send_sem=n_send.at[slot],
            recv_sem=n_recv.at[slot],
            device_id={"mp": near},
            device_id_type=MESH,
        )

    loads = []
    for slot, device in ((0, across), (1, mine)):
        loads.append(
            (
                latent_in.at[rows_of(device), :],
                x_all.at[pl.ds(slot * own_rows, own_rows), pl.ds(0, lat_width)],
            )
        )
    for slot, device in ((0, across), (1, mine)):
        loads.append((next_in.at[rows_of(device), :], next_lat.at[slot, half]))
    for source, target, _ in w_pairs:
        loads.append((source, target))
    loads = [
        pltpu.make_async_copy(source, target, load_sem.at[i])
        for i, (source, target) in enumerate(loads)
    ]
    for copy in loads:
        copy.start()
    for index in order:
        for flip in (2, 3, 1):
            weight_copy(index, flip).start()
    next_copy(0).start()
    next_copy(1).start()

    for ref in (g1, g2t, rg2t, col_acc, sum_acc, row_acc, b2_acc):
        ref[...] = jnp.zeros_like(ref)

    for slot, device in ((0, across), (1, mine)):
        base = device * own_rows

        @pl.loop(0, n_tiles)
        def _(tile):
            lanes = aligned(base + tile * TILE, TILE)
            ids = ids_ref[:, lanes]
            tasks = lax.broadcasted_iota(jnp.int32, (n_task, TILE), 0)
            onehot = jnp.where(tasks == ids, 1.0, 0.0).astype(BF16)
            masks = dot(masks_ref[...], onehot)
            masked = (act_ref[:, lanes].astype(F32) * masks).astype(BF16)
            rest = LANES - n_task - masked.shape[0]
            extra = jnp.concatenate([onehot, masked, jnp.zeros((rest, TILE), BF16)], axis=0)
            rows = aligned(slot * own_rows + tile * TILE, TILE)
            x_all[rows, pl.ds(lat_width, LANES)] = extra.T
            if slot == 1:
                x_t[pl.ds(lat_width, LANES), aligned(tile * TILE, TILE)] = extra

    for copy in loads[:2]:
        copy.wait()

    @pl.loop(0, n_tiles)
    def _(tile):
        rows = aligned(own_rows + tile * TILE, TILE)
        x_t[pl.ds(0, lat_width), aligned(tile * TILE, TILE)] = x_all[
            rows, pl.ds(0, lat_width)
        ].T

    def centre(values):
        return values - jnp.sum(values, axis=1, keepdims=True) * (1.0 / hid_width)

    def prepare(net):
        for index in range(len(w_pairs)):
            if w_pairs[index][2] == net:
                loads[4 + index].wait()
                for flip in (1, 2, 3):
                    weight_copy(index, flip).wait_recv()
        cols = pl.ds(net * hid_width, hid_width)

        @pl.loop(0, lat_width // SUB)
        def _(step):
            rows = aligned(step * SUB, SUB)
            w1_c[rows, cols] = centre(w1_raw[rows, cols].astype(F32)).astype(BF16)

        n_embed = embed_ref.shape[1]
        table = dot(embed_ref[...], w1_raw[pl.ds(lat_width, n_embed), cols])
        w1_c[pl.ds(lat_width, n_task), cols] = centre(table).astype(BF16)
        act = centre(w1_raw[pl.ds(lat_width + n_embed, 16), cols].astype(F32))
        bias = centre(vecs[pl.ds(0, 1), cols])
        high = bias.astype(BF16).astype(F32)
        row = lax.broadcasted_iota(jnp.int32, act.shape, 0)
        act = jnp.where(row == 6, high, jnp.where(row == 7, bias - high, act))
        w1_c[pl.ds(lat_width + n_task, 16), cols] = act.astype(BF16)
        rest = LANES - n_task - 16
        w1_c[pl.ds(lat_width + n_task + 16, rest), cols] = jnp.zeros((rest, hid_width), BF16)

    def forward(net, rows, keep):
        cols = pl.ds(net * hid_width, hid_width)
        pre[...] = dot(x_all[rows, :], w1_c[:, cols])

        @pl.loop(0, TILE // SUB)
        def _(step):
            part = aligned(step * SUB, SUB)
            values = pre[part, :]
            square = jnp.sum(values * values, axis=1, keepdims=True)
            inv_ref[part, :] = jnp.broadcast_to(
                lax.rsqrt(square * (1.0 / hid_width) + EPS), (SUB, LANES)
            )

        @pl.loop(0, TILE // SUB)
        def _(step):
            part = aligned(step * SUB, SUB)
            inv = inv_ref[part, :]
            for lane in range(n_lane):
                lanes = pl.ds(lane * LANES, LANES)
                wide = pl.ds(net * hid_width + lane * LANES, LANES)
                xhat = pre[part, lanes] * inv
                y = xhat * vecs[pl.ds(1, 1), wide] + vecs[pl.ds(2, 1), wide]
                e = jnp.exp(jnp.minimum(y, 20.0))
                e2 = e + 2.0
                r = 1.0 / (e * e2 + 2.0)
                u = e * r
                t = u * e2
                hid[part, lanes] = (y * t).astype(BF16)
                if keep:
                    pre[part, lanes] = xhat
                    dm[part, lanes] = t + (4.0 * y) * (u * (r + u))

    def backward(net, target, first_row):
        @pl.loop(0, TILE // SUB)
        def _(step):
            part = aligned(step * SUB, SUB)
            first = jnp.zeros((SUB, LANES), F32)
            second = jnp.zeros((SUB, LANES), F32)
            for lane in range(n_lane):
                lanes = pl.ds(lane * LANES, LANES)
                wide = pl.ds(net * hid_width + lane * LANES, LANES)
                d_y = dh[part, lanes] * dm[part, lanes]
                xhat = pre[part, lanes]
                scaled = d_y * xhat
                col_acc[pl.ds(0, 8), wide] += jnp.sum(
                    scaled.reshape(SUB // 8, 8, LANES), axis=0
                )
                col_acc[pl.ds(8, 8), wide] += jnp.sum(d_y.reshape(SUB // 8, 8, LANES), axis=0)
                gain = vecs[pl.ds(1, 1), wide]
                g = d_y * gain
                first += g
                second += scaled * gain
                dh[part, lanes] = g
            inv = inv_ref[part, :]
            first = jnp.broadcast_to(
                jnp.sum(first, axis=1, keepdims=True) * (1.0 / hid_width), (SUB, LANES)
            )
            second = jnp.broadcast_to(
                jnp.sum(second, axis=1, keepdims=True) * (1.0 / hid_width), (SUB, LANES)
            )
            first = first * inv
            second = second * inv
            for lane in range(n_lane):
                lanes = pl.ds(lane * LANES, LANES)
                value = dh[part, lanes] * inv - first - pre[part, lanes] * second
                target[aligned(first_row + step * SUB, SUB), lanes] = value.astype(BF16)

    d_scale = 2.0 * CONS_COEF / total_rows

    def simnorm(slot, tile, target, row, col):
        rows = aligned(tile * TILE, TILE)
        zt[...] = dot(w2_t[aligned(pair * chip_cols, chip_cols), :], hid[...], 1, 1)
        for side in range(2):
            latt[pl.ds(side * share, share), :] = next_lat[slot, side, rows, :].T.astype(F32)

        @pl.loop(0, chip_cols // SUB)
        def _(step):
            part = aligned(step * SUB, SUB)
            bias = b2_ref[aligned(pair * chip_cols + step * SUB, SUB), :]
            for lane in range(TILE // LANES):
                lanes = pl.ds(lane * LANES, LANES)
                z = (zt[part, lanes] + bias).reshape(SUB // GROUP, GROUP, LANES)
                e = jnp.exp(z - jnp.max(z, axis=1, keepdims=True))
                s = e * (1.0 / jnp.sum(e, axis=1, keepdims=True))
                error = s - latt[part, lanes].reshape(z.shape)
                sum_acc[pl.ds(0, 8), :] += jnp.sum(error * error, axis=0)
                d_lat = d_scale * error
                d_z = s * (d_lat - jnp.sum(s * d_lat, axis=1, keepdims=True))
                zt[part, lanes] = s.reshape(SUB, LANES)
                target[
                    aligned(row + step * SUB, SUB), aligned(col + lane * LANES, LANES)
                ] = d_z.reshape(SUB, LANES).astype(BF16)

        for side in range(2):
            lat_stage[slot, side, rows, :] = zt[pl.ds(side * share, share), :].astype(BF16).T

    def lat_copies(slot, tile):
        device = across if slot == 0 else mine
        rows = aligned(tile * TILE, TILE)
        out_rows = lat_out.at[aligned(device * own_rows + tile * TILE, TILE), :]
        index = slot * n_tiles + tile
        local = pltpu.make_async_copy(
            lat_stage.at[slot, half, rows, :], out_rows, l_local.at[index]
        )
        remote = pltpu.make_async_remote_copy(
            src_ref=lat_stage.at[slot, 1 - half, rows, :],
            dst_ref=out_rows,
            send_sem=l_send.at[index],
            recv_sem=l_recv.at[index],
            device_id={"mp": near},
            device_id_type=MESH,
        )
        return local, remote

    def dpl_copy(tile):
        cols = aligned(tile * TILE, TILE)
        return pltpu.make_async_remote_copy(
            src_ref=dpl_send.at[:, cols],
            dst_ref=dpl.at[aligned(pair * chip_cols, chip_cols), cols],
            send_sem=d_send.at[tile],
            recv_sem=d_recv.at[tile],
            device_id={"mp": across},
            device_id_type=MESH,
        )

    def grad_copies(tile):
        rows = aligned(tile * TILE, TILE)
        out_rows = grad_out.at[aligned(mine * own_rows + tile * TILE, TILE), :]
        remotes = []
        for flip in (2, 3, 1):
            peer = peer_of(flip)
            remotes.append(
                pltpu.make_async_remote_copy(
                    src_ref=lg_stage.at[peer, rows, :],
                    dst_ref=out_rows,
                    send_sem=g_send.at[flip - 1, tile],
                    recv_sem=g_recv.at[flip - 1, tile],
                    device_id={"mp": peer},
                    device_id_type=MESH,
                )
            )
        local = pltpu.make_async_copy(lg_stage.at[mine, rows, :], out_rows, g_local.at[tile])
        return local, remotes

    prepare(0)
    loads[2].wait()
    next_copy(0).wait_recv()

    @pl.loop(0, n_tiles)
    def _(tile):
        forward(0, aligned(tile * TILE, TILE), False)
        simnorm(0, tile, dpl_send, 0, tile * TILE)
        dpl_copy(tile).start()
        local, remote = lat_copies(0, tile)
        local.start()
        remote.start()

    prepare(1)

    @pl.loop(0, n_tiles)
    def _(tile):
        cols = aligned(tile * TILE, TILE)
        forward(1, aligned(own_rows + tile * TILE, TILE), True)
        bins = bins_ref[:, aligned(mine * own_rows + tile * TILE, TILE)]
        frac = frac_ref[:, aligned(mine * own_rows + tile * TILE, TILE)]
        z = dot(rw2_t[...], hid[...], 1, 1)
        bias = rb2_ref[...]
        z = z + jnp.concatenate([bias] * (TILE // LANES), axis=1)
        z = z - jnp.max(z, axis=0, keepdims=True)
        e = jnp.exp(z)
        total = jnp.sum(e, axis=0, keepdims=True)
        row = lax.broadcasted_iota(jnp.int32, z.shape, 0)
        target = jnp.where(row == bins, 1.0 - frac, 0.0) + jnp.where(row == bins + 1, frac, 0.0)
        loss = jnp.sum(target * (jnp.log(total) - z), axis=0, keepdims=True)
        row_acc[...] += loss
        d_logits = (REW_COEF / total_rows) * (e * (1.0 / total) - target)
        dlog[...] = d_logits.astype(BF16)
        sum_acc[pl.ds(8, 8), :] += dot(jnp.ones((8, TILE), BF16), dlog[...], 1, 1)
        rg2t[...] += dot(dlog[...], hid[...])
        dh[...] = dot(dlog[...], rw2_t[...], 0, 0)
        backward(1, d_rew, tile * TILE)
        g1[:, pl.ds(hid_width, hid_width)] += dot(x_t[:, cols], d_rew[cols, :])

    loads[3].wait()
    next_copy(1).wait_recv()

    @pl.loop(0, n_tiles)
    def _(tile):
        cols = aligned(tile * TILE, TILE)
        forward(0, aligned(own_rows + tile * TILE, TILE), True)
        simnorm(1, tile, dpl, pair * chip_cols, tile * TILE)
        local, remote = lat_copies(1, tile)
        local.start()
        remote.start()
        dpl_copy(tile).wait_recv()
        d_lat = dpl[:, cols]
        b2_acc[...] += dot(jnp.ones((8, TILE), BF16), d_lat, 1, 1)
        g2t[...] += dot(d_lat, hid[...])
        dh[...] = dot(d_lat, w2_t[...], 0, 0)
        backward(0, d_pre, 0)
        g1[:, pl.ds(0, hid_width)] += dot(x_t[:, cols], d_pre[...])
        lat_rows = pl.ds(0, lat_width)
        lg = dot(d_pre[...], w1_raw[lat_rows, pl.ds(0, hid_width)], 1, 1)
        lg = lg + dot(d_rew[cols, :], w1_raw[lat_rows, pl.ds(hid_width, hid_width)], 1, 1)
        lg = (lg * total_rows).astype(BF16)
        for device in range(n_mp):
            lg_stage[device, cols, :] = lg[:, device * share : (device + 1) * share]
        local, remotes = grad_copies(tile)
        local.start()
        for remote in remotes:
            remote.start()

    for device in range(n_mp):
        for net in range(2):
            wide = pl.ds(net * hid_width + device * shard, shard)
            cols = pl.ds(net * shard, shard)
            ga_ref[device, :, cols] = g1[pl.ds(0, ga_ref.shape[1]), wide].astype(BF16)
        block_cols = pl.ds(device * shard, shard)
        gb_ref[device, pl.ds(0, lat_width), :] = g2t[:, block_cols].astype(BF16)
        gb_ref[device, pl.ds(lat_width, LANES), :] = rg2t[:, block_cols].astype(BF16)
    tasks = g1[pl.ds(lat_width, n_task), :]
    n_embed = embed_ref.shape[1]
    ge_ref[...] = split_dot(tasks, w1_raw[pl.ds(lat_width, n_embed), :], 1, 1)
    cons = jnp.sum(sum_acc[pl.ds(0, 8), :])
    rew = jnp.sum(row_acc[...])
    gs_ref[...] = jnp.zeros_like(gs_ref)
    for device in range(n_mp):
        for net in range(2):
            wide = pl.ds(net * hid_width + device * shard, shard)
            cols = pl.ds(net * shard, shard)
            for line in range(2):
                gs_ref[device, pl.ds(line, 1), cols] = jnp.sum(
                    col_acc[pl.ds(8 * line, 8), wide], axis=0, keepdims=True
                )
        gs_ref[device, pl.ds(2, 1), :] = b2_acc[pl.ds(0, 1), :]
        gs_ref[device, pl.ds(3, 1), pl.ds(0, LANES)] = sum_acc[pl.ds(8, 1), :]
        gs_ref[device, pl.ds(4, 1), :] = jnp.full((1, lat_width), cons)
        gs_ref[device, pl.ds(5, 1), :] = jnp.full((1, lat_width), rew)

    for index in range(len(w_pairs)):
        for flip in (1, 2, 3):
            weight_copy(index, flip).wait_send()
    for slot in range(2):
        next_copy(slot).wait_send()

        @pl.loop(0, n_tiles)
        def _(tile):
            local, remote = lat_copies(slot, tile)
            local.wait()
            remote.wait()

    @pl.loop(0, n_tiles)
    def _(tile):
        dpl_copy(tile).wait_send()
        local, remotes = grad_copies(tile)
        local.wait()
        for remote in remotes:
            remote.wait()


def run_main(n_mp, total_rows, args):
    latent, next_latent, w1, w2t = args[0], args[1], args[2], args[3]
    tok_rows, lat_width = latent.shape
    share = next_latent.shape[1]
    shard = w1.shape[2]
    hid_width = n_mp * shard
    own = tok_rows // n_mp
    in_rows = lat_width + LANES
    n_tiles = own // TILE
    embed = args[11]
    n_task, n_embed = embed.shape
    ga_rows = lat_width + n_task + 16
    any_spec = pl.BlockSpec(memory_space=pl.ANY)
    vmem_spec = pl.BlockSpec(memory_space=pltpu.VMEM)
    shape = jax.ShapeDtypeStruct
    dma = pltpu.SemaphoreType.DMA
    return pl.pallas_call(
        functools.partial(main_kernel, (n_mp, total_rows, hid_width)),
        out_shape=(
            shape((tok_rows, share), BF16),
            shape((tok_rows, share), BF16),
            shape((n_mp, ga_rows, 2 * shard), BF16),
            shape((n_mp, in_rows, shard), BF16),
            shape((n_mp, 8, lat_width), F32),
            shape((n_task, n_embed), F32),
        ),
        in_specs=[any_spec] * 6 + [vmem_spec] * 8,
        out_specs=[any_spec] * 2 + [vmem_spec] * 4,
        scratch_shapes=[
            pltpu.VMEM((2 * own, in_rows), BF16),
            pltpu.VMEM((in_rows, own), BF16),
            pltpu.VMEM((in_rows, 2 * hid_width), BF16),
            pltpu.VMEM((in_rows, 2 * hid_width), BF16),
            pltpu.VMEM((lat_width, hid_width), BF16),
            pltpu.VMEM((LANES, hid_width), BF16),
            pltpu.VMEM((8, 2 * hid_width), F32),
            pltpu.VMEM((2, 2, own, share), BF16),
            pltpu.VMEM((lat_width, own), BF16),
            pltpu.VMEM((2 * share, own), BF16),
            pltpu.VMEM((2, 2, own, share), BF16),
            pltpu.VMEM((n_mp, own, share), BF16),
            pltpu.VMEM((own, hid_width), BF16),
            pltpu.VMEM((in_rows, 2 * hid_width), F32),
            pltpu.VMEM((lat_width, hid_width), F32),
            pltpu.VMEM((LANES, hid_width), F32),
            pltpu.VMEM((TILE, hid_width), F32),
            pltpu.VMEM((TILE, hid_width), F32),
            pltpu.VMEM((TILE, hid_width), F32),
            pltpu.VMEM((TILE, hid_width), BF16),
            pltpu.VMEM((TILE, hid_width), BF16),
            pltpu.VMEM((2 * share, TILE), F32),
            pltpu.VMEM((2 * share, TILE), F32),
            pltpu.VMEM((LANES, TILE), BF16),
            pltpu.VMEM((TILE, LANES), F32),
            pltpu.VMEM((16, 2 * hid_width), F32),
            pltpu.VMEM((16, LANES), F32),
            pltpu.VMEM((1, TILE), F32),
            pltpu.VMEM((8, lat_width), F32),
            dma((10,)),
            dma((3, 6)),
            dma((3, 6)),
            dma((2,)),
            dma((2,)),
            dma((n_tiles,)),
            dma((n_tiles,)),
            dma((2 * n_tiles,)),
            dma((2 * n_tiles,)),
            dma((2 * n_tiles,)),
            dma((n_tiles,)),
            dma((3, n_tiles)),
            dma((3, n_tiles)),
        ],
        compiler_params=pltpu.CompilerParams(
            collective_id=0, has_side_effects=True, vmem_limit_bytes=60 << 20
        ),
    )(*args)


def on_device(
    latent,
    actions,
    task_ids,
    action_masks,
    next_latent,
    reward_bins,
    reward_frac,
    task_embed,
    dyn_w1,
    dyn_b1,
    dyn_gain,
    dyn_shift,
    rew_w1,
    rew_b1,
    rew_gain,
    rew_shift,
    dyn_w2,
    dyn_b2,
    rew_w2,
    rew_b2,
):
    n_mp = lax.axis_size("mp")
    tok_rows, lat_width = latent.shape
    total_rows = tok_rows * lax.axis_size("dp")
    n_act = actions.shape[0]
    n_task, n_embed = task_embed.shape
    n_bins = rew_w2.shape[1]
    shard = dyn_w1.shape[1]
    in_rows = lat_width + LANES

    def first_layer(w1):
        pad = jnp.zeros((in_rows - w1.shape[0], shard), BF16)
        return jnp.concatenate(
            [w1[:lat_width], w1[lat_width + n_act :], w1[lat_width : lat_width + n_act], pad]
        )

    w1 = jnp.stack([first_layer(dyn_w1), first_layer(rew_w1)])
    none = jnp.zeros_like(dyn_b1)
    vecs = jnp.stack(
        [
            jnp.stack([dyn_b1, dyn_gain, dyn_shift] + [none] * 5),
            jnp.stack([rew_b1, rew_gain, rew_shift] + [none] * 5),
        ]
    )
    rw2t = jnp.pad(rew_w2.T, ((0, LANES - n_bins), (0, 0)))
    act = jnp.concatenate(
        [actions, jnp.ones((2, tok_rows), BF16), jnp.zeros((14 - n_act, tok_rows), BF16)]
    )
    masks = jnp.concatenate(
        [
            action_masks.astype(BF16).T,
            jnp.ones((2, n_task), BF16),
            jnp.zeros((14 - n_act, n_task), BF16),
        ]
    )
    b2 = jnp.broadcast_to(dyn_b2[:, None], (lat_width, LANES))
    rb2 = jnp.pad(rew_b2, (0, LANES - n_bins), constant_values=-1e30)
    rb2 = jnp.broadcast_to(rb2[:, None], (LANES, LANES))
    args = (
        latent,
        next_latent,
        w1,
        dyn_w2.T,
        rw2t,
        vecs,
        task_ids[None, :],
        act,
        masks,
        reward_bins[None, :],
        reward_frac[None, :],
        task_embed,
        b2,
        rb2,
    )
    latents, latent_grad, ga, gb, gs, ge = run_main(n_mp, total_rows, args)
    ga = lax.psum_scatter(ga, "mp", scatter_dimension=0, tiled=True)
    gb = lax.psum_scatter(gb, "mp", scatter_dimension=0, tiled=True)
    gs = lax.psum_scatter(gs, "mp", scatter_dimension=0, tiled=True)
    ga, gb = lax.psum((ga, gb), "dp")
    gs = lax.psum(gs, "dp")
    ge = lax.psum(ge, ("dp", "mp"))
    ga, gb, gs = ga[0].astype(F32), gb[0].astype(F32), gs[0]
    grad_task = jnp.dot(
        task_embed.astype(F32).T,
        ga[lat_width : lat_width + n_task],
        precision=lax.Precision.HIGHEST,
    )
    first = lat_width + n_task
    grad_w1 = jnp.concatenate([ga[:lat_width], ga[first : first + n_act], grad_task])
    grad_b1 = ga[first + n_act]
    losses = jnp.stack([gs[4, 0], gs[5, 0]]) / total_rows
    return (
        latents,
        latent_grad,
        losses,
        ge,
        grad_w1[:, :shard],
        grad_b1[:shard],
        gs[0, :shard],
        gs[1, :shard],
        grad_w1[:, shard:],
        grad_b1[shard:],
        gs[0, shard:],
        gs[1, shard:],
        gb[:lat_width].T,
        gs[2],
        gb[lat_width : lat_width + n_bins].T,
        gs[3, :n_bins],
    )


def solution(mesh):
    return jax.shard_map(
        on_device,
        mesh=mesh,
        in_specs=(
            P("dp", None),
            P(None, "dp"),
            P("dp"),
            P(),
            P("dp", "mp"),
            P("dp"),
            P("dp"),
            P(),
            P(None, "mp"),
            P("mp"),
            P("mp"),
            P("mp"),
            P(None, "mp"),
            P("mp"),
            P("mp"),
            P("mp"),
            P("mp", None),
            P(),
            P("mp", None),
            P(),
        ),
        out_specs=(
            P("dp", "mp"),
            P("dp", "mp"),
            P(),
            P(),
            P(None, "mp"),
            P("mp"),
            P("mp"),
            P("mp"),
            P(None, "mp"),
            P("mp"),
            P("mp"),
            P("mp"),
            P("mp", None),
            P(),
            P("mp", None),
            P(),
        ),
        check_vma=False,
    )
```

time: 637 us -> 324 us (0.51); the launches traced: 630 us -> 324 us
  waiting for transfers between devices: 263 us -> 85 us
  other arithmetic: 136 us -> 6.44 us
  Pallas kernels: 0 us -> 125 us
  matrix products: 102 us -> 1.09 us
  local copies, waits for them, and re-layouts: 47.8 us -> 15.2 us
  blocking collectives: 64.2 us -> 77.2 us
    unnamed x9 -> x4, waiting for transfers between devices: 126 us -> 1.4 us
    pallas_call x0 -> x1, Pallas kernels: none -> 125 us  [run_main(): pl.pallas_call(functools.partial(main_kernel, (n_mp, total_rows, hid_widt...]
    dot_general x16 -> x1, matrix products: 102 us -> 1.09 us  [on_device(): jnp.dot(task_embed.astype(F32).T, ga[lat_width:lat_width + n_task], preci...]
    psum x4 -> x1, waiting for transfers between devices: 93.5 us -> 21.5 us  [on_device(): ga, gb = lax.psum((ga, gb), 'dp')]
    reduce_sum x8 -> x0, other arithmetic: 69.6 us -> none  [the longest x1 28.7 us: on_device(): grad_shift = jnp.sum(d_normed, axis=0)]
    reduce_scatter x0 -> x3, waiting for transfers between devices: none -> 62.1 us  [the longest x1 36.6 us: on_device(): ga = lax.psum_scatter(ga, 'mp', scatter_dimension=0, tiled=True)]
    all_gather x1 -> x0, waiting for transfers between devices: 43.2 us -> none  [on_device(): d_full = lax.all_gather(d_share, 'mp', axis=1, tiled=True)]
    unnamed x86 -> x38, local copies, waits for them, and re-layouts: 41.7 us -> 6.19 us
  transfers between devices with their start and end apart: 7 -> 4, of which waited for: 5 -> 3; matrix products, arithmetic and copies ran while one was open for 19% -> 1% of each run, Pallas kernels for 0% -> 0%
where the time goes in v1:
time: 324 us
  Pallas kernels  125 us (39%)
  waiting for transfers between devices  85 us (26%)
  blocking collectives  77.2 us (24%)
  local copies, waits for them, and re-layouts  15.2 us (5%)
  between operations  14.1 us (4%)
  other arithmetic  6.44 us (2%)
    pallas_call x1, Pallas kernels, run_main(): pl.pallas_call(functools.partial(main_kernel, (n_mp, total_rows, hid_widt...  125 us
    psum x1, blocking collectives, on_device(): ge = lax.psum(ge, ('dp', 'mp'))  40.2 us
    psum x1, blocking collectives, on_device(): gs = lax.psum(gs, 'dp')  37 us
    reduce_scatter x1, waiting for transfers between devices, on_device(): ga = lax.psum_scatter(ga, 'mp', scatter_dimension=0, tiled=True)  36.6 us
    reduce_scatter x1, waiting for transfers between devices, on_device(): gb = lax.psum_scatter(gb, 'mp', scatter_dimension=0, tiled=True)  25.5 us
    psum x1, waiting for transfers between devices, on_device(): ga, gb = lax.psum((ga, gb), 'dp')  21.5 us
  transfers between devices with their start and end apart: 4, of which 3 were waited for; matrix products, arithmetic and copies ran while one was open for 1% of the time, Pallas kernels for 0%

profile of v1, /device:TPU:0, one launch (start us, length us, event | category | flops | bytes accessed | tf_op | source)
XLA Modules:
  0.0 323.8 jit_solution(10204243265670935474)
XLA Ops:
  7.4 1.0 slice.95
  8.4 0.8 slice.98
  9.5 0.8 maximum_maximum_fusion.act_ref
  10.3 0.7 maximum_maximum_fusion.1.masks_ref
  11.0 0.8 copy.36
  11.8 0.6 pad.8.rw2t_in
  12.5 0.6 pad_maximum_fusion.2.vecs_in
  13.4 0.9 pad_maximum_fusion.1.w1_in
  14.3 0.8 broadcast_in_dim.40.b2_ref
  15.1 0.7 broadcast_in_dim.41.rb2_ref
  15.8 124.6 %shard_map.315 = (bf16[8192,128]{1,0:T(8,128)(2,1)}, bf16[8192,128]{1,0:T(8,128)(2,1)}, bf16[4,608,512]{2,1,0:T(8,128)(2,1)}, bf16[4,640,256]{2,1,0:T(8,128)(2,1...) custom-call(bf16[8192,512]{1,0:T(8,128)(2,1)} %latent_in.1, bf16[8192,128]{1,0:T(8,128)(2,1)} %next_in.1, ...), custom_call_target="tpu_custom_call" | custom-call | tf_op jit(solution)/shard_map/pallas_call | solution.py:526
  140.5 0.7 reduce-scatter.6.cloned.1.call-update
  141.2 0.7 reduce-scatter.4.cloned.1.call-update
  142.0 25.5 %reduce-scatter.8.cloned.1.call-done = bf16[1,640,256]{2,1,0:T(8,128)(2,1)} async-done(((bf16[4,640,256]{2,1,0:T(8,128)(2,1)}), bf16[1,640,256]{2,1,0:T(8,128)(2,1)}) %reduce-scatter.8.cloned.1.call-update) | async-done | bytes 327696 | tf_op jit(solution)/shard_map/reduce_scatter | solution.py:665
  167.4 36.6 %reduce-scatter.6.cloned.1.call-done = bf16[1,608,512]{2,1,0:T(8,128)(2,1)} async-done(((bf16[4,608,512]{2,1,0:T(8,128)(2,1)}), bf16[1,608,512]{2,1,0:T(8,128)(2,1)}) %reduce-scatter.6.cloned.1.call-update) | async-done | bytes 622608 | tf_op jit(solution)/shard_map/reduce_scatter | solution.py:664
  204.1 40.2 %psum.29 = f32[80,96]{1,0:T(8,128)} all-reduce(f32[80,96]{1,0:T(8,128)S(1)} %copy-done.7), channel_id=1, replica_groups=mesh['dp'=8,'mp'=4] {'dp','mp'}, use_global_device_ids=true, to_apply=%region_2.3 | all-reduce | flops 7680 | bytes 61440 | tf_op jit(solution)/shard_map/psum | solution.py:669
  244.3 37.0 %psum.28 = f32[1,8,512]{2,1,0:T(8,128)S(1)} all-reduce(f32[1,8,512]{2,1,0:T(8,128)} %reduce-scatter.4.cloned.1.call-done), channel_id=1, replica_groups=mesh['dp'=8,'mp'=4] {'dp'}, use_global_device_ids=true, to_apply=%region_1.2 | all-reduce | flops 4096 | bytes 32768 | tf_op jit(solution)/shard_map/psum | solution.py:668
  281.3 0.6 slice.138
  281.9 0.5 fusion.3
  282.4 1.9 maximum_multiply_fusion
  284.8 0.6 fusion.2
  285.4 21.5 %all-reduce.5.cloned.1.call-done = (bf16[1,608,512]{2,1,0:T(8,128)(2,1)}, bf16[1,640,256]{2,1,0:T(8,128)(2,1)}) async-done(((bf16[1,608,512]{2,1,0:T(8,128)(2,1)}, bf16[1,640,256]{2,1,0:T(8,128)(2,1)}), (bf16[1,608,512]{2,1,0:T(8,128)(2,1)}, bf16[1,640,256]{2,1,0:T(8,128)(2,1)})) %all-reduce.5.cloned.1.call-update) | async-done | bytes 950288 | tf_op jit(solution)/shard_map/psum | solution.py:667
  306.9 1.2 convert_bitcast_fusion
  308.3 0.6 copy-done.5
  308.9 1.1 convolution_bitcast_fusion
  310.1 0.7 slice_bitcast_fusion.2
  310.9 1.1 fusion
  312.0 0.6 fusion.1
  312.6 1.0 copy.37
  313.6 1.3 copy.42
  314.9 1.0 copy-done
  315.9 1.3 copy.43
  (66 shorter events, 1.6 us)
Async XLA Ops:
  7.2 6.0 %slice-start = ((bf16[614,256]{1,0:T(8,128)(2,1)}), bf16[512,256]{1,0:T(8,128)(2,1)S(1)}, s32[]{:S(2)}) async-start(bf16[614,256]{1,0:T(8,128)(2,1)} %param.28), calls=%async_computation.7 | async-start | bytes 524288 | tf_op jit(solution)/shard_map/slice | solution.py:622
  7.2 6.0 %slice-start.1 = ((bf16[614,256]{1,0:T(8,128)(2,1)}), bf16[6,256]{1,0:T(8,128)(2,1)S(1)}, s32[]{:S(2)}) async-start(bf16[614,256]{1,0:T(8,128)(2,1)} %param.28), calls=%async_computation.8 | async-start | bytes 8192 | tf_op jit(solution)/shard_map/slice | solution.py:622
  7.2 6.0 %slice-start.2 = ((bf16[614,256]{1,0:T(8,128)(2,1)}), bf16[512,256]{1,0:T(8,128)(2,1)S(1)}, s32[]{:S(2)}) async-start(bf16[614,256]{1,0:T(8,128)(2,1)} %param.32), calls=%async_computation.9 | async-start | bytes 524288 | tf_op jit(solution)/shard_map/slice | solution.py:622
  7.2 5.9 %slice-start.3 = ((bf16[614,256]{1,0:T(8,128)(2,1)}), bf16[6,256]{1,0:T(8,128)(2,1)S(1)}, s32[]{:S(2)}) async-start(bf16[614,256]{1,0:T(8,128)(2,1)} %param.32), calls=%async_computation.10 | async-start | bytes 8192 | tf_op jit(solution)/shard_map/slice | solution.py:622
  7.2 2.2 copy-start.8
  7.2 2.2 copy-start.4
  7.2 3.7 %copy-start.3 = (bf16[256,512]{1,0:T(8,128)(2,1)S(1)}, bf16[256,512]{1,0:T(8,128)(2,1)}, u32[]{:S(2)}) copy-start(bf16[256,512]{1,0:T(8,128)(2,1)} %param.36) | copy-start | bytes 786436
  7.3 4.5 %copy-start.6 = (bf16[256,101]{0,1:T(8,128)(2,1)S(1)}, bf16[256,101]{0,1:T(8,128)(2,1)}, u32[]{:S(2)}) copy-start(bf16[256,101]{0,1:T(8,128)(2,1)} %param.38) | copy-start | bytes 155140
  7.3 5.2 %copy-start.12 = (f32[256]{0:T(256)S(1)}, f32[256]{0:T(256)}, u32[]{:S(2)}) copy-start(f32[256]{0:T(256)} %param.35) | copy-start | bytes 3076
  7.3 5.2 %copy-start.10 = (f32[256]{0:T(256)S(1)}, f32[256]{0:T(256)}, u32[]{:S(2)}) copy-start(f32[256]{0:T(256)} %param.33) | copy-start | bytes 3076
  7.3 5.2 %copy-start.11 = (f32[256]{0:T(256)S(1)}, f32[256]{0:T(256)}, u32[]{:S(2)}) copy-start(f32[256]{0:T(256)} %param.34) | copy-start | bytes 3076
  7.3 5.2 %copy-start.13 = (f32[256]{0:T(256)S(1)}, f32[256]{0:T(256)}, u32[]{:S(2)}) copy-start(f32[256]{0:T(256)} %param.29) | copy-start | bytes 3076
  7.3 5.2 %copy-start.14 = (f32[256]{0:T(256)S(1)}, f32[256]{0:T(256)}, u32[]{:S(2)}) copy-start(f32[256]{0:T(256)} %param.30) | copy-start | bytes 3076
  7.3 5.2 %copy-start.15 = (f32[256]{0:T(256)S(1)}, f32[256]{0:T(256)}, u32[]{:S(2)}) copy-start(f32[256]{0:T(256)} %param.31) | copy-start | bytes 3076
  7.3 160.1 %reduce-scatter.8.cloned.1.call-start = ((), (), s32[]{:S(2)}) async-start(), calls=%async_computation.5 | async-start | bytes 1638400 | tf_op jit(solution)/shard_map/reduce_scatter | solution.py:665
  13.2 1.1 copy-start.16
  13.2 1.1 copy-start.9
  140.4 63.6 %reduce-scatter.6.cloned.1.call-start = ((), (), s32[]{:S(2)}) async-start(), calls=%async_computation.4 | async-start | bytes 3112960 | tf_op jit(solution)/shard_map/reduce_scatter | solution.py:664
  140.5 63.6 %copy-start.7 = (f32[80,96]{1,0:T(8,128)S(1)}, f32[80,96]{1,0:T(8,128)}, u32[]{:S(2)}) copy-start(f32[80,96]{1,0:T(8,128)} %get-tuple-element.25) | copy-start | bytes 92164
  141.2 103.1 %reduce-scatter.4.cloned.1.call-start = ((), (), s32[]{:S(2)}) async-start(), calls=%async_computation.3 | async-start | bytes 81920 | tf_op jit(solution)/shard_map/reduce_scatter | solution.py:666
  141.9 165.0 %all-reduce.5.cloned.1.call-start = ((), (), s32[]{:S(2)}) async-start(), calls=%async_computation.6 | async-start | bytes 1900544 | tf_op jit(solution)/shard_map/psum | solution.py:667
  308.2 0.7 copy-start.5
  308.2 1.8 copy-start.2
  310.9 2.7 copy-start.1
  313.6 2.3 copy-start
Sparse Core Ops, SparseCore 0:
  140.6 26.8 reduce-scatter.7
  170.2 33.8 reduce-scatter.5
  206.5 19.4 reduce-scatter.3
  229.7 77.1 all-reduce.4

commit v2 on v1

--- a/solution.py
+++ b/solution.py
@@ -27,6 +27,10 @@
 
 def aligned(start, size):
     return pl.ds(pl.multiple_of(start, size), size)
+
+
+def aligned_to(start, size):
+    return pl.ds(pl.multiple_of(start, 16), size)
 
 
 def split_dot(left, right, left_dim, right_dim):
@@ -53,10 +57,9 @@
     rb2_ref,
     lat_out,
     grad_out,
-    ga_ref,
-    gb_ref,
-    gs_ref,
-    ge_ref,
+    fin_dyn,
+    fin_rew,
+    fin_sums,
     x_all,
     x_t,
     w1_raw,
@@ -69,7 +72,13 @@
     dpl_send,
     lat_stage,
     lg_stage,
-    d_rew,
+    d_dyn,
+    part_dyn,
+    part_rew,
+    got_dyn,
+    got_rew,
+    sums,
+    got_sums,
     g1,
     g2t,
     rg2t,
@@ -99,9 +108,15 @@
     g_local,
     g_send,
     g_recv,
+    r_send,
+    r_recv,
+    s_send,
+    s_recv,
 ):
-    n_mp, total_rows, hid_width = sizes
+    n_mp, n_dp, total_rows, hid_width = sizes
+    n_bits = n_dp.bit_length() - 1
     mine = lax.axis_index("mp")
+    column = lax.axis_index("dp")
     pair = mine // 2
     half = mine % 2
     own_rows = x_all.shape[0] // 2
@@ -120,6 +135,12 @@
         across = 2 * (1 - pair)
         return across + half if flip == 2 else across + 1 - half
 
+    def bit_of(bit):
+        return (column // (1 << bit)) % 2
+
+    def column_peer(bit):
+        return column + (1 - 2 * bit_of(bit)) * (1 << bit)
+
     def rows_of(device):
         return aligned(device * own_rows, own_rows)
 
@@ -128,28 +149,38 @@
         pl.semaphore_signal(
             barrier, inc=1, device_id={"mp": peer_of(flip)}, device_id_type=MESH
         )
-    pl.semaphore_wait(barrier, 3)
+    for bit in range(n_bits):
+        pl.semaphore_signal(
+            barrier, inc=1, device_id={"dp": column_peer(bit)}, device_id_type=MESH
+        )
+    pl.semaphore_wait(barrier, 3 + n_bits)
 
     near, across = peer_of(1), peer_of(2)
 
-    w_pairs = []
-    for net in range(2):
-        cols = aligned(net * hid_width + mine * shard, shard)
-        w_pairs.append((w1_in.at[net], w1_raw.at[:, cols], net))
-        w_pairs.append((vecs_in.at[net], vecs.at[:, cols], net))
-    block = aligned(mine * shard, shard)
-    w_pairs.append((w2t_in, w2_t.at[:, block], 0))
-    w_pairs.append((rw2t_in, rw2_t.at[:, block], 1))
-    order = [0, 1, 4, 2, 3, 5]
-
-    def weight_copy(index, flip):
-        source, target, _ = w_pairs[index]
+    def w_pairs(block):
+        pairs = []
+        for net in range(2):
+            cols = aligned(net * hid_width + block * shard, shard)
+            pairs.append((w1_in.at[net], w1_raw.at[:, cols]))
+            pairs.append((vecs_in.at[net], vecs.at[:, cols]))
+        cols = aligned(block * shard, shard)
+        pairs.append((w2t_in, w2_t.at[:, cols]))
+        pairs.append((rw2t_in, rw2_t.at[:, cols]))
+        return pairs
+
+    w_needs = ((0, 1, 4), (2, 3, 5))
+    own_weights = w_pairs(mine)
+
+    def weight_copy(index, kind):
+        source, target = own_weights[index]
+        if kind == 2:
+            source = target = w_pairs(across)[index][1]
         return pltpu.make_async_remote_copy(
             src_ref=source,
             dst_ref=target,
-            send_sem=w_send.at[flip - 1, index],
-            recv_sem=w_recv.at[flip - 1, index],
-            device_id={"mp": peer_of(flip)},
+            send_sem=w_send.at[kind, index],
+            recv_sem=w_recv.at[kind, index],
+            device_id={"mp": across if kind == 1 else near},
             device_id_type=MESH,
         )
 
@@ -174,17 +205,16 @@
         )
     for slot, device in ((0, across), (1, mine)):
         loads.append((next_in.at[rows_of(device), :], next_lat.at[slot, half]))
-    for source, target, _ in w_pairs:
-        loads.append((source, target))
+    loads += own_weights
     loads = [
         pltpu.make_async_copy(source, target, load_sem.at[i])
         for i, (source, target) in enumerate(loads)
     ]
     for copy in loads:
         copy.start()
-    for index in order:
-        for flip in (2, 3, 1):
-            weight_copy(index, flip).start()
+    for index in w_needs[0] + w_needs[1]:
+        weight_copy(index, 1).start()
+        weight_copy(index, 0).start()
     next_copy(0).start()
     next_copy(1).start()
 
@@ -223,11 +253,13 @@
         return values - jnp.sum(values, axis=1, keepdims=True) * (1.0 / hid_width)
 
     def prepare(net):
-        for index in range(len(w_pairs)):
-            if w_pairs[index][2] == net:
-                loads[4 + index].wait()
-                for flip in (1, 2, 3):
-                    weight_copy(index, flip).wait_recv()
+        for index in w_needs[net]:
+            weight_copy(index, 1).wait_recv()
+            weight_copy(index, 2).start()
+        for index in w_needs[net]:
+            loads[4 + index].wait()
+            weight_copy(index, 0).wait_recv()
+            weight_copy(index, 2).wait_recv()
         cols = pl.ds(net * hid_width, hid_width)
 
         @pl.loop(0, lat_width // SUB)
@@ -404,12 +436,171 @@
         local.start()
         remote.start()
 
+    loads[3].wait()
+    next_copy(1).wait_recv()
+
+    @pl.loop(0, n_tiles)
+    def _(tile):
+        cols = aligned(tile * TILE, TILE)
+        forward(0, aligned(own_rows + tile * TILE, TILE), True)
+        simnorm(1, tile, dpl, pair * chip_cols, tile * TILE)
+        local, remote = lat_copies(1, tile)
+        local.start()
+        remote.start()
+        dpl_copy(tile).wait_recv()
+        d_lat = dpl[:, cols]
+        b2_acc[...] += dot(jnp.ones((8, TILE), BF16), d_lat, 1, 1)
+        g2t[...] += dot(d_lat, hid[...])
+        dh[...] = dot(d_lat, w2_t[...], 0, 0)
+        backward(0, d_dyn, tile * TILE)
+        g1[:, pl.ds(0, hid_width)] += dot(x_t[:, cols], d_dyn[cols, :])
+
+    def add_into(target, other, n_rows):
+        step_rows = 48 if n_rows % 48 == 0 else 16
+
+        @pl.loop(0, n_rows // step_rows)
+        def _(step):
+            rows = aligned(step * step_rows, step_rows)
+            total = target[rows, :].astype(F32) + other[rows, :].astype(F32)
+            target[rows, :] = total.astype(BF16)
+
+    def reduction(key, part, got, fin, with_sums):
+        n_rows = part.shape[2]
+        stages = [("near", 0, n_rows), ("across", 0, n_rows)]
+        offset, length = 0, n_rows
+        place = 3 * n_rows
+        gathers = []
+        for bit in range(n_bits):
+            if length % 32 == 0:
+                length //= 2
+                keep = offset + bit_of(bit) * length
+                stages.append(("half", bit, offset + (1 - bit_of(bit)) * length, keep, length, place))
+                gathers.append(("gather", bit, keep, length))
+                offset = keep
+            else:
+                stages.append(("whole", bit, offset, offset, length, place))
+            place += length
+        last = len(stages)
+        stages += gathers[::-1]
+        whole = part.at[half, pair]
+
+        def ends(index):
+            stage = stages[index]
+            kind = stage[0]
+            if kind == "near":
+                return part.at[1 - half], got.at[:, pl.ds(0, n_rows), :], {"mp": near}
+            if kind == "across":
+                return part.at[half, 1 - pair], got.at[0, pl.ds(n_rows, n_rows), :], {"mp": across}
+            device = {"dp": column_peer(stage[1])}
+            if kind == "gather":
+                rows = aligned_to(stage[2], stage[3])
+                return fin.at[rows, :], fin.at[rows, :], device
+            rows = aligned_to(stage[2], stage[4])
+            base = 2 * n_rows + stage[5] - 3 * n_rows
+            return whole.at[rows, :], got.at[0, pl.ds(base, stage[4]), :], device
+
+        def copy(index):
+            source, target, device = ends(index)
+            return pltpu.make_async_remote_copy(
+                src_ref=source,
+                dst_ref=target,
+                send_sem=r_send.at[key, index],
+                recv_sem=r_recv.at[key, index],
+                device_id=device,
+                device_id_type=MESH,
+            )
+
+        def sums_copy(index):
+            return pltpu.make_async_remote_copy(
+                src_ref=sums.at[index],
+                dst_ref=got_sums.at[index],
+                send_sem=s_send.at[index],
+                recv_sem=s_recv.at[index],
+                device_id=ends(index)[2],
+                device_id_type=MESH,
+            )
+
+        def start(index):
+            copy(index).start()
+            if with_sums and index < last:
+                sums_copy(index).start()
+
+        def finish(index):
+            stage = stages[index]
+            kind = stage[0]
+            if kind == "whole":
+                copy(index).wait_send()
+            copy(index).wait_recv()
+            if with_sums and index < last:
+                sums_copy(index).wait_recv()
+                sums[index + 1] = sums[index] + got_sums[index]
+            if kind == "near":
+                for other in range(2):
+                    add_into(
+                        part.at[half, other], got.at[other, pl.ds(0, n_rows), :], n_rows
+                    )
+            elif kind == "across":
+                add_into(whole, got.at[0, pl.ds(n_rows, n_rows), :], n_rows)
+            elif kind != "gather":
+                base = 2 * n_rows + stage[5] - 3 * n_rows
+                add_into(
+                    whole.at[aligned_to(stage[3], stage[4]), :],
+                    got.at[0, pl.ds(base, stage[4]), :],
+                    stage[4],
+                )
+            if index + 1 == last:
+                rows = aligned_to(offset, length)
+                fin[rows, :] = whole[rows, :]
+            if index + 1 < len(stages):
+                start(index + 1)
+
+        def drain():
+            for index, stage in enumerate(stages):
+                if stage[0] != "whole":
+                    copy(index).wait_send()
+                if with_sums and index < last:
+                    sums_copy(index).wait_send()
+
+        return start, finish, drain, len(stages)
+
+    def fill(part, net, first, count, source, base):
+        for device in range(n_mp):
+            cols = pl.ds(net * hid_width + device * shard, shard)
+            part[device % 2, device // 2, pl.ds(first, count), :] = source[
+                pl.ds(base, count), cols
+            ].astype(BF16)
+
+    def add_columns(net):
+        cols = pl.ds(net * hid_width, hid_width)
+        for line in range(2):
+            g1[pl.ds(lat_width + n_task + 8 + line, 1), cols] = jnp.sum(
+                col_acc[pl.ds(8 * line, 8), cols], axis=0, keepdims=True
+            )
+
+    in_rows = g1.shape[0]
+    add_columns(0)
+    fill(part_dyn, 0, 0, in_rows, g1, 0)
+    fill(part_dyn, 0, in_rows, lat_width, g2t, 0)
+    start, finish, drain_dyn, n_stages = reduction(0, part_dyn, got_dyn, fin_dyn, False)
+    start(0)
+    points = [0, 1, 2]
+    waiting = list(range(n_stages))
+
     prepare(1)
+
+    def point(tile, number):
+        for index in range(n_stages):
+            if index % len(points) == number and index // len(points) < n_tiles:
+
+                @pl.when(tile == index // len(points))
+                def _():
+                    finish(index)
 
     @pl.loop(0, n_tiles)
     def _(tile):
         cols = aligned(tile * TILE, TILE)
         forward(1, aligned(own_rows + tile * TILE, TILE), True)
+        point(tile, 0)
         bins = bins_ref[:, aligned(mine * own_rows + tile * TILE, TILE)]
         frac = frac_ref[:, aligned(mine * own_rows + tile * TILE, TILE)]
         z = dot(rw2_t[...], hid[...], 1, 1)
@@ -427,30 +618,11 @@
         sum_acc[pl.ds(8, 8), :] += dot(jnp.ones((8, TILE), BF16), dlog[...], 1, 1)
         rg2t[...] += dot(dlog[...], hid[...])
         dh[...] = dot(dlog[...], rw2_t[...], 0, 0)
-        backward(1, d_rew, tile * TILE)
-        g1[:, pl.ds(hid_width, hid_width)] += dot(x_t[:, cols], d_rew[cols, :])
-
-    loads[3].wait()
-    next_copy(1).wait_recv()
-
-    @pl.loop(0, n_tiles)
-    def _(tile):
-        cols = aligned(tile * TILE, TILE)
-        forward(0, aligned(own_rows + tile * TILE, TILE), True)
-        simnorm(1, tile, dpl, pair * chip_cols, tile * TILE)
-        local, remote = lat_copies(1, tile)
-        local.start()
-        remote.start()
-        dpl_copy(tile).wait_recv()
-        d_lat = dpl[:, cols]
-        b2_acc[...] += dot(jnp.ones((8, TILE), BF16), d_lat, 1, 1)
-        g2t[...] += dot(d_lat, hid[...])
-        dh[...] = dot(d_lat, w2_t[...], 0, 0)
-        backward(0, d_pre, 0)
-        g1[:, pl.ds(0, hid_width)] += dot(x_t[:, cols], d_pre[...])
+        backward(1, d_pre, 0)
+        point(tile, 1)
         lat_rows = pl.ds(0, lat_width)
-        lg = dot(d_pre[...], w1_raw[lat_rows, pl.ds(0, hid_width)], 1, 1)
-        lg = lg + dot(d_rew[cols, :], w1_raw[lat_rows, pl.ds(hid_width, hid_width)], 1, 1)
+        lg = dot(d_dyn[cols, :], w1_raw[lat_rows, pl.ds(0, hid_width)], 1, 1)
+        lg = lg + dot(d_pre[...], w1_raw[lat_rows, pl.ds(hid_width, hid_width)], 1, 1)
         lg = (lg * total_rows).astype(BF16)
         for device in range(n_mp):
             lg_stage[device, cols, :] = lg[:, device * share : (device + 1) * share]
@@ -458,37 +630,58 @@
         local.start()
         for remote in remotes:
             remote.start()
-
+        g1[:, pl.ds(hid_width, hid_width)] += dot(x_t[:, cols], d_pre[...])
+        point(tile, 2)
+
+    for index in range(n_tiles * len(points), n_stages):
+        finish(index)
+
+    add_columns(1)
+    fill_rows = part_rew.shape[3]
     for device in range(n_mp):
-        for net in range(2):
-            wide = pl.ds(net * hid_width + device * shard, shard)
-            cols = pl.ds(net * shard, shard)
-            ga_ref[device, :, cols] = g1[pl.ds(0, ga_ref.shape[1]), wide].astype(BF16)
-        block_cols = pl.ds(device * shard, shard)
-        gb_ref[device, pl.ds(0, lat_width), :] = g2t[:, block_cols].astype(BF16)
-        gb_ref[device, pl.ds(lat_width, LANES), :] = rg2t[:, block_cols].astype(BF16)
+        cols = pl.ds(hid_width + device * shard, shard)
+        block = pl.ds(device * shard, shard)
+        where = (device % 2, device // 2)
+        part_rew[(0,) + where] = g1[pl.ds(0, fill_rows), cols].astype(BF16)
+        part_rew[(1,) + where + (pl.ds(0, in_rows - fill_rows),)] = g1[
+            pl.ds(fill_rows, in_rows - fill_rows), cols
+        ].astype(BF16)
+        part_rew[(1,) + where + (pl.ds(in_rows - fill_rows, LANES),)] = rg2t[:, block].astype(BF16)
+    n_embed = embed_ref.shape[1]
     tasks = g1[pl.ds(lat_width, n_task), :]
-    n_embed = embed_ref.shape[1]
-    ge_ref[...] = split_dot(tasks, w1_raw[pl.ds(lat_width, n_embed), :], 1, 1)
+    table = split_dot(tasks, w1_raw[pl.ds(lat_width, n_embed), :], 1, 1).astype(BF16)
+    spare = in_rows - fill_rows - 32
+    for device in range(n_mp):
+        where = (1, device % 2, device // 2)
+        part_rew[where + (pl.ds(spare, 32), pl.ds(0, n_embed))] = table[0:32]
+        part_rew[where + (pl.ds(spare, 32), pl.ds(LANES, n_embed))] = table[32:64]
+        part_rew[where + (pl.ds(fill_rows - 16, 16), pl.ds(0, n_embed))] = table[64:80]
+    sums[0] = jnp.zeros(sums.shape[1:], F32)
+    sums[0, pl.ds(0, 1), :] = b2_acc[pl.ds(0, 1), :]
+    sums[0, pl.ds(1, 1), pl.ds(0, LANES)] = sum_acc[pl.ds(8, 1), :]
     cons = jnp.sum(sum_acc[pl.ds(0, 8), :])
     rew = jnp.sum(row_acc[...])
-    gs_ref[...] = jnp.zeros_like(gs_ref)
-    for device in range(n_mp):
-        for net in range(2):
-            wide = pl.ds(net * hid_width + device * shard, shard)
-            cols = pl.ds(net * shard, shard)
-            for line in range(2):
-                gs_ref[device, pl.ds(line, 1), cols] = jnp.sum(
-                    col_acc[pl.ds(8 * line, 8), wide], axis=0, keepdims=True
-                )
-        gs_ref[device, pl.ds(2, 1), :] = b2_acc[pl.ds(0, 1), :]
-        gs_ref[device, pl.ds(3, 1), pl.ds(0, LANES)] = sum_acc[pl.ds(8, 1), :]
-        gs_ref[device, pl.ds(4, 1), :] = jnp.full((1, lat_width), cons)
-        gs_ref[device, pl.ds(5, 1), :] = jnp.full((1, lat_width), rew)
-
-    for index in range(len(w_pairs)):
-        for flip in (1, 2, 3):
-            weight_copy(index, flip).wait_send()
+    sums[0, pl.ds(2, 1), :] = jnp.full((1, lat_width), cons)
+    sums[0, pl.ds(3, 1), :] = jnp.full((1, lat_width), rew)
+    parts = [
+        reduction(
+            1 + k, part_rew.at[k], got_rew.at[k], fin_rew.at[pl.ds(k * fill_rows, fill_rows), :], k == 0
+        )
+        for k in range(2)
+    ]
+    for part in parts:
+        part[0](0)
+    for index in range(parts[0][3]):
+        for part in parts:
+            part[1](index)
+    fin_sums[...] = sums[2 + n_bits]
+    drain_dyn()
+    for part in parts:
+        part[2]()
+
+    for index in range(6):
+        for kind in range(3):
+            weight_copy(index, kind).wait_send()
     for slot in range(2):
         next_copy(slot).wait_send()
 
@@ -507,7 +700,7 @@
             remote.wait()
 
 
-def run_main(n_mp, total_rows, args):
+def run_main(n_mp, n_dp, total_rows, args):
     latent, next_latent, w1, w2t = args[0], args[1], args[2], args[3]
     tok_rows, lat_width = latent.shape
     share = next_latent.shape[1]
@@ -518,23 +711,32 @@
     n_tiles = own // TILE
     embed = args[11]
     n_task, n_embed = embed.shape
-    ga_rows = lat_width + n_task + 16
+    n_bits = n_dp.bit_length() - 1
+    dyn_rows = in_rows + lat_width
+    rew_rows = (in_rows + LANES) // 2
+
+    def room(rows):
+        extra, length = 0, rows
+        for _ in range(n_bits):
+            length = length // 2 if length % 32 == 0 else length
+            extra += length
+        return 2 * rows + extra
+
     any_spec = pl.BlockSpec(memory_space=pl.ANY)
     vmem_spec = pl.BlockSpec(memory_space=pltpu.VMEM)
     shape = jax.ShapeDtypeStruct
     dma = pltpu.SemaphoreType.DMA
     return pl.pallas_call(
-        functools.partial(main_kernel, (n_mp, total_rows, hid_width)),
+        functools.partial(main_kernel, (n_mp, n_dp, total_rows, hid_width)),
         out_shape=(
             shape((tok_rows, share), BF16),
             shape((tok_rows, share), BF16),
-            shape((n_mp, ga_rows, 2 * shard), BF16),
-            shape((n_mp, in_rows, shard), BF16),
-            shape((n_mp, 8, lat_width), F32),
-            shape((n_task, n_embed), F32),
+            shape((dyn_rows, shard), BF16),
+            shape((2 * rew_rows, shard), BF16),
+            shape((8, lat_width), F32),
         ),
         in_specs=[any_spec] * 6 + [vmem_spec] * 8,
-        out_specs=[any_spec] * 2 + [vmem_spec] * 4,
+        out_specs=[any_spec] * 2 + [vmem_spec] * 3,
         scratch_shapes=[
             pltpu.VMEM((2 * own, in_rows), BF16),
             pltpu.VMEM((in_rows, own), BF16),
@@ -549,6 +751,12 @@
             pltpu.VMEM((2, 2, own, share), BF16),
             pltpu.VMEM((n_mp, own, share), BF16),
             pltpu.VMEM((own, hid_width), BF16),
+            pltpu.VMEM((2, 2, dyn_rows, shard), BF16),
+            pltpu.VMEM((2, 2, 2, rew_rows, shard), BF16),
+            pltpu.VMEM((2, room(dyn_rows), shard), BF16),
+            pltpu.VMEM((2, 2, room(rew_rows), shard), BF16),
+            pltpu.VMEM((3 + n_bits, 8, lat_width), F32),
+            pltpu.VMEM((2 + n_bits, 8, lat_width), F32),
             pltpu.VMEM((in_rows, 2 * hid_width), F32),
             pltpu.VMEM((lat_width, hid_width), F32),
             pltpu.VMEM((LANES, hid_width), F32),
@@ -578,6 +786,10 @@
             dma((n_tiles,)),
             dma((3, n_tiles)),
             dma((3, n_tiles)),
+            dma((3, 2 + 2 * n_bits)),
+            dma((3, 2 + 2 * n_bits)),
+            dma((2 + n_bits,)),
+            dma((2 + n_bits,)),
         ],
         compiler_params=pltpu.CompilerParams(
             collective_id=0, has_side_effects=True, vmem_limit_bytes=60 << 20
@@ -660,40 +872,42 @@
         b2,
         rb2,
     )
-    latents, latent_grad, ga, gb, gs, ge = run_main(n_mp, total_rows, args)
-    ga = lax.psum_scatter(ga, "mp", scatter_dimension=0, tiled=True)
-    gb = lax.psum_scatter(gb, "mp", scatter_dimension=0, tiled=True)
-    gs = lax.psum_scatter(gs, "mp", scatter_dimension=0, tiled=True)
-    ga, gb = lax.psum((ga, gb), "dp")
-    gs = lax.psum(gs, "dp")
-    ge = lax.psum(ge, ("dp", "mp"))
-    ga, gb, gs = ga[0].astype(F32), gb[0].astype(F32), gs[0]
-    grad_task = jnp.dot(
-        task_embed.astype(F32).T,
-        ga[lat_width : lat_width + n_task],
-        precision=lax.Precision.HIGHEST,
+    n_dp = lax.axis_size("dp")
+    latents, latent_grad, dyn, rew, sums = run_main(n_mp, n_dp, total_rows, args)
+    dyn = dyn.astype(F32)
+    rew = rew.astype(F32)
+    first = lat_width + n_task
+    tasks = jnp.concatenate([dyn[lat_width:first], rew[lat_width:first]], axis=1)
+    grad_task = jnp.dot(task_embed.astype(F32).T, tasks, precision=lax.Precision.HIGHEST)
+
+    def first_grads(net, task):
+        return (
+            jnp.concatenate([net[:lat_width], net[first : first + n_act], task]),
+            net[first + n_act],
+            net[first + 8],
+            net[first + 9],
+        )
+
+    spare = in_rows - 32
+    grad_embed = jnp.concatenate(
+        [
+            rew[spare : spare + 32, :n_embed],
+            rew[spare : spare + 32, LANES : LANES + n_embed],
+            rew[in_rows + LANES - 16 :, :n_embed],
+        ]
     )
-    first = lat_width + n_task
-    grad_w1 = jnp.concatenate([ga[:lat_width], ga[first : first + n_act], grad_task])
-    grad_b1 = ga[first + n_act]
-    losses = jnp.stack([gs[4, 0], gs[5, 0]]) / total_rows
+    losses = jnp.stack([sums[2, 0], sums[3, 0]]) / total_rows
     return (
         latents,
         latent_grad,
         losses,
-        ge,
-        grad_w1[:, :shard],
-        grad_b1[:shard],
-        gs[0, :shard],
-        gs[1, :shard],
-        grad_w1[:, shard:],
-        grad_b1[shard:],
-        gs[0, shard:],
-        gs[1, shard:],
-        gb[:lat_width].T,
-        gs[2],
-        gb[lat_width : lat_width + n_bins].T,
-        gs[3, :n_bins],
+        grad_embed,
+        *first_grads(dyn, grad_task[:, :shard]),
+        *first_grads(rew, grad_task[:, shard:]),
+        dyn[in_rows:].T,
+        sums[0],
+        rew[in_rows : in_rows + n_bins].T,
+        sums[1, :n_bins],
     )
 
 

time: 324 us -> 205 us (0.63)
  waiting for transfers between devices: 85 us -> 0 us
  blocking collectives: 77.2 us -> 0 us
  Pallas kernels: 125 us -> 173 us
  between operations: 14.1 us -> 0.92 us
  local copies, waits for them, and re-layouts: 15.2 us -> 22.9 us
    psum x2 -> x0, blocking collectives: 77.2 us -> none  [the longest x1 40.2 us: on_device(): ge = lax.psum(ge, ('dp', 'mp'))]
    reduce_scatter x3 -> x0, waiting for transfers between devices: 62.1 us -> none  [the longest x1 36.6 us: on_device(): ga = lax.psum_scatter(ga, 'mp', scatter_dimension=0, tiled=True)]
    pallas_call x1, Pallas kernels: 125 us -> 173 us  [run_main(): pl.pallas_call(functools.partial(main_kernel, (n_mp, n_dp, total_rows, hi...]
    psum x1 -> x0, waiting for transfers between devices: 21.5 us -> none  [on_device(): ga, gb = lax.psum((ga, gb), 'dp')]
    slice x7 -> x12, local copies, waits for them, and re-layouts: 3.44 us -> 7.91 us  [the longest x1 1.3 us: on_device(): sums[0]]
  transfers between devices with their start and end apart: 4 -> 0, of which waited for: 3 -> 0; matrix products, arithmetic and copies ran while one was open for 1% -> 0% of each run, Pallas kernels for 0% -> 0%
where the time goes in v2:
time: 205 us; the launch traced here: 204 us
  Pallas kernels  173 us (84%)
  local copies, waits for them, and re-layouts  22.9 us (11%)
  other arithmetic  6.93 us (3%)
    pallas_call x1, Pallas kernels, run_main(): pl.pallas_call(functools.partial(main_kernel, (n_mp, n_dp, total_rows, hi...  173 us
    unnamed x38, local copies, waits for them, and re-layouts  5.59 us

profile of v2, /device:TPU:0, one launch (start us, length us, event | category | flops | bytes accessed | tf_op | source)
XLA Modules:
  0.0 204.4 jit_solution(9831214807421700239)
XLA Ops:
  0.7 0.7 slice.89
  1.4 0.8 slice.88
  2.3 1.0 slice.87
  3.4 0.7 slice.92
  4.1 0.8 slice.91
  4.9 1.0 slice.90
  6.1 0.9 pad_maximum_fusion.w1_in
  7.0 0.8 copy.36
  7.9 0.6 pad.8.rw2t_in
  8.6 0.6 pad_maximum_fusion.4.vecs_in
  9.4 0.8 maximum_maximum_fusion.act_ref
  10.2 0.7 maximum_maximum_fusion.1.masks_ref
  10.9 0.8 broadcast_in_dim.40.b2_ref
  11.7 0.7 broadcast_in_dim.41.rb2_ref
  12.4 173.4 %shard_map.315 = (bf16[8192,128]{1,0:T(8,128)(2,1)}, bf16[8192,128]{1,0:T(8,128)(2,1)}, bf16[1152,256]{1,0:T(8,128)(2,1)}, bf16[768,256]{1,0:T(8,128)(2,1)}, f32[8,512]{1,0:T(8,128)}) custom-call(bf16[8192,512]{1,0:T(8,128)(2,1)} %latent_in.1, bf16[8192,128]{1,0:T(8,128)(2,1)} %next_in.1, bf16[2,640,256]{2,1,0:T(8,128)(2,1)} %pad_maximum_fusion.w1_in, ...), custom_call_target="tpu_custom_call" | custom-call | tf_op jit(solution)/shard_map/pallas_call | solution.py:729
  185.8 1.3 fusion.8
  187.1 1.9 maximum_multiply_fusion
  189.0 0.7 slice.118
  189.7 0.7 fusion.6
  190.4 0.6 pad_maximum_fusion.3
  191.0 0.8 slice.122
  191.8 0.8 slice.121
  192.9 0.7 slice.120
  193.6 1.1 slice.119
  194.7 1.1 pad_maximum_fusion.1
  196.6 1.0 copy.37
  197.6 1.3 slice.113
  198.9 0.7 slice_bitcast_fusion.1
  199.6 1.2 slice_bitcast_fusion.2
  200.8 1.3 copy.40
  202.1 1.0 copy-done.2
  203.1 1.3 copy.41
  (54 shorter events, 1.7 us)
Async XLA Ops:
  0.6 6.4 %copy-start.4 = (bf16[256,512]{1,0:T(8,128)(2,1)S(1)}, bf16[256,512]{1,0:T(8,128)(2,1)}, u32[]{:S(2)}) copy-start(bf16[256,512]{1,0:T(8,128)(2,1)} %param.36) | copy-start | bytes 786436
  2.2 5.7 %copy-start.7 = (bf16[256,101]{0,1:T(8,128)(2,1)S(1)}, bf16[256,101]{0,1:T(8,128)(2,1)}, u32[]{:S(2)}) copy-start(bf16[256,101]{0,1:T(8,128)(2,1)} %param.38) | copy-start | bytes 155140
  2.2 6.3 %copy-start.10 = (f32[256]{0:T(256)S(1)}, f32[256]{0:T(256)}, u32[]{:S(2)}) copy-start(f32[256]{0:T(256)} %param.33) | copy-start | bytes 3076
  2.2 6.3 %copy-start.11 = (f32[256]{0:T(256)S(1)}, f32[256]{0:T(256)}, u32[]{:S(2)}) copy-start(f32[256]{0:T(256)} %param.34) | copy-start | bytes 3076
  2.2 6.3 %copy-start.12 = (f32[256]{0:T(256)S(1)}, f32[256]{0:T(256)}, u32[]{:S(2)}) copy-start(f32[256]{0:T(256)} %param.35) | copy-start | bytes 3076
  2.3 6.3 %copy-start.13 = (f32[256]{0:T(256)S(1)}, f32[256]{0:T(256)}, u32[]{:S(2)}) copy-start(f32[256]{0:T(256)} %param.29) | copy-start | bytes 3076
  2.3 6.3 %copy-start.14 = (f32[256]{0:T(256)S(1)}, f32[256]{0:T(256)}, u32[]{:S(2)}) copy-start(f32[256]{0:T(256)} %param.30) | copy-start | bytes 3076
  2.3 6.3 %copy-start.15 = (f32[256]{0:T(256)S(1)}, f32[256]{0:T(256)}, u32[]{:S(2)}) copy-start(f32[256]{0:T(256)} %param.31) | copy-start | bytes 3076
  3.3 6.1 %copy-start.5 = (bf16[6,8192]{1,0:T(8,128)(2,1)S(1)}, bf16[6,8192]{1,0:T(8,128)(2,1)}, u32[]{:S(2)}) copy-start(bf16[6,8192]{1,0:T(8,128)(2,1)} %param.21) | copy-start | bytes 294916
  4.9 5.3 %copy-start.8 = (s32[80,6]{0,1:T(8,128)S(1)}, s32[80,6]{0,1:T(8,128)}, u32[]{:S(2)}) copy-start(s32[80,6]{0,1:T(8,128)} %param.23) | copy-start | bytes 5764
  4.9 5.9 %copy-start.9 = (f32[512]{0:T(512)S(1)}, f32[512]{0:T(512)}, u32[]{:S(2)}) copy-start(f32[512]{0:T(512)} %param.37) | copy-start | bytes 6148
  5.9 5.8 %copy-start.16 = (f32[101]{0:T(128)S(1)}, f32[101]{0:T(128)}, u32[]{:S(2)}) copy-start(f32[101]{0:T(128)} %param.39) | copy-start | bytes 1216
  12.4 180.1 %copy-start.6 = (bf16[80,96]{1,0:T(8,128)(2,1)S(1)}, bf16[80,96]{1,0:T(8,128)(2,1)}, u32[]{:S(2)}) copy-start(bf16[80,96]{1,0:T(8,128)(2,1)} %embed_ref.1) | copy-start | bytes 46084
  185.8 8.8 %copy-start = (bf16[768,256]{1,0:T(8,128)(2,1)S(1)}, bf16[768,256]{1,0:T(8,128)(2,1)}, u32[]{:S(2)}) copy-start(bf16[768,256]{1,0:T(8,128)(2,1)} %get-tuple-element.24) | copy-start | bytes 1179652
  193.6 2.3 %copy-start.1 = (bf16[1152,256]{1,0:T(8,128)(2,1)S(1)}, bf16[1152,256]{1,0:T(8,128)(2,1)}, u32[]{:S(2)}) copy-start(bf16[1152,256]{1,0:T(8,128)(2,1)} %get-tuple-element.25) | copy-start | bytes 1769476
  196.5 4.2 %copy-start.3 = (bf16[8192,128]{1,0:T(8,128)(2,1)S(1)}, bf16[8192,128]{1,0:T(8,128)(2,1)}, u32[]{:S(2)}) copy-start(bf16[8192,128]{1,0:T(8,128)(2,1)} %get-tuple-element.77) | copy-start | bytes 6291460
  200.8 2.3 %copy-start.2 = (bf16[8192,128]{1,0:T(8,128)(2,1)S(1)}, bf16[8192,128]{1,0:T(8,128)(2,1)}, u32[]{:S(2)}) copy-start(bf16[8192,128]{1,0:T(8,128)(2,1)} %get-tuple-element.78) | copy-start | bytes 6291460

commit v3 on v2

--- a/solution.py
+++ b/solution.py
@@ -13,7 +13,10 @@
 EPS = 1e-05
 LANES = 128
 TILE = 512
-SUB = 64
+SUB = 128
+PART = 64
+FIRST = (0, 3, 5, 6, 7, 8, 9, 11)
+SECOND = (1, 6, 8, 10, 11)
 MESH = pl.DeviceIdType.MESH
 F32 = jnp.float32
 BF16 = jnp.bfloat16
@@ -43,18 +46,24 @@
     sizes,
     latent_in,
     next_in,
-    w1_in,
-    w2t_in,
-    rw2t_in,
-    vecs_in,
+    dyn_w1,
+    rew_w1,
+    dyn_w2,
+    rew_w2,
+    dyn_b1,
+    dyn_gain,
+    dyn_shift,
+    rew_b1,
+    rew_gain,
+    rew_shift,
     ids_ref,
     act_ref,
     masks_ref,
     bins_ref,
     frac_ref,
     embed_ref,
-    b2_ref,
-    rb2_ref,
+    dyn_b2,
+    rew_b2,
     lat_out,
     grad_out,
     fin_dyn,
@@ -67,15 +76,24 @@
     w2_t,
     rw2_t,
     vecs,
+    w2_own,
+    rw2_own,
+    vecs_own,
+    embed_wide,
+    extra_rows,
+    b2_ref,
+    rb2_ref,
     next_lat,
     dpl,
     dpl_send,
     lat_stage,
     lg_stage,
     d_dyn,
-    part_dyn,
+    part_a,
+    part_b,
     part_rew,
-    got_dyn,
+    got_a,
+    got_b,
     got_rew,
     sums,
     got_sums,
@@ -121,7 +139,9 @@
     half = mine % 2
     own_rows = x_all.shape[0] // 2
     lat_width = latent_in.shape[1]
-    shard = w1_in.shape[2]
+    shard = dyn_w1.shape[1]
+    n_act = act_ref.shape[0]
+    in_rows = g1.shape[0]
     share = next_in.shape[1]
     n_task = embed_ref.shape[0]
     chip_cols = 2 * share
@@ -143,6 +163,15 @@
 
     def rows_of(device):
         return aligned(device * own_rows, own_rows)
+
+    vecs_own[...] = jnp.zeros_like(vecs_own)
+    for net, rows in enumerate(((dyn_b1, dyn_gain, dyn_shift), (rew_b1, rew_gain, rew_shift))):
+        for line, ref in enumerate(rows):
+            vecs_own[net, pl.ds(line, 1), :] = ref[...]
+    w2_own[...] = dyn_w2[...].T
+    n_bins = rew_w2.shape[0]
+    rw2_own[...] = jnp.zeros_like(rw2_own)
+    rw2_own[pl.ds(0, n_bins), :] = rew_w2[...]
 
     barrier = pltpu.get_barrier_semaphore()
     for flip in (1, 2, 3):
@@ -161,14 +190,14 @@
         pairs = []
         for net in range(2):
             cols = aligned(net * hid_width + block * shard, shard)
-            pairs.append((w1_in.at[net], w1_raw.at[:, cols]))
-            pairs.append((vecs_in.at[net], vecs.at[:, cols]))
+            pairs.append(((dyn_w1, rew_w1)[net], w1_raw.at[:, cols]))
+            pairs.append((vecs_own.at[net], vecs.at[:, cols]))
         cols = aligned(block * shard, shard)
-        pairs.append((w2t_in, w2_t.at[:, cols]))
-        pairs.append((rw2t_in, rw2_t.at[:, cols]))
+        pairs.append((w2_own, w2_t.at[:, cols]))
+        pairs.append((rw2_own, rw2_t.at[:, cols]))
         return pairs
 
-    w_needs = ((0, 1, 4), (2, 3, 5))
+    w_needs = ((1, 0, 4), (3, 2, 5))
     own_weights = w_pairs(mine)
 
     def weight_copy(index, kind):
@@ -221,6 +250,19 @@
     for ref in (g1, g2t, rg2t, col_acc, sum_acc, row_acc, b2_acc):
         ref[...] = jnp.zeros_like(ref)
 
+    line = lax.broadcasted_iota(jnp.int32, extra_rows.shape, 0)
+    extra_rows[...] = jnp.where((line == n_act) | (line == n_act + 1), 1.0, 0.0)
+    n_embed = embed_ref.shape[1]
+    n_rest = n_act + n_embed
+    moved = lax.broadcasted_iota(jnp.int32, (n_embed, n_rest), 1) == (
+        lax.broadcasted_iota(jnp.int32, (n_embed, n_rest), 0) + n_act
+    )
+    embed_wide[...] = dot(embed_ref[...], jnp.where(moved, 1.0, 0.0).astype(BF16)).astype(BF16)
+    b2_ref[...] = jnp.broadcast_to(dyn_b2[...], (LANES, lat_width)).T
+    rb2_ref[...] = jnp.full(rb2_ref.shape, -1e30, F32)
+    rb2_ref[:, pl.ds(0, n_bins)] = jnp.broadcast_to(rew_b2[...], (LANES, n_bins))
+    rb2_ref[...] = rb2_ref[...].T
+
     for slot, device in ((0, across), (1, mine)):
         base = device * own_rows
 
@@ -230,8 +272,9 @@
             ids = ids_ref[:, lanes]
             tasks = lax.broadcasted_iota(jnp.int32, (n_task, TILE), 0)
             onehot = jnp.where(tasks == ids, 1.0, 0.0).astype(BF16)
-            masks = dot(masks_ref[...], onehot)
-            masked = (act_ref[:, lanes].astype(F32) * masks).astype(BF16)
+            masks = dot(masks_ref[...].astype(F32).astype(BF16), onehot)
+            extra_rows[pl.ds(0, n_act), :] = act_ref[:, lanes].astype(F32) * masks
+            masked = extra_rows[...].astype(BF16)
             rest = LANES - n_task - masked.shape[0]
             extra = jnp.concatenate([onehot, masked, jnp.zeros((rest, TILE), BF16)], axis=0)
             rows = aligned(slot * own_rows + tile * TILE, TILE)
@@ -262,35 +305,31 @@
             weight_copy(index, 2).wait_recv()
         cols = pl.ds(net * hid_width, hid_width)
 
-        @pl.loop(0, lat_width // SUB)
+        @pl.loop(0, lat_width // PART)
         def _(step):
-            rows = aligned(step * SUB, SUB)
+            rows = aligned(step * PART, PART)
             w1_c[rows, cols] = centre(w1_raw[rows, cols].astype(F32)).astype(BF16)
 
-        n_embed = embed_ref.shape[1]
-        table = dot(embed_ref[...], w1_raw[pl.ds(lat_width, n_embed), cols])
+        table = dot(embed_wide[...], w1_raw[pl.ds(lat_width, n_rest), cols])
         w1_c[pl.ds(lat_width, n_task), cols] = centre(table).astype(BF16)
-        act = centre(w1_raw[pl.ds(lat_width + n_embed, 16), cols].astype(F32))
+        act = centre(w1_raw[pl.ds(lat_width, 16), cols].astype(F32))
         bias = centre(vecs[pl.ds(0, 1), cols])
         high = bias.astype(BF16).astype(F32)
         row = lax.broadcasted_iota(jnp.int32, act.shape, 0)
-        act = jnp.where(row == 6, high, jnp.where(row == 7, bias - high, act))
+        act = jnp.where(row < n_act, act, 0.0)
+        act = jnp.where(row == n_act, high, jnp.where(row == n_act + 1, bias - high, act))
         w1_c[pl.ds(lat_width + n_task, 16), cols] = act.astype(BF16)
         rest = LANES - n_task - 16
         w1_c[pl.ds(lat_width + n_task + 16, rest), cols] = jnp.zeros((rest, hid_width), BF16)
 
     def forward(net, rows, keep):
         cols = pl.ds(net * hid_width, hid_width)
-        pre[...] = dot(x_all[rows, :], w1_c[:, cols])
-
-        @pl.loop(0, TILE // SUB)
-        def _(step):
-            part = aligned(step * SUB, SUB)
-            values = pre[part, :]
-            square = jnp.sum(values * values, axis=1, keepdims=True)
-            inv_ref[part, :] = jnp.broadcast_to(
-                lax.rsqrt(square * (1.0 / hid_width) + EPS), (SUB, LANES)
-            )
+        values = dot(x_all[rows, :], w1_c[:, cols])
+        pre[...] = values
+        square = jnp.sum(values * values, axis=1, keepdims=True)
+        inv_ref[...] = jnp.broadcast_to(
+            lax.rsqrt(square * (1.0 / hid_width) + EPS), (TILE, LANES)
+        )
 
         @pl.loop(0, TILE // SUB)
         def _(step):
@@ -354,23 +393,23 @@
         for side in range(2):
             latt[pl.ds(side * share, share), :] = next_lat[slot, side, rows, :].T.astype(F32)
 
-        @pl.loop(0, chip_cols // SUB)
+        @pl.loop(0, chip_cols // PART)
         def _(step):
-            part = aligned(step * SUB, SUB)
-            bias = b2_ref[aligned(pair * chip_cols + step * SUB, SUB), :]
+            part = aligned(step * PART, PART)
+            bias = b2_ref[aligned(pair * chip_cols + step * PART, PART), :]
             for lane in range(TILE // LANES):
                 lanes = pl.ds(lane * LANES, LANES)
-                z = (zt[part, lanes] + bias).reshape(SUB // GROUP, GROUP, LANES)
+                z = (zt[part, lanes] + bias).reshape(PART // GROUP, GROUP, LANES)
                 e = jnp.exp(z - jnp.max(z, axis=1, keepdims=True))
                 s = e * (1.0 / jnp.sum(e, axis=1, keepdims=True))
                 error = s - latt[part, lanes].reshape(z.shape)
                 sum_acc[pl.ds(0, 8), :] += jnp.sum(error * error, axis=0)
                 d_lat = d_scale * error
                 d_z = s * (d_lat - jnp.sum(s * d_lat, axis=1, keepdims=True))
-                zt[part, lanes] = s.reshape(SUB, LANES)
+                zt[part, lanes] = s.reshape(PART, LANES)
                 target[
-                    aligned(row + step * SUB, SUB), aligned(col + lane * LANES, LANES)
-                ] = d_z.reshape(SUB, LANES).astype(BF16)
+                    aligned(row + step * PART, PART), aligned(col + lane * LANES, LANES)
+                ] = d_z.reshape(PART, LANES).astype(BF16)
 
         for side in range(2):
             lat_stage[slot, side, rows, :] = zt[pl.ds(side * share, share), :].astype(BF16).T
@@ -464,40 +503,43 @@
             total = target[rows, :].astype(F32) + other[rows, :].astype(F32)
             target[rows, :] = total.astype(BF16)
 
-    def reduction(key, part, got, fin, with_sums):
+    def reduction(key, part, got, fin, order, with_sums):
         n_rows = part.shape[2]
-        stages = [("near", 0, n_rows), ("across", 0, n_rows)]
-        offset, length = 0, n_rows
-        place = 3 * n_rows
-        gathers = []
-        for bit in range(n_bits):
-            if length % 32 == 0:
+        stages, gathers = [], []
+        offset, length, place, both = 0, n_rows, n_rows, True
+        for what in order:
+            if what == "near":
+                stages.append((what, 0, 0, 0, n_rows, 0, True))
+                continue
+            if what == "across":
+                both = False
+                stages.append((what, 0, offset, offset, length, place, False))
+            elif length % 32 == 0:
                 length //= 2
-                keep = offset + bit_of(bit) * length
-                stages.append(("half", bit, offset + (1 - bit_of(bit)) * length, keep, length, place))
-                gathers.append(("gather", bit, keep, length))
+                keep = offset + bit_of(what) * length
+                send = offset + (1 - bit_of(what)) * length
+                stages.append(("half", what, send, keep, length, place, both))
+                gathers.append(("gather", what, keep, keep, length, 0, False))
                 offset = keep
             else:
-                stages.append(("whole", bit, offset, offset, length, place))
+                stages.append(("whole", what, offset, offset, length, place, both))
             place += length
         last = len(stages)
         stages += gathers[::-1]
-        whole = part.at[half, pair]
 
         def ends(index):
-            stage = stages[index]
-            kind = stage[0]
+            kind, bit, send, keep, count, spot, two = stages[index]
             if kind == "near":
                 return part.at[1 - half], got.at[:, pl.ds(0, n_rows), :], {"mp": near}
+            rows, spots = aligned_to(send, count), pl.ds(spot, count)
             if kind == "across":
-                return part.at[half, 1 - pair], got.at[0, pl.ds(n_rows, n_rows), :], {"mp": across}
-            device = {"dp": column_peer(stage[1])}
+                return part.at[half, 1 - pair, rows, :], got.at[0, spots, :], {"mp": across}
+            device = {"dp": column_peer(bit)}
             if kind == "gather":
-                rows = aligned_to(stage[2], stage[3])
                 return fin.at[rows, :], fin.at[rows, :], device
-            rows = aligned_to(stage[2], stage[4])
-            base = 2 * n_rows + stage[5] - 3 * n_rows
-            return whole.at[rows, :], got.at[0, pl.ds(base, stage[4]), :], device
+            if two:
+                return part.at[half, :, rows, :], got.at[:, spots, :], device
+            return part.at[half, pair, rows, :], got.at[0, spots, :], device
 
         def copy(index):
             source, target, device = ends(index)
@@ -526,31 +568,23 @@
                 sums_copy(index).start()
 
         def finish(index):
-            stage = stages[index]
-            kind = stage[0]
+            kind, bit, send, keep, count, spot, two = stages[index]
             if kind == "whole":
                 copy(index).wait_send()
             copy(index).wait_recv()
             if with_sums and index < last:
                 sums_copy(index).wait_recv()
                 sums[index + 1] = sums[index] + got_sums[index]
-            if kind == "near":
-                for other in range(2):
-                    add_into(
-                        part.at[half, other], got.at[other, pl.ds(0, n_rows), :], n_rows
-                    )
-            elif kind == "across":
-                add_into(whole, got.at[0, pl.ds(n_rows, n_rows), :], n_rows)
-            elif kind != "gather":
-                base = 2 * n_rows + stage[5] - 3 * n_rows
-                add_into(
-                    whole.at[aligned_to(stage[3], stage[4]), :],
-                    got.at[0, pl.ds(base, stage[4]), :],
-                    stage[4],
-                )
+            if kind != "gather":
+                rows, spots = aligned_to(keep, count), pl.ds(spot, count)
+                for side in range(2):
+                    if two:
+                        add_into(part.at[half, side, rows, :], got.at[side, spots, :], count)
+                    elif side == 0:
+                        add_into(part.at[half, pair, rows, :], got.at[0, spots, :], count)
             if index + 1 == last:
                 rows = aligned_to(offset, length)
-                fin[rows, :] = whole[rows, :]
+                fin[rows, :] = part[half, pair, rows, :]
             if index + 1 < len(stages):
                 start(index + 1)
 
@@ -577,24 +611,37 @@
                 col_acc[pl.ds(8 * line, 8), cols], axis=0, keepdims=True
             )
 
-    in_rows = g1.shape[0]
+    bits = list(range(n_bits))
     add_columns(0)
-    fill(part_dyn, 0, 0, in_rows, g1, 0)
-    fill(part_dyn, 0, in_rows, lat_width, g2t, 0)
-    start, finish, drain_dyn, n_stages = reduction(0, part_dyn, got_dyn, fin_dyn, False)
-    start(0)
-    points = [0, 1, 2]
-    waiting = list(range(n_stages))
+    fill(part_a, 0, 0, lat_width, g2t, 0)
+    fill(part_b, 0, 0, in_rows, g1, 0)
+    chunks = [
+        reduction(0, part_a, got_a, fin_dyn.at[pl.ds(in_rows, lat_width), :], ["near"] + bits + ["across"], False),
+        reduction(1, part_b, got_b, fin_dyn.at[pl.ds(0, in_rows), :], ["near"] + bits + ["across"], False),
+    ]
+    for chunk in chunks:
+        chunk[0](0)
+    n_stages = 2 + 2 * n_bits
+    per_tile = 3
+    events = [
+        (chunk, index, (FIRST, SECOND)[chunk][index])
+        for index in range(n_stages)
+        for chunk in range(2)
+        if index < min(chunks[chunk][3], len((FIRST, SECOND)[chunk]))
+    ]
+    inside = [event for event in events if event[2] < per_tile * n_tiles]
+    inside.sort(key=lambda event: event[2])
+    done = [(event[0], event[1]) for event in inside]
 
     prepare(1)
 
     def point(tile, number):
-        for index in range(n_stages):
-            if index % len(points) == number and index // len(points) < n_tiles:
-
-                @pl.when(tile == index // len(points))
+        for chunk, index, place in inside:
+            if place % per_tile == number:
+
+                @pl.when(tile == place // per_tile)
                 def _():
-                    finish(index)
+                    chunks[chunk][1](index)
 
     @pl.loop(0, n_tiles)
     def _(tile):
@@ -633,9 +680,6 @@
         g1[:, pl.ds(hid_width, hid_width)] += dot(x_t[:, cols], d_pre[...])
         point(tile, 2)
 
-    for index in range(n_tiles * len(points), n_stages):
-        finish(index)
-
     add_columns(1)
     fill_rows = part_rew.shape[3]
     for device in range(n_mp):
@@ -647,15 +691,14 @@
             pl.ds(fill_rows, in_rows - fill_rows), cols
         ].astype(BF16)
         part_rew[(1,) + where + (pl.ds(in_rows - fill_rows, LANES),)] = rg2t[:, block].astype(BF16)
-    n_embed = embed_ref.shape[1]
     tasks = g1[pl.ds(lat_width, n_task), :]
-    table = split_dot(tasks, w1_raw[pl.ds(lat_width, n_embed), :], 1, 1).astype(BF16)
+    table = split_dot(tasks, w1_raw[pl.ds(lat_width, n_rest), :], 1, 1).astype(BF16)
     spare = in_rows - fill_rows - 32
     for device in range(n_mp):
         where = (1, device % 2, device // 2)
-        part_rew[where + (pl.ds(spare, 32), pl.ds(0, n_embed))] = table[0:32]
-        part_rew[where + (pl.ds(spare, 32), pl.ds(LANES, n_embed))] = table[32:64]
-        part_rew[where + (pl.ds(fill_rows - 16, 16), pl.ds(0, n_embed))] = table[64:80]
+        part_rew[where + (pl.ds(spare, 32), pl.ds(0, n_rest))] = table[0:32]
+        part_rew[where + (pl.ds(spare, 32), pl.ds(LANES, n_rest))] = table[32:64]
+        part_rew[where + (pl.ds(fill_rows - 16, 16), pl.ds(0, n_rest))] = table[64:80]
     sums[0] = jnp.zeros(sums.shape[1:], F32)
     sums[0, pl.ds(0, 1), :] = b2_acc[pl.ds(0, 1), :]
     sums[0, pl.ds(1, 1), pl.ds(0, LANES)] = sum_acc[pl.ds(8, 1), :]
@@ -663,21 +706,29 @@
     rew = jnp.sum(row_acc[...])
     sums[0, pl.ds(2, 1), :] = jnp.full((1, lat_width), cons)
     sums[0, pl.ds(3, 1), :] = jnp.full((1, lat_width), rew)
-    parts = [
-        reduction(
-            1 + k, part_rew.at[k], got_rew.at[k], fin_rew.at[pl.ds(k * fill_rows, fill_rows), :], k == 0
+    orders = (["near", "across"] + bits, ["near"] + bits[:1] + ["across"] + bits[1:])
+    for k in range(2):
+        chunks.append(
+            reduction(
+                2 + k,
+                part_rew.at[k],
+                got_rew.at[k],
+                fin_rew.at[pl.ds(k * fill_rows, fill_rows), :],
+                orders[k],
+                k == 0,
+            )
         )
-        for k in range(2)
-    ]
-    for part in parts:
-        part[0](0)
-    for index in range(parts[0][3]):
-        for part in parts:
-            part[1](index)
+    chunks[2][0](0)
+    chunks[3][0](0)
+    left = [(c, index) for index in range(n_stages) for c in range(2) if (c, index) not in done]
+    left += [(c, index) for index in range(n_stages) for c in (2, 3)]
+    left.sort(key=lambda event: event[1] if event[0] > 1 else event[1] - len(done) // 2)
+    for chunk, index in left:
+        if index < chunks[chunk][3]:
+            chunks[chunk][1](index)
     fin_sums[...] = sums[2 + n_bits]
-    drain_dyn()
-    for part in parts:
-        part[2]()
+    for chunk in chunks:
+        chunk[2]()
 
     for index in range(6):
         for kind in range(3):
@@ -700,19 +751,108 @@
             remote.wait()
 
 
+def finish_kernel(
+    dyn,
+    rew,
+    sums,
+    embed,
+    losses,
+    grad_embed,
+    dyn_w1,
+    dyn_b1,
+    dyn_gain,
+    dyn_shift,
+    rew_w1,
+    rew_b1,
+    rew_gain,
+    rew_shift,
+    dyn_w2,
+    dyn_b2,
+    rew_w2,
+    rew_b2,
+    *,
+    total_rows,
+    lat_width,
+):
+    n_task, n_embed = embed.shape
+    n_rest = dyn_w1.shape[0] - lat_width
+    n_act = n_rest - n_embed
+    in_rows = lat_width + LANES
+    first = lat_width + n_task
+    moved = lax.broadcasted_iota(jnp.int32, (n_embed, n_rest), 1) == (
+        lax.broadcasted_iota(jnp.int32, (n_embed, n_rest), 0) + n_act
+    )
+    moved = jnp.where(moved, 1.0, 0.0).astype(BF16)
+    line = lax.broadcasted_iota(jnp.int32, (LANES - n_task, n_rest), 0)
+    lane = lax.broadcasted_iota(jnp.int32, (LANES - n_task, n_rest), 1)
+    acts = jnp.where((line == lane) & (line < n_act), 1.0, 0.0).astype(BF16)
+    mix = jnp.concatenate([dot(embed[...], moved).astype(BF16), acts], axis=0)
+    for net, w1, b1, gain, shift in (
+        (dyn, dyn_w1, dyn_b1, dyn_gain, dyn_shift),
+        (rew, rew_w1, rew_b1, rew_gain, rew_shift),
+    ):
+        w1[pl.ds(0, lat_width), :] = net[pl.ds(0, lat_width), :].astype(F32)
+        w1[pl.ds(lat_width, n_rest), :] = dot(mix, net[pl.ds(lat_width, LANES), :], 0, 0)
+        small = net[pl.ds(first, 16), :].astype(F32)
+        b1[...] = small[n_act : n_act + 1]
+        gain[...] = small[8:9]
+        shift[...] = small[9:10]
+    dyn_w2[...] = dyn[pl.ds(in_rows, lat_width), :].astype(F32).T
+    n_bins = rew_w2.shape[0]
+    rew_w2[...] = rew[pl.ds(in_rows, LANES), :].astype(F32)[:n_bins]
+    dyn_b2[...] = sums[pl.ds(0, 1), :]
+    rew_b2[...] = sums[pl.ds(1, 1), pl.ds(0, n_bins)]
+    pieces = (
+        (0, 32, in_rows - 32, 0),
+        (32, 32, in_rows - 32, LANES),
+        (64, n_task - 64, in_rows + LANES - 16, 0),
+    )
+    for to, count, row, col in pieces:
+        grad_embed[pl.ds(to, count), :] = dot(
+            rew[pl.ds(row, count), pl.ds(col, n_rest)], moved, 1, 1
+        )
+    pick = lax.broadcasted_iota(jnp.int32, losses.shape, 1) == 0
+    both = jnp.where(pick, sums[pl.ds(2, 1), pl.ds(0, 2)], sums[pl.ds(3, 1), pl.ds(0, 2)])
+    losses[...] = both * (1.0 / total_rows)
+
+
+def run_finish(total_rows, lat_width, n_in, n_bins, dyn, rew, sums, embed):
+    shape = jax.ShapeDtypeStruct
+    shard = dyn.shape[1]
+    line = shape((1, shard), F32)
+    first = [shape((n_in, shard), F32), line, line, line]
+    return pl.pallas_call(
+        functools.partial(finish_kernel, total_rows=total_rows, lat_width=lat_width),
+        out_shape=(
+            shape((1, 2), F32),
+            shape(embed.shape, F32),
+            *first,
+            *first,
+            shape((shard, lat_width), F32),
+            shape((1, lat_width), F32),
+            shape((n_bins, shard), F32),
+            shape((1, n_bins), F32),
+        ),
+        compiler_params=pltpu.CompilerParams(vmem_limit_bytes=32 << 20),
+    )(dyn, rew, sums, embed)
+
+
 def run_main(n_mp, n_dp, total_rows, args):
-    latent, next_latent, w1, w2t = args[0], args[1], args[2], args[3]
+    latent, next_latent, w1, dyn_w2, rew_w2 = args[0], args[1], args[2], args[4], args[5]
     tok_rows, lat_width = latent.shape
     share = next_latent.shape[1]
-    shard = w1.shape[2]
+    n_in, shard = w1.shape
     hid_width = n_mp * shard
     own = tok_rows // n_mp
     in_rows = lat_width + LANES
     n_tiles = own // TILE
-    embed = args[11]
-    n_task, n_embed = embed.shape
+    n_task = args[17].shape[0]
+    any_spec = pl.BlockSpec(memory_space=pl.ANY)
+    vmem_spec = pl.BlockSpec(memory_space=pltpu.VMEM)
+    shape = jax.ShapeDtypeStruct
+    dma = pltpu.SemaphoreType.DMA
     n_bits = n_dp.bit_length() - 1
-    dyn_rows = in_rows + lat_width
+    n_stages = 2 + 2 * n_bits
     rew_rows = (in_rows + LANES) // 2
 
     def room(rows):
@@ -731,29 +871,38 @@
         out_shape=(
             shape((tok_rows, share), BF16),
             shape((tok_rows, share), BF16),
-            shape((dyn_rows, shard), BF16),
+            shape((in_rows + lat_width, shard), BF16),
             shape((2 * rew_rows, shard), BF16),
             shape((8, lat_width), F32),
         ),
-        in_specs=[any_spec] * 6 + [vmem_spec] * 8,
+        in_specs=[any_spec] * 4 + [vmem_spec] * 16,
         out_specs=[any_spec] * 2 + [vmem_spec] * 3,
         scratch_shapes=[
             pltpu.VMEM((2 * own, in_rows), BF16),
             pltpu.VMEM((in_rows, own), BF16),
-            pltpu.VMEM((in_rows, 2 * hid_width), BF16),
+            pltpu.VMEM((n_in, 2 * hid_width), BF16),
             pltpu.VMEM((in_rows, 2 * hid_width), BF16),
             pltpu.VMEM((lat_width, hid_width), BF16),
             pltpu.VMEM((LANES, hid_width), BF16),
             pltpu.VMEM((8, 2 * hid_width), F32),
+            pltpu.VMEM((lat_width, shard), BF16),
+            pltpu.VMEM((LANES, shard), BF16),
+            pltpu.VMEM((2, 8, shard), F32),
+            pltpu.VMEM((n_task, n_in - lat_width), BF16),
+            pltpu.VMEM((16, TILE), F32),
+            pltpu.VMEM((lat_width, LANES), F32),
+            pltpu.VMEM((LANES, LANES), F32),
             pltpu.VMEM((2, 2, own, share), BF16),
             pltpu.VMEM((lat_width, own), BF16),
             pltpu.VMEM((2 * share, own), BF16),
             pltpu.VMEM((2, 2, own, share), BF16),
             pltpu.VMEM((n_mp, own, share), BF16),
             pltpu.VMEM((own, hid_width), BF16),
-            pltpu.VMEM((2, 2, dyn_rows, shard), BF16),
+            pltpu.VMEM((2, 2, lat_width, shard), BF16),
+            pltpu.VMEM((2, 2, in_rows, shard), BF16),
             pltpu.VMEM((2, 2, 2, rew_rows, shard), BF16),
-            pltpu.VMEM((2, room(dyn_rows), shard), BF16),
+            pltpu.VMEM((2, room(lat_width), shard), BF16),
+            pltpu.VMEM((2, room(in_rows), shard), BF16),
             pltpu.VMEM((2, 2, room(rew_rows), shard), BF16),
             pltpu.VMEM((3 + n_bits, 8, lat_width), F32),
             pltpu.VMEM((2 + n_bits, 8, lat_width), F32),
@@ -786,8 +935,8 @@
             dma((n_tiles,)),
             dma((3, n_tiles)),
             dma((3, n_tiles)),
-            dma((3, 2 + 2 * n_bits)),
-            dma((3, 2 + 2 * n_bits)),
+            dma((4, n_stages)),
+            dma((4, n_stages)),
             dma((2 + n_bits,)),
             dma((2 + n_bits,)),
         ],
@@ -819,96 +968,37 @@
     rew_w2,
     rew_b2,
 ):
-    n_mp = lax.axis_size("mp")
+    n_mp, n_dp = lax.axis_size("mp"), lax.axis_size("dp")
     tok_rows, lat_width = latent.shape
-    total_rows = tok_rows * lax.axis_size("dp")
-    n_act = actions.shape[0]
-    n_task, n_embed = task_embed.shape
-    n_bins = rew_w2.shape[1]
-    shard = dyn_w1.shape[1]
-    in_rows = lat_width + LANES
-
-    def first_layer(w1):
-        pad = jnp.zeros((in_rows - w1.shape[0], shard), BF16)
-        return jnp.concatenate(
-            [w1[:lat_width], w1[lat_width + n_act :], w1[lat_width : lat_width + n_act], pad]
-        )
-
-    w1 = jnp.stack([first_layer(dyn_w1), first_layer(rew_w1)])
-    none = jnp.zeros_like(dyn_b1)
-    vecs = jnp.stack(
-        [
-            jnp.stack([dyn_b1, dyn_gain, dyn_shift] + [none] * 5),
-            jnp.stack([rew_b1, rew_gain, rew_shift] + [none] * 5),
-        ]
-    )
-    rw2t = jnp.pad(rew_w2.T, ((0, LANES - n_bins), (0, 0)))
-    act = jnp.concatenate(
-        [actions, jnp.ones((2, tok_rows), BF16), jnp.zeros((14 - n_act, tok_rows), BF16)]
-    )
-    masks = jnp.concatenate(
-        [
-            action_masks.astype(BF16).T,
-            jnp.ones((2, n_task), BF16),
-            jnp.zeros((14 - n_act, n_task), BF16),
-        ]
-    )
-    b2 = jnp.broadcast_to(dyn_b2[:, None], (lat_width, LANES))
-    rb2 = jnp.pad(rew_b2, (0, LANES - n_bins), constant_values=-1e30)
-    rb2 = jnp.broadcast_to(rb2[:, None], (LANES, LANES))
+    total_rows = tok_rows * n_dp
+
+    def row(vector):
+        return vector.reshape(1, -1)
+
     args = (
         latent,
         next_latent,
-        w1,
-        dyn_w2.T,
-        rw2t,
-        vecs,
-        task_ids[None, :],
-        act,
-        masks,
-        reward_bins[None, :],
-        reward_frac[None, :],
+        dyn_w1,
+        rew_w1,
+        dyn_w2,
+        rew_w2.T,
+        *(row(v) for v in (dyn_b1, dyn_gain, dyn_shift, rew_b1, rew_gain, rew_shift)),
+        row(task_ids),
+        actions,
+        action_masks.T,
+        row(reward_bins),
+        row(reward_frac),
         task_embed,
-        b2,
-        rb2,
+        row(dyn_b2),
+        row(rew_b2),
     )
-    n_dp = lax.axis_size("dp")
     latents, latent_grad, dyn, rew, sums = run_main(n_mp, n_dp, total_rows, args)
-    dyn = dyn.astype(F32)
-    rew = rew.astype(F32)
-    first = lat_width + n_task
-    tasks = jnp.concatenate([dyn[lat_width:first], rew[lat_width:first]], axis=1)
-    grad_task = jnp.dot(task_embed.astype(F32).T, tasks, precision=lax.Precision.HIGHEST)
-
-    def first_grads(net, task):
-        return (
-            jnp.concatenate([net[:lat_width], net[first : first + n_act], task]),
-            net[first + n_act],
-            net[first + 8],
-            net[first + 9],
-        )
-
-    spare = in_rows - 32
-    grad_embed = jnp.concatenate(
-        [
-            rew[spare : spare + 32, :n_embed],
-            rew[spare : spare + 32, LANES : LANES + n_embed],
-            rew[in_rows + LANES - 16 :, :n_embed],
-        ]
+    outs = run_finish(
+        total_rows, lat_width, dyn_w1.shape[0], rew_b2.shape[0], dyn, rew, sums, task_embed
     )
-    losses = jnp.stack([sums[2, 0], sums[3, 0]]) / total_rows
-    return (
-        latents,
-        latent_grad,
-        losses,
-        grad_embed,
-        *first_grads(dyn, grad_task[:, :shard]),
-        *first_grads(rew, grad_task[:, shard:]),
-        dyn[in_rows:].T,
-        sums[0],
-        rew[in_rows : in_rows + n_bins].T,
-        sums[1, :n_bins],
-    )
+    outs = [out.reshape(-1) if out.shape[0] == 1 else out for out in outs]
+    outs[12] = outs[12].T
+    return (latents, latent_grad, *outs)
 
 
 def solution(mesh):

time: 205 us -> 154 us (0.75)
  Pallas kernels: 173 us -> 146 us
  local copies, waits for them, and re-layouts: 22.9 us -> 7.29 us
  other arithmetic: 6.93 us -> 0 us
    pallas_call x1, Pallas kernels: 173 us -> 144 us  [run_main(): pl.pallas_call(functools.partial(main_kernel, (n_mp, n_dp, total_rows, hi...]
    slice x18 -> x0, local copies, waits for them, and re-layouts: 13 us -> none  [the longest x2 1.98 us: first_layer(): w1[:lat_width]]
    concatenate x4 -> x0, other arithmetic: 3.21 us -> none  [the longest x1 1.12 us: first_grads(): jnp.concatenate([net[:lat_width], net[first:first + n_act], task])]
    unnamed x38 -> x12, local copies, waits for them, and re-layouts: 5.59 us -> 7.29 us
where the time goes in v3:
time: 154 us
  Pallas kernels  146 us (95%)
  local copies, waits for them, and re-layouts  7.29 us (5%)
    pallas_call x1, Pallas kernels, run_main(): pl.pallas_call(functools.partial(main_kernel, (n_mp, n_dp, total_rows, hi...  144 us
    unnamed x12, local copies, waits for them, and re-layouts  7.29 us

profile of v3, /device:TPU:0, one launch (start us, length us, event | category | flops | bytes accessed | tf_op | source)
XLA Modules:
  0.0 153.6 jit_solution(12101023512181618387)
XLA Ops:
  0.7 0.0 copy-start.2
  0.7 144.0 %shard_map.315 = (bf16[8192,128]{1,0:T(8,128)(2,1)}, bf16[8192,128]{1,0:T(8,128)(2,1)}, bf16[1152,256]{1,0:T(8,128)(2,1)}, bf16[768,256]{1,0:T(8,128)(2,1)}, f32[8,512]{1,0:T(8,128)}) custom-call(bf16[8192,512]{1,0:T(8,128)(2,1)} %latent_in.1, bf16[8192,128]{1,0:T(8,128)(2,1)} %next_in.1, bf16[614,256]{1,0:T(8,128)(2,1)} %dyn_w1.1, bf16[614,256]{1,0:T(8,128)(2,1)} %rew_w1.1, ...), custom_call_target="tpu_custom_call" | custom-call | tf_op jit(solution)/shard_map/pallas_call | solution.py:869
  144.7 0.0 copy-done.2
  144.7 0.0 copy-start
  144.7 1.1 copy-done
  145.8 0.0 copy-start.1
  145.8 1.0 copy-done.1
  146.8 0.0 copy-start.3
  146.8 0.7 copy-done.3
  147.5 1.6 %shard_map.316 = (f32[1,2]{1,0:T(1,128)}, f32[80,96]{1,0:T(8,128)}, f32[614,256]{1,0:T(8,128)}, f32[1,256]{1,0:T(1,128)}, f32[1,256]{1,0:T(1,128)}, /*index=5*/f...) custom-call(bf16[1152,256]{1,0:T(8,128)(2,1)S(1)} %copy-done, ...), custom_call_target="tpu_custom_call" | custom-call | tf_op jit(solution)/shard_map/pallas_call | solution.py:824
  149.1 0.0 copy-start.4
  149.1 3.2 %copy.38 = bf16[8192,128]{1,0:T(8,128)(2,1)} copy(bf16[8192,128]{1,0:T(8,128)(2,1)} %get-tuple-element.70) | data formatting | bytes 4194304
  152.3 0.0 copy-done.4
  152.3 1.3 copy.39
Async XLA Ops:
  0.7 144.0 %copy-start.2 = (bf16[80,96]{1,0:T(8,128)(2,1)S(1)}, bf16[80,96]{1,0:T(8,128)(2,1)}, u32[]{:S(2)}) copy-start(bf16[80,96]{1,0:T(8,128)(2,1)} %embed.1) | copy-start | bytes 46084
  144.7 1.1 copy-start
  145.8 1.0 copy-start.1
  146.8 0.7 copy-start.3
  149.1 3.2 %copy-start.4 = (bf16[8192,128]{1,0:T(8,128)(2,1)S(1)}, bf16[8192,128]{1,0:T(8,128)(2,1)}, u32[]{:S(2)}) copy-start(bf16[8192,128]{1,0:T(8,128)(2,1)} %get-tuple-element.71) | copy-start | bytes 6291460

commit v4 on v3

--- a/solution.py
+++ b/solution.py
@@ -15,8 +15,9 @@
 TILE = 512
 SUB = 128
 PART = 64
-FIRST = (0, 3, 5, 6, 7, 8, 9, 11)
-SECOND = (1, 6, 8, 10, 11)
+LATE = 1
+PIECES = 4
+EVENTS = ((0, 6, 10, 13, 99, 99), (0, 5, 9, 12, 15, 99), (0, 6, 9, 11, 13, 99))
 MESH = pl.DeviceIdType.MESH
 F32 = jnp.float32
 BF16 = jnp.bfloat16
@@ -34,6 +35,36 @@
 
 def aligned_to(start, size):
     return pl.ds(pl.multiple_of(start, 16), size)
+
+
+def column_groups(n_bits):
+    groups = [group for group in ((0,), (1, 2)) if group[-1] < n_bits]
+    return groups + [(bit,) for bit in range(sum(map(len, groups)), n_bits)]
+
+
+def flips(group):
+    return range(1, 1 << len(group))
+
+
+def mask_of(group, flip):
+    return sum(1 << bit for at, bit in enumerate(group) if flip >> at & 1)
+
+
+def group_masks(group):
+    return [mask_of(group, flip) for flip in flips(group)] + [1 << bit for bit in group]
+
+
+def room(n_rows, n_bits):
+    extra, length = 2 * n_rows, n_rows
+    for group in column_groups(n_bits):
+        if length % (16 << len(group)) == 0:
+            length >>= len(group)
+            extra += length * ((1 << len(group)) - 1)
+        else:
+            for _ in group:
+                length = length // 2 if length % 32 == 0 else length
+                extra += length
+    return extra
 
 
 def split_dot(left, right, left_dim, right_dim):
@@ -91,9 +122,11 @@
     d_dyn,
     part_a,
     part_b,
+    part_c,
     part_rew,
     got_a,
     got_b,
+    got_c,
     got_rew,
     sums,
     got_sums,
@@ -158,8 +191,21 @@
     def bit_of(bit):
         return (column // (1 << bit)) % 2
 
-    def column_peer(bit):
-        return column + (1 - 2 * bit_of(bit)) * (1 << bit)
+    def column_peer(mask):
+        peer = column
+        for bit in range(n_bits):
+            if mask >> bit & 1:
+                peer = peer + (1 - 2 * bit_of(bit)) * (1 << bit)
+        return peer
+
+    groups = column_groups(n_bits)
+
+    def place_in(group, flip):
+        place = 0
+        for at, bit in enumerate(group):
+            here = 1 - bit_of(bit) if flip >> at & 1 else bit_of(bit)
+            place = place + here * (1 << (len(group) - 1 - at))
+        return place
 
     def rows_of(device):
         return aligned(device * own_rows, own_rows)
@@ -178,11 +224,12 @@
         pl.semaphore_signal(
             barrier, inc=1, device_id={"mp": peer_of(flip)}, device_id_type=MESH
         )
-    for bit in range(n_bits):
+    masks = sorted({mask for group in groups for mask in group_masks(group)})
+    for mask in masks:
         pl.semaphore_signal(
-            barrier, inc=1, device_id={"dp": column_peer(bit)}, device_id_type=MESH
+            barrier, inc=1, device_id={"dp": column_peer(mask)}, device_id_type=MESH
         )
-    pl.semaphore_wait(barrier, 3 + n_bits)
+    pl.semaphore_wait(barrier, 3 + len(masks))
 
     near, across = peer_of(1), peer_of(2)
 
@@ -295,14 +342,17 @@
     def centre(values):
         return values - jnp.sum(values, axis=1, keepdims=True) * (1.0 / hid_width)
 
-    def prepare(net):
-        for index in w_needs[net]:
+    def gathered(indices):
+        for index in indices:
             weight_copy(index, 1).wait_recv()
             weight_copy(index, 2).start()
-        for index in w_needs[net]:
+        for index in indices:
             loads[4 + index].wait()
             weight_copy(index, 0).wait_recv()
             weight_copy(index, 2).wait_recv()
+
+    def prepare(net):
+        gathered(w_needs[net][:2])
         cols = pl.ds(net * hid_width, hid_width)
 
         @pl.loop(0, lat_width // PART)
@@ -407,6 +457,7 @@
                 d_lat = d_scale * error
                 d_z = s * (d_lat - jnp.sum(s * d_lat, axis=1, keepdims=True))
                 zt[part, lanes] = s.reshape(PART, LANES)
+                b2_acc[part, :] += d_z.reshape(PART, LANES)
                 target[
                     aligned(row + step * PART, PART), aligned(col + lane * LANES, LANES)
                 ] = d_z.reshape(PART, LANES).astype(BF16)
@@ -469,6 +520,11 @@
     @pl.loop(0, n_tiles)
     def _(tile):
         forward(0, aligned(tile * TILE, TILE), False)
+
+        @pl.when(tile == 0)
+        def _():
+            gathered(w_needs[0][2:])
+
         simnorm(0, tile, dpl_send, 0, tile * TILE)
         dpl_copy(tile).start()
         local, remote = lat_copies(0, tile)
@@ -488,114 +544,149 @@
         remote.start()
         dpl_copy(tile).wait_recv()
         d_lat = dpl[:, cols]
-        b2_acc[...] += dot(jnp.ones((8, TILE), BF16), d_lat, 1, 1)
         g2t[...] += dot(d_lat, hid[...])
         dh[...] = dot(d_lat, w2_t[...], 0, 0)
         backward(0, d_dyn, tile * TILE)
         g1[:, pl.ds(0, hid_width)] += dot(x_t[:, cols], d_dyn[cols, :])
 
-    def add_into(target, other, n_rows):
-        step_rows = 48 if n_rows % 48 == 0 else 16
+    def add_into(target, others, n_rows):
+        step_rows = next(size for size in (128, 96, 80, 64, 48, 32, 16) if n_rows % size == 0)
 
         @pl.loop(0, n_rows // step_rows)
         def _(step):
             rows = aligned(step * step_rows, step_rows)
-            total = target[rows, :].astype(F32) + other[rows, :].astype(F32)
+            total = target[rows, :].astype(F32)
+            for other in others:
+                total = total + other[rows, :].astype(F32)
             target[rows, :] = total.astype(BF16)
 
     def reduction(key, part, got, fin, order, with_sums):
         n_rows = part.shape[2]
         stages, gathers = [], []
-        offset, length, place, both = 0, n_rows, n_rows, True
+        offset, length, spot, both = 0, n_rows, n_rows, True
+
+        def sides(rows, where, other_side):
+            if both:
+                return part.at[half, :, rows, :], got.at[:, where, :]
+            return part.at[half, other_side, rows, :], got.at[0, where, :]
+
+        def adds(rows, wheres, count):
+            if both:
+                return [
+                    (part.at[half, k, rows, :], [got.at[k, where, :] for where in wheres], count)
+                    for k in range(2)
+                ]
+            return [(part.at[half, pair, rows, :], [got.at[0, w, :] for w in wheres], count)]
+
         for what in order:
             if what == "near":
-                stages.append((what, 0, 0, 0, n_rows, 0, True))
+                where = pl.ds(0, n_rows)
+                copies = [(part.at[1 - half], got.at[:, where, :], {"mp": near})]
+                stages.append((copies, adds(pl.ds(0, n_rows), [where], n_rows), None, half))
                 continue
             if what == "across":
                 both = False
-                stages.append((what, 0, offset, offset, length, place, False))
-            elif length % 32 == 0:
-                length //= 2
-                keep = offset + bit_of(what) * length
-                send = offset + (1 - bit_of(what)) * length
-                stages.append(("half", what, send, keep, length, place, both))
-                gathers.append(("gather", what, keep, keep, length, 0, False))
-                offset = keep
+                rows, where = aligned_to(offset, length), pl.ds(spot, length)
+                source, target = sides(rows, where, 1 - pair)
+                copies = [(source, target, {"mp": across})]
+                stages.append((copies, adds(rows, [where], length), None, pair))
+                spot += length
+                continue
+            if length % (16 << len(what)) == 0:
+                parts = [what]
             else:
-                stages.append(("whole", what, offset, offset, length, place, both))
-            place += length
+                parts = [(bit,) for bit in what]
+            for group in parts:
+                whole = length % (16 << len(group)) != 0
+                if not whole:
+                    length >>= len(group)
+                mine_at = 0 if whole else place_in(group, 0) * length
+                copies, wheres = [], []
+                for flip in flips(group):
+                    at = 0 if whole else place_in(group, flip) * length
+                    where = pl.ds(spot, length)
+                    spot += length
+                    source, target = sides(aligned_to(offset + at, length), where, pair)
+                    copies.append((source, target, {"dp": column_peer(mask_of(group, flip))}))
+                    wheres.append(where)
+                keep = aligned_to(offset + mine_at, length)
+                kind = "whole" if whole else None
+                stages.append((copies, adds(keep, wheres, length), kind, place_in(group, 0)))
+                if not whole:
+                    gathers.append((group, offset + mine_at, length))
+                offset = offset + mine_at
         last = len(stages)
-        stages += gathers[::-1]
-
-        def ends(index):
-            kind, bit, send, keep, count, spot, two = stages[index]
-            if kind == "near":
-                return part.at[1 - half], got.at[:, pl.ds(0, n_rows), :], {"mp": near}
-            rows, spots = aligned_to(send, count), pl.ds(spot, count)
-            if kind == "across":
-                return part.at[half, 1 - pair, rows, :], got.at[0, spots, :], {"mp": across}
-            device = {"dp": column_peer(bit)}
-            if kind == "gather":
-                return fin.at[rows, :], fin.at[rows, :], device
-            if two:
-                return part.at[half, :, rows, :], got.at[:, spots, :], device
-            return part.at[half, pair, rows, :], got.at[0, spots, :], device
-
-        def copy(index):
-            source, target, device = ends(index)
-            return pltpu.make_async_remote_copy(
-                src_ref=source,
-                dst_ref=target,
-                send_sem=r_send.at[key, index],
-                recv_sem=r_recv.at[key, index],
-                device_id=device,
-                device_id_type=MESH,
-            )
-
-        def sums_copy(index):
-            return pltpu.make_async_remote_copy(
-                src_ref=sums.at[index],
-                dst_ref=got_sums.at[index],
-                send_sem=s_send.at[index],
-                recv_sem=s_recv.at[index],
-                device_id=ends(index)[2],
-                device_id_type=MESH,
-            )
+        final = aligned_to(offset, length)
+        for group, start, count in gathers[::-1]:
+            rows = aligned_to(start, count)
+            copies = [
+                (fin.at[rows, :], fin.at[rows, :], {"dp": column_peer(mask_of(group, flip))})
+                for flip in flips(group)
+            ]
+            stages.append((copies, [], None, None))
+        firsts = [sum(len(stage[0]) for stage in stages[:i]) for i in range(len(stages))]
+        slots = [sum(len(stage[0]) + 1 for stage in stages[:i]) for i in range(last)]
+
+        def copies_of(index):
+            for number, (source, target, device) in enumerate(stages[index][0]):
+                at = firsts[index] + number
+                yield pltpu.make_async_remote_copy(
+                    src_ref=source,
+                    dst_ref=target,
+                    send_sem=r_send.at[key, at],
+                    recv_sem=r_recv.at[key, at],
+                    device_id=device,
+                    device_id_type=MESH,
+                )
+
+        def sums_copies(index):
+            if with_sums and index < last:
+                for number, (_, _, device) in enumerate(stages[index][0]):
+                    at = firsts[index] + number
+                    yield pltpu.make_async_remote_copy(
+                        src_ref=sums.at[index],
+                        dst_ref=got_sums.at[slots[index] + stages[index][3]],
+                        send_sem=s_send.at[at],
+                        recv_sem=s_recv.at[at],
+                        device_id=device,
+                        device_id_type=MESH,
+                    )
 
         def start(index):
-            copy(index).start()
+            for copy in copies_of(index):
+                copy.start()
+            for copy in sums_copies(index):
+                copy.start()
+
+        def finish(index):
+            for copy in copies_of(index):
+                if stages[index][2] == "whole":
+                    copy.wait_send()
+                copy.wait_recv()
+            for copy in sums_copies(index):
+                copy.wait_recv()
             if with_sums and index < last:
-                sums_copy(index).start()
-
-        def finish(index):
-            kind, bit, send, keep, count, spot, two = stages[index]
-            if kind == "whole":
-                copy(index).wait_send()
-            copy(index).wait_recv()
-            if with_sums and index < last:
-                sums_copy(index).wait_recv()
-                sums[index + 1] = sums[index] + got_sums[index]
-            if kind != "gather":
-                rows, spots = aligned_to(keep, count), pl.ds(spot, count)
-                for side in range(2):
-                    if two:
-                        add_into(part.at[half, side, rows, :], got.at[side, spots, :], count)
-                    elif side == 0:
-                        add_into(part.at[half, pair, rows, :], got.at[0, spots, :], count)
+                got_sums[slots[index] + stages[index][3]] = sums[index]
+                total = got_sums[slots[index]]
+                for other in range(len(stages[index][0])):
+                    total = total + got_sums[slots[index] + 1 + other]
+                sums[index + 1] = total
+            for target, others, count in stages[index][1]:
+                add_into(target, others, count)
             if index + 1 == last:
-                rows = aligned_to(offset, length)
-                fin[rows, :] = part[half, pair, rows, :]
+                fin[final, :] = part[half, pair, final, :]
             if index + 1 < len(stages):
                 start(index + 1)
 
         def drain():
             for index, stage in enumerate(stages):
-                if stage[0] != "whole":
-                    copy(index).wait_send()
-                if with_sums and index < last:
-                    sums_copy(index).wait_send()
-
-        return start, finish, drain, len(stages)
+                if stage[2] != "whole":
+                    for copy in copies_of(index):
+                        copy.wait_send()
+                for copy in sums_copies(index):
+                    copy.wait_send()
+
+        return start, finish, drain, len(stages), last
 
     def fill(part, net, first, count, source, base):
         for device in range(n_mp):
@@ -611,37 +702,69 @@
                 col_acc[pl.ds(8 * line, 8), cols], axis=0, keepdims=True
             )
 
-    bits = list(range(n_bits))
+    def order_of(kind):
+        if kind == 0:
+            return ["near", "across"] + groups
+        if kind == 1 or len(groups) < 2:
+            return ["near"] + groups[:1] + ["across"] + groups[1:]
+        return ["near", groups[1], "across", groups[0]] + groups[2:]
+
+    split = part_b.shape[2]
     add_columns(0)
     fill(part_a, 0, 0, lat_width, g2t, 0)
-    fill(part_b, 0, 0, in_rows, g1, 0)
+    fill(part_b, 0, 0, split, g1, 0)
+    fill(part_c, 0, 0, in_rows - split, g1, split)
+    dyn_places = (
+        (part_a, got_a, in_rows, lat_width),
+        (part_b, got_b, 0, split),
+        (part_c, got_c, split, in_rows - split),
+    )
     chunks = [
-        reduction(0, part_a, got_a, fin_dyn.at[pl.ds(in_rows, lat_width), :], ["near"] + bits + ["across"], False),
-        reduction(1, part_b, got_b, fin_dyn.at[pl.ds(0, in_rows), :], ["near"] + bits + ["across"], False),
+        reduction(k, part, got, fin_dyn.at[pl.ds(first, count), :], order_of(k), False)
+        for k, (part, got, first, count) in enumerate(dyn_places)
     ]
     for chunk in chunks:
         chunk[0](0)
-    n_stages = 2 + 2 * n_bits
-    per_tile = 3
-    events = [
-        (chunk, index, (FIRST, SECOND)[chunk][index])
-        for index in range(n_stages)
-        for chunk in range(2)
-        if index < min(chunks[chunk][3], len((FIRST, SECOND)[chunk]))
-    ]
-    inside = [event for event in events if event[2] < per_tile * n_tiles]
-    inside.sort(key=lambda event: event[2])
-    done = [(event[0], event[1]) for event in inside]
+    per_tile = 4
+    inside = sorted(
+        (place, chunk, index)
+        for chunk, places in enumerate(EVENTS)
+        for index, place in enumerate(places)
+        if index < chunks[chunk][3] and place < per_tile * n_tiles
+    )
 
     prepare(1)
+    gathered(w_needs[1][2:])
+
+    for place, chunk, index in inside:
+        if place < 0:
+            chunks[chunk][1](index)
 
     def point(tile, number):
-        for chunk, index, place in inside:
-            if place % per_tile == number:
+        for place, chunk, index in inside:
+            if place >= 0 and place % per_tile == number:
 
                 @pl.when(tile == place // per_tile)
                 def _():
                     chunks[chunk][1](index)
+
+    def kept(tile):
+        return aligned(jnp.maximum(tile - (n_tiles - LATE - 1), 0) * TILE, TILE)
+
+    def latent_grads(tile):
+        cols = aligned(tile * TILE, TILE)
+        lat_rows = pl.ds(0, lat_width)
+        lg = dot(d_dyn[cols, :], w1_raw[lat_rows, pl.ds(0, hid_width)], 1, 1)
+        lg = lg + dot(d_pre[kept(tile), :], w1_raw[lat_rows, pl.ds(hid_width, hid_width)], 1, 1)
+        lg = (lg * total_rows).astype(BF16)
+        for device in range(n_mp):
+            lg_stage[device, cols, :] = lg[:, device * share : (device + 1) * share]
+
+    def send_grads(tile):
+        local, remotes = grad_copies(tile)
+        local.start()
+        for remote in remotes:
+            remote.start()
 
     @pl.loop(0, n_tiles)
     def _(tile):
@@ -665,68 +788,85 @@
         sum_acc[pl.ds(8, 8), :] += dot(jnp.ones((8, TILE), BF16), dlog[...], 1, 1)
         rg2t[...] += dot(dlog[...], hid[...])
         dh[...] = dot(dlog[...], rw2_t[...], 0, 0)
-        backward(1, d_pre, 0)
         point(tile, 1)
-        lat_rows = pl.ds(0, lat_width)
-        lg = dot(d_dyn[cols, :], w1_raw[lat_rows, pl.ds(0, hid_width)], 1, 1)
-        lg = lg + dot(d_pre[...], w1_raw[lat_rows, pl.ds(hid_width, hid_width)], 1, 1)
-        lg = (lg * total_rows).astype(BF16)
+        backward(1, d_pre, jnp.maximum(tile - (n_tiles - LATE - 1), 0) * TILE)
+        point(tile, 2)
+        g1[:, pl.ds(hid_width, hid_width)] += dot(x_t[:, cols], d_pre[kept(tile), :])
+
+        if LATE < n_tiles:
+
+            @pl.when(tile < n_tiles - LATE)
+            def _():
+                latent_grads(tile)
+
+        point(tile, 3)
+
+        if LATE < n_tiles:
+
+            @pl.when(tile < n_tiles - LATE)
+            def _():
+                send_grads(tile)
+
+
+    add_columns(1)
+    third = part_rew.shape[3]
+    for k in range(3):
+        rest = min(third, in_rows - k * third)
         for device in range(n_mp):
-            lg_stage[device, cols, :] = lg[:, device * share : (device + 1) * share]
-        local, remotes = grad_copies(tile)
-        local.start()
-        for remote in remotes:
-            remote.start()
-        g1[:, pl.ds(hid_width, hid_width)] += dot(x_t[:, cols], d_pre[...])
-        point(tile, 2)
-
-    add_columns(1)
-    fill_rows = part_rew.shape[3]
-    for device in range(n_mp):
-        cols = pl.ds(hid_width + device * shard, shard)
-        block = pl.ds(device * shard, shard)
-        where = (device % 2, device // 2)
-        part_rew[(0,) + where] = g1[pl.ds(0, fill_rows), cols].astype(BF16)
-        part_rew[(1,) + where + (pl.ds(0, in_rows - fill_rows),)] = g1[
-            pl.ds(fill_rows, in_rows - fill_rows), cols
-        ].astype(BF16)
-        part_rew[(1,) + where + (pl.ds(in_rows - fill_rows, LANES),)] = rg2t[:, block].astype(BF16)
+            cols = pl.ds(hid_width + device * shard, shard)
+            where = (k, device % 2, device // 2)
+            part_rew[where + (pl.ds(0, rest),)] = g1[pl.ds(k * third, rest), cols].astype(BF16)
+            if rest < third:
+                block = pl.ds(device * shard, shard)
+                part_rew[where + (pl.ds(rest, LANES),)] = rg2t[:, block].astype(BF16)
     tasks = g1[pl.ds(lat_width, n_task), :]
     table = split_dot(tasks, w1_raw[pl.ds(lat_width, n_rest), :], 1, 1).astype(BF16)
-    spare = in_rows - fill_rows - 32
+    spare = in_rows - 2 * third - 32
     for device in range(n_mp):
-        where = (1, device % 2, device // 2)
+        where = (2, device % 2, device // 2)
         part_rew[where + (pl.ds(spare, 32), pl.ds(0, n_rest))] = table[0:32]
         part_rew[where + (pl.ds(spare, 32), pl.ds(LANES, n_rest))] = table[32:64]
-        part_rew[where + (pl.ds(fill_rows - 16, 16), pl.ds(0, n_rest))] = table[64:80]
+        part_rew[where + (pl.ds(third - 16, 16), pl.ds(0, n_rest))] = table[64:80]
     sums[0] = jnp.zeros(sums.shape[1:], F32)
-    sums[0, pl.ds(0, 1), :] = b2_acc[pl.ds(0, 1), :]
+    sums[0, pl.ds(0, 1), aligned(pair * chip_cols, chip_cols)] = jnp.sum(
+        b2_acc[...].T, axis=0, keepdims=True
+    )
     sums[0, pl.ds(1, 1), pl.ds(0, LANES)] = sum_acc[pl.ds(8, 1), :]
     cons = jnp.sum(sum_acc[pl.ds(0, 8), :])
     rew = jnp.sum(row_acc[...])
     sums[0, pl.ds(2, 1), :] = jnp.full((1, lat_width), cons)
     sums[0, pl.ds(3, 1), :] = jnp.full((1, lat_width), rew)
-    orders = (["near", "across"] + bits, ["near"] + bits[:1] + ["across"] + bits[1:])
-    for k in range(2):
+    for k in range(3):
         chunks.append(
             reduction(
-                2 + k,
+                3 + k,
                 part_rew.at[k],
                 got_rew.at[k],
-                fin_rew.at[pl.ds(k * fill_rows, fill_rows), :],
-                orders[k],
+                fin_rew.at[pl.ds(k * third, third), :],
+                order_of(k),
                 k == 0,
             )
         )
-    chunks[2][0](0)
-    chunks[3][0](0)
-    left = [(c, index) for index in range(n_stages) for c in range(2) if (c, index) not in done]
-    left += [(c, index) for index in range(n_stages) for c in (2, 3)]
-    left.sort(key=lambda event: event[1] if event[0] > 1 else event[1] - len(done) // 2)
-    for chunk, index in left:
-        if index < chunks[chunk][3]:
-            chunks[chunk][1](index)
-    fin_sums[...] = sums[2 + n_bits]
+    for chunk in chunks[3:]:
+        chunk[0](0)
+    done = [(chunk, index) for _, chunk, index in inside]
+    left = [(index, c) for c in range(3) for index in range(chunks[c][3]) if (c, index) not in done]
+    base = min([index for index, _ in left], default=0)
+    left = [(index - base, c, index) for index, c in left]
+    left += [(index, c, index) for c in range(3, 6) for index in range(chunks[c][3])]
+    late = [n_tiles - LATE + k for k in range(LATE)]
+    for tile in late[:1]:
+        latent_grads(tile)
+    step = 0
+    for when, chunk, index in sorted(left):
+        if when > step:
+            step = when
+            for tile in late[step - 1 : step]:
+                send_grads(tile)
+            for tile in late[step : step + 1]:
+                latent_grads(tile)
+        chunks[chunk][1](index)
+    fin_sums[...] = sums[chunks[3][4]]
     for chunk in chunks:
         chunk[2]()
 
@@ -752,10 +892,14 @@
 
 
 def finish_kernel(
-    dyn,
-    rew,
-    sums,
+    lat_in,
+    grad_in,
+    dyn_in,
+    rew_in,
+    sums_in,
     embed,
+    lat_out,
+    grad_out,
     losses,
     grad_embed,
     dyn_w1,
@@ -770,10 +914,37 @@
     dyn_b2,
     rew_w2,
     rew_b2,
+    dyn,
+    rew,
+    sums,
+    stage,
+    sems,
     *,
     total_rows,
     lat_width,
 ):
+    n_big = stage.shape[1]
+    copies = [
+        pltpu.make_async_copy(source, target, sems.at[i])
+        for i, (source, target) in enumerate(((dyn_in, dyn), (rew_in, rew), (sums_in, sums)))
+    ]
+    rows = stage.shape[2]
+    outs = []
+    for k in range(n_big):
+        part = pl.ds(k * rows, rows)
+        for side, (source, target) in enumerate(((lat_in, lat_out), (grad_in, grad_out))):
+            first, last = sems.at[3 + 4 * k + 2 * side], sems.at[4 + 4 * k + 2 * side]
+            copies.append(
+                pltpu.make_async_copy(source.at[part, :], stage.at[side, k], first)
+            )
+            outs.append(pltpu.make_async_copy(stage.at[side, k], target.at[part, :], last))
+    for copy in copies:
+        copy.start()
+    for copy, out in zip(copies[3:], outs):
+        copy.wait()
+        out.start()
+    for copy in copies[:3]:
+        copy.wait()
     n_task, n_embed = embed.shape
     n_rest = dyn_w1.shape[0] - lat_width
     n_act = n_rest - n_embed
@@ -814,16 +985,22 @@
     pick = lax.broadcasted_iota(jnp.int32, losses.shape, 1) == 0
     both = jnp.where(pick, sums[pl.ds(2, 1), pl.ds(0, 2)], sums[pl.ds(3, 1), pl.ds(0, 2)])
     losses[...] = both * (1.0 / total_rows)
-
-
-def run_finish(total_rows, lat_width, n_in, n_bins, dyn, rew, sums, embed):
+    for out in outs:
+        out.wait()
+
+
+def run_finish(total_rows, lat_width, n_in, n_bins, lat, grad, dyn, rew, sums, embed):
     shape = jax.ShapeDtypeStruct
     shard = dyn.shape[1]
     line = shape((1, shard), F32)
     first = [shape((n_in, shard), F32), line, line, line]
+    any_spec = pl.BlockSpec(memory_space=pl.ANY)
+    vmem_spec = pl.BlockSpec(memory_space=pltpu.VMEM)
     return pl.pallas_call(
         functools.partial(finish_kernel, total_rows=total_rows, lat_width=lat_width),
         out_shape=(
+            shape(lat.shape, BF16),
+            shape(grad.shape, BF16),
             shape((1, 2), F32),
             shape(embed.shape, F32),
             *first,
@@ -833,8 +1010,17 @@
             shape((n_bins, shard), F32),
             shape((1, n_bins), F32),
         ),
-        compiler_params=pltpu.CompilerParams(vmem_limit_bytes=32 << 20),
-    )(dyn, rew, sums, embed)
+        in_specs=[any_spec] * 5 + [vmem_spec],
+        out_specs=[any_spec] * 2 + [vmem_spec] * 14,
+        scratch_shapes=[
+            pltpu.VMEM(dyn.shape, BF16),
+            pltpu.VMEM(rew.shape, BF16),
+            pltpu.VMEM(sums.shape, F32),
+            pltpu.VMEM((2, PIECES, lat.shape[0] // PIECES, lat.shape[1]), BF16),
+            pltpu.SemaphoreType.DMA((3 + 4 * PIECES,)),
+        ],
+        compiler_params=pltpu.CompilerParams(vmem_limit_bytes=60 << 20),
+    )(lat, grad, dyn, rew, sums, embed)
 
 
 def run_main(n_mp, n_dp, total_rows, args):
@@ -852,27 +1038,16 @@
     shape = jax.ShapeDtypeStruct
     dma = pltpu.SemaphoreType.DMA
     n_bits = n_dp.bit_length() - 1
-    n_stages = 2 + 2 * n_bits
-    rew_rows = (in_rows + LANES) // 2
-
-    def room(rows):
-        extra, length = 0, rows
-        for _ in range(n_bits):
-            length = length // 2 if length % 32 == 0 else length
-            extra += length
-        return 2 * rows + extra
-
-    any_spec = pl.BlockSpec(memory_space=pl.ANY)
-    vmem_spec = pl.BlockSpec(memory_space=pltpu.VMEM)
-    shape = jax.ShapeDtypeStruct
-    dma = pltpu.SemaphoreType.DMA
+    n_copies = 2 + 2 * sum(len(flips(group)) for group in column_groups(n_bits))
+    third = (in_rows + LANES) // 3
+    split = 3 * in_rows // 5
     return pl.pallas_call(
         functools.partial(main_kernel, (n_mp, n_dp, total_rows, hid_width)),
         out_shape=(
             shape((tok_rows, share), BF16),
             shape((tok_rows, share), BF16),
             shape((in_rows + lat_width, shard), BF16),
-            shape((2 * rew_rows, shard), BF16),
+            shape((3 * third, shard), BF16),
             shape((8, lat_width), F32),
         ),
         in_specs=[any_spec] * 4 + [vmem_spec] * 16,
@@ -899,13 +1074,15 @@
             pltpu.VMEM((n_mp, own, share), BF16),
             pltpu.VMEM((own, hid_width), BF16),
             pltpu.VMEM((2, 2, lat_width, shard), BF16),
-            pltpu.VMEM((2, 2, in_rows, shard), BF16),
-            pltpu.VMEM((2, 2, 2, rew_rows, shard), BF16),
-            pltpu.VMEM((2, room(lat_width), shard), BF16),
-            pltpu.VMEM((2, room(in_rows), shard), BF16),
-            pltpu.VMEM((2, 2, room(rew_rows), shard), BF16),
+            pltpu.VMEM((2, 2, split, shard), BF16),
+            pltpu.VMEM((2, 2, in_rows - split, shard), BF16),
+            pltpu.VMEM((3, 2, 2, third, shard), BF16),
+            pltpu.VMEM((2, room(lat_width, n_bits), shard), BF16),
+            pltpu.VMEM((2, room(split, n_bits), shard), BF16),
+            pltpu.VMEM((2, room(in_rows - split, n_bits), shard), BF16),
+            pltpu.VMEM((3, 2, room(third, n_bits), shard), BF16),
             pltpu.VMEM((3 + n_bits, 8, lat_width), F32),
-            pltpu.VMEM((2 + n_bits, 8, lat_width), F32),
+            pltpu.VMEM((4 + 2 * n_bits, 8, lat_width), F32),
             pltpu.VMEM((in_rows, 2 * hid_width), F32),
             pltpu.VMEM((lat_width, hid_width), F32),
             pltpu.VMEM((LANES, hid_width), F32),
@@ -913,7 +1090,7 @@
             pltpu.VMEM((TILE, hid_width), F32),
             pltpu.VMEM((TILE, hid_width), F32),
             pltpu.VMEM((TILE, hid_width), BF16),
-            pltpu.VMEM((TILE, hid_width), BF16),
+            pltpu.VMEM(((LATE + 1) * TILE, hid_width), BF16),
             pltpu.VMEM((2 * share, TILE), F32),
             pltpu.VMEM((2 * share, TILE), F32),
             pltpu.VMEM((LANES, TILE), BF16),
@@ -921,7 +1098,7 @@
             pltpu.VMEM((16, 2 * hid_width), F32),
             pltpu.VMEM((16, LANES), F32),
             pltpu.VMEM((1, TILE), F32),
-            pltpu.VMEM((8, lat_width), F32),
+            pltpu.VMEM((2 * share, LANES), F32),
             dma((10,)),
             dma((3, 6)),
             dma((3, 6)),
@@ -935,10 +1112,10 @@
             dma((n_tiles,)),
             dma((3, n_tiles)),
             dma((3, n_tiles)),
-            dma((4, n_stages)),
-            dma((4, n_stages)),
-            dma((2 + n_bits,)),
-            dma((2 + n_bits,)),
+            dma((6, n_copies)),
+            dma((6, n_copies)),
+            dma((n_copies,)),
+            dma((n_copies,)),
         ],
         compiler_params=pltpu.CompilerParams(
             collective_id=0, has_side_effects=True, vmem_limit_bytes=60 << 20
@@ -993,12 +1170,14 @@
         row(rew_b2),
     )
     latents, latent_grad, dyn, rew, sums = run_main(n_mp, n_dp, total_rows, args)
+    n_bins = rew_b2.shape[0]
+    n_in = dyn_w1.shape[0]
     outs = run_finish(
-        total_rows, lat_width, dyn_w1.shape[0], rew_b2.shape[0], dyn, rew, sums, task_embed
+        total_rows, lat_width, n_in, n_bins, latents, latent_grad, dyn, rew, sums, task_embed
     )
     outs = [out.reshape(-1) if out.shape[0] == 1 else out for out in outs]
-    outs[12] = outs[12].T
-    return (latents, latent_grad, *outs)
+    outs[14] = outs[14].T
+    return tuple(outs)
 
 
 def solution(mesh):

time: 154 us -> 135 us (0.88)
  Pallas kernels: 146 us -> 134 us
  local copies, waits for them, and re-layouts: 7.29 us -> 0 us
    pallas_call x1, Pallas kernels: 144 us -> 128 us  [run_main(): pl.pallas_call(functools.partial(main_kernel, (n_mp, n_dp, total_rows, hi...]
    unnamed x12 -> x0, local copies, waits for them, and re-layouts: 7.29 us -> none
    pallas_call x1, Pallas kernels: 1.6 us -> 5.94 us  [run_finish(): pl.pallas_call(functools.partial(finish_kernel, total_rows=total_rows, la...]
where the time goes in v4:
time: 135 us
  Pallas kernels  134 us (99%)
    pallas_call x1, Pallas kernels, run_main(): pl.pallas_call(functools.partial(main_kernel, (n_mp, n_dp, total_rows, hi...  128 us
    pallas_call x1, Pallas kernels, run_finish(): pl.pallas_call(functools.partial(finish_kernel, total_rows=total_rows, la...  5.94 us

profile of v4, /device:TPU:0, one launch (start us, length us, event | category | flops | bytes accessed | tf_op | source)
XLA Modules:
  0.0 134.7 jit_solution(11661521193486757740)
XLA Ops:
  0.7 127.9 %shard_map.315 = (bf16[8192,128]{1,0:T(8,128)(2,1)}, bf16[8192,128]{1,0:T(8,128)(2,1)}, bf16[1152,256]{1,0:T(8,128)(2,1)}, bf16[768,256]{1,0:T(8,128)(2,1)}, f32[8,512]{1,0:T(8,128)}) custom-call(bf16[8192,512]{1,0:T(8,128)(2,1)} %latent_in.1, bf16[8192,128]{1,0:T(8,128)(2,1)} %next_in.1, bf16[614,256]{1,0:T(8,128)(2,1)} %dyn_w1.1, bf16[614,256]{1,0:T(8,128)(2,1)} %rew_w1.1, ...), custom_call_target="tpu_custom_call" | custom-call | tf_op jit(solution)/shard_map/pallas_call | solution.py:1044
  128.6 5.9 %shard_map.316 = (bf16[8192,128]{1,0:T(8,128)(2,1)}, bf16[8192,128]{1,0:T(8,128)(2,1)}, f32[1,2]{1,0:T(1,128)}, f32[80,96]{1,0:T(8,128)}, f32[614,256]{1,0:T(8,1...) custom-call(bf16[8192,128]{1,0:T(8,128)(2,1)} %get-tuple-element.37., ...), custom_call_target="tpu_custom_call" | custom-call | tf_op jit(solution)/shard_map/pallas_call | solution.py:999

commit v5 on v4

--- a/solution.py
+++ b/solution.py
@@ -16,8 +16,8 @@
 SUB = 128
 PART = 64
 LATE = 1
-PIECES = 4
-EVENTS = ((0, 6, 10, 13, 99, 99), (0, 5, 9, 12, 15, 99), (0, 6, 9, 11, 13, 99))
+PIECES = 2
+EVENTS = ((-1, 6, 10, 13, 99, 99), (0, 5, 9, 12, 15, 99), (0, 4, 9, 11, 13, 99))
 MESH = pl.DeviceIdType.MESH
 F32 = jnp.float32
 BF16 = jnp.bfloat16
@@ -106,6 +106,8 @@
     w1_c,
     w2_t,
     rw2_t,
+    w2_g,
+    rw2_g,
     vecs,
     w2_own,
     rw2_own,
@@ -210,15 +212,6 @@
     def rows_of(device):
         return aligned(device * own_rows, own_rows)
 
-    vecs_own[...] = jnp.zeros_like(vecs_own)
-    for net, rows in enumerate(((dyn_b1, dyn_gain, dyn_shift), (rew_b1, rew_gain, rew_shift))):
-        for line, ref in enumerate(rows):
-            vecs_own[net, pl.ds(line, 1), :] = ref[...]
-    w2_own[...] = dyn_w2[...].T
-    n_bins = rew_w2.shape[0]
-    rw2_own[...] = jnp.zeros_like(rw2_own)
-    rw2_own[pl.ds(0, n_bins), :] = rew_w2[...]
-
     barrier = pltpu.get_barrier_semaphore()
     for flip in (1, 2, 3):
         pl.semaphore_signal(
@@ -229,28 +222,38 @@
         pl.semaphore_signal(
             barrier, inc=1, device_id={"dp": column_peer(mask)}, device_id_type=MESH
         )
-    pl.semaphore_wait(barrier, 3 + len(masks))
+
+    vecs_own[...] = jnp.zeros_like(vecs_own)
+    for net, rows in enumerate(((dyn_b1, dyn_gain, dyn_shift), (rew_b1, rew_gain, rew_shift))):
+        for line, ref in enumerate(rows):
+            vecs_own[net, pl.ds(line, 1), :] = ref[...]
+    w2_own[...] = dyn_w2[...].T
+    n_bins = rew_w2.shape[0]
+    rw2_own[...] = jnp.zeros_like(rw2_own)
+    rw2_own[pl.ds(0, n_bins), :] = rew_w2[...]
 
     near, across = peer_of(1), peer_of(2)
 
-    def w_pairs(block):
+    def w_pairs(block, rows_first):
         pairs = []
         for net in range(2):
             cols = aligned(net * hid_width + block * shard, shard)
             pairs.append(((dyn_w1, rew_w1)[net], w1_raw.at[:, cols]))
             pairs.append((vecs_own.at[net], vecs.at[:, cols]))
         cols = aligned(block * shard, shard)
-        pairs.append((w2_own, w2_t.at[:, cols]))
+        for side in (rows_first, 1 - rows_first):
+            rows = aligned(side * chip_cols, chip_cols)
+            pairs.append((w2_own.at[rows, :], w2_t.at[rows, cols]))
         pairs.append((rw2_own, rw2_t.at[:, cols]))
         return pairs
 
-    w_needs = ((1, 0, 4), (3, 2, 5))
-    own_weights = w_pairs(mine)
+    w_needs = ((1, 0, 4, 5), (3, 2, 6))
+    n_weights = 7
 
     def weight_copy(index, kind):
-        source, target = own_weights[index]
+        source, target = w_pairs(mine, 1 - pair if kind == 1 else pair)[index]
         if kind == 2:
-            source = target = w_pairs(across)[index][1]
+            source = target = w_pairs(across, pair)[index][1]
         return pltpu.make_async_remote_copy(
             src_ref=source,
             dst_ref=target,
@@ -281,13 +284,14 @@
         )
     for slot, device in ((0, across), (1, mine)):
         loads.append((next_in.at[rows_of(device), :], next_lat.at[slot, half]))
-    loads += own_weights
+    loads += w_pairs(mine, pair)
     loads = [
         pltpu.make_async_copy(source, target, load_sem.at[i])
         for i, (source, target) in enumerate(loads)
     ]
     for copy in loads:
         copy.start()
+    pl.semaphore_wait(barrier, 3 + len(masks))
     for index in w_needs[0] + w_needs[1]:
         weight_copy(index, 1).start()
         weight_copy(index, 0).start()
@@ -351,6 +355,14 @@
             weight_copy(index, 0).wait_recv()
             weight_copy(index, 2).wait_recv()
 
+    def with_gain(weights, scaled, net):
+        gain = vecs[pl.ds(1, 1), pl.ds(net * hid_width, hid_width)]
+
+        @pl.loop(0, weights.shape[0] // PART)
+        def _(step):
+            rows = aligned(step * PART, PART)
+            scaled[rows, :] = (weights[rows, :].astype(F32) * gain).astype(BF16)
+
     def prepare(net):
         gathered(w_needs[net][:2])
         cols = pl.ds(net * hid_width, hid_width)
@@ -390,14 +402,16 @@
                 wide = pl.ds(net * hid_width + lane * LANES, LANES)
                 xhat = pre[part, lanes] * inv
                 y = xhat * vecs[pl.ds(1, 1), wide] + vecs[pl.ds(2, 1), wide]
+                if keep:
+                    pre[part, lanes] = xhat
+                y = y.astype(BF16)
                 e = jnp.exp(jnp.minimum(y, 20.0))
                 e2 = e + 2.0
                 r = 1.0 / (e * e2 + 2.0)
                 u = e * r
                 t = u * e2
-                hid[part, lanes] = (y * t).astype(BF16)
+                hid[part, lanes] = y * t
                 if keep:
-                    pre[part, lanes] = xhat
                     dm[part, lanes] = t + (4.0 * y) * (u * (r + u))
 
     def backward(net, target, first_row):
@@ -409,17 +423,14 @@
             for lane in range(n_lane):
                 lanes = pl.ds(lane * LANES, LANES)
                 wide = pl.ds(net * hid_width + lane * LANES, LANES)
-                d_y = dh[part, lanes] * dm[part, lanes]
-                xhat = pre[part, lanes]
-                scaled = d_y * xhat
+                g = dh[part, lanes] * dm[part, lanes].astype(F32)
+                scaled = g * pre[part, lanes]
                 col_acc[pl.ds(0, 8), wide] += jnp.sum(
                     scaled.reshape(SUB // 8, 8, LANES), axis=0
                 )
-                col_acc[pl.ds(8, 8), wide] += jnp.sum(d_y.reshape(SUB // 8, 8, LANES), axis=0)
-                gain = vecs[pl.ds(1, 1), wide]
-                g = d_y * gain
+                col_acc[pl.ds(8, 8), wide] += jnp.sum(g.reshape(SUB // 8, 8, LANES), axis=0)
                 first += g
-                second += scaled * gain
+                second += scaled
                 dh[part, lanes] = g
             inv = inv_ref[part, :]
             first = jnp.broadcast_to(
@@ -523,7 +534,7 @@
 
         @pl.when(tile == 0)
         def _():
-            gathered(w_needs[0][2:])
+            gathered(w_needs[0][2:3])
 
         simnorm(0, tile, dpl_send, 0, tile * TILE)
         dpl_copy(tile).start()
@@ -531,6 +542,8 @@
         local.start()
         remote.start()
 
+    gathered(w_needs[0][3:])
+    with_gain(w2_t, w2_g, 0)
     loads[3].wait()
     next_copy(1).wait_recv()
 
@@ -545,7 +558,7 @@
         dpl_copy(tile).wait_recv()
         d_lat = dpl[:, cols]
         g2t[...] += dot(d_lat, hid[...])
-        dh[...] = dot(d_lat, w2_t[...], 0, 0)
+        dh[...] = dot(d_lat, w2_g[...], 0, 0)
         backward(0, d_dyn, tile * TILE)
         g1[:, pl.ds(0, hid_width)] += dot(x_t[:, cols], d_dyn[cols, :])
 
@@ -698,9 +711,8 @@
     def add_columns(net):
         cols = pl.ds(net * hid_width, hid_width)
         for line in range(2):
-            g1[pl.ds(lat_width + n_task + 8 + line, 1), cols] = jnp.sum(
-                col_acc[pl.ds(8 * line, 8), cols], axis=0, keepdims=True
-            )
+            total = jnp.sum(col_acc[pl.ds(8 * line, 8), cols], axis=0, keepdims=True)
+            g1[pl.ds(lat_width + n_task + 8 + line, 1), cols] = total / vecs[pl.ds(1, 1), cols]
 
     def order_of(kind):
         if kind == 0:
@@ -735,6 +747,7 @@
 
     prepare(1)
     gathered(w_needs[1][2:])
+    with_gain(rw2_t, rw2_g, 1)
 
     for place, chunk, index in inside:
         if place < 0:
@@ -787,7 +800,7 @@
         dlog[...] = d_logits.astype(BF16)
         sum_acc[pl.ds(8, 8), :] += dot(jnp.ones((8, TILE), BF16), dlog[...], 1, 1)
         rg2t[...] += dot(dlog[...], hid[...])
-        dh[...] = dot(dlog[...], rw2_t[...], 0, 0)
+        dh[...] = dot(dlog[...], rw2_g[...], 0, 0)
         point(tile, 1)
         backward(1, d_pre, jnp.maximum(tile - (n_tiles - LATE - 1), 0) * TILE)
         point(tile, 2)
@@ -810,6 +823,18 @@
 
     add_columns(1)
     third = part_rew.shape[3]
+    spare = in_rows - 2 * third - 32
+    for k in range(3):
+        chunks.append(
+            reduction(
+                3 + k,
+                part_rew.at[k],
+                got_rew.at[k],
+                fin_rew.at[pl.ds(k * third, third), :],
+                order_of(k),
+                k == 2,
+            )
+        )
     for k in range(3):
         rest = min(third, in_rows - k * third)
         for device in range(n_mp):
@@ -819,9 +844,10 @@
             if rest < third:
                 block = pl.ds(device * shard, shard)
                 part_rew[where + (pl.ds(rest, LANES),)] = rg2t[:, block].astype(BF16)
+        if k < 2:
+            chunks[3 + k][0](0)
     tasks = g1[pl.ds(lat_width, n_task), :]
     table = split_dot(tasks, w1_raw[pl.ds(lat_width, n_rest), :], 1, 1).astype(BF16)
-    spare = in_rows - 2 * third - 32
     for device in range(n_mp):
         where = (2, device % 2, device // 2)
         part_rew[where + (pl.ds(spare, 32), pl.ds(0, n_rest))] = table[0:32]
@@ -836,19 +862,7 @@
     rew = jnp.sum(row_acc[...])
     sums[0, pl.ds(2, 1), :] = jnp.full((1, lat_width), cons)
     sums[0, pl.ds(3, 1), :] = jnp.full((1, lat_width), rew)
-    for k in range(3):
-        chunks.append(
-            reduction(
-                3 + k,
-                part_rew.at[k],
-                got_rew.at[k],
-                fin_rew.at[pl.ds(k * third, third), :],
-                order_of(k),
-                k == 0,
-            )
-        )
-    for chunk in chunks[3:]:
-        chunk[0](0)
+    chunks[5][0](0)
     done = [(chunk, index) for _, chunk, index in inside]
     left = [(index, c) for c in range(3) for index in range(chunks[c][3]) if (c, index) not in done]
     base = min([index for index, _ in left], default=0)
@@ -866,11 +880,11 @@
             for tile in late[step : step + 1]:
                 latent_grads(tile)
         chunks[chunk][1](index)
-    fin_sums[...] = sums[chunks[3][4]]
+    fin_sums[...] = sums[chunks[5][4]]
     for chunk in chunks:
         chunk[2]()
 
-    for index in range(6):
+    for index in range(n_weights):
         for kind in range(3):
             weight_copy(index, kind).wait_send()
     for slot in range(2):
@@ -1059,6 +1073,8 @@
             pltpu.VMEM((in_rows, 2 * hid_width), BF16),
             pltpu.VMEM((lat_width, hid_width), BF16),
             pltpu.VMEM((LANES, hid_width), BF16),
+            pltpu.VMEM((lat_width, hid_width), BF16),
+            pltpu.VMEM((LANES, hid_width), BF16),
             pltpu.VMEM((8, 2 * hid_width), F32),
             pltpu.VMEM((lat_width, shard), BF16),
             pltpu.VMEM((LANES, shard), BF16),
@@ -1088,7 +1104,7 @@
             pltpu.VMEM((LANES, hid_width), F32),
             pltpu.VMEM((TILE, hid_width), F32),
             pltpu.VMEM((TILE, hid_width), F32),
-            pltpu.VMEM((TILE, hid_width), F32),
+            pltpu.VMEM((TILE, hid_width), BF16),
             pltpu.VMEM((TILE, hid_width), BF16),
             pltpu.VMEM(((LATE + 1) * TILE, hid_width), BF16),
             pltpu.VMEM((2 * share, TILE), F32),
@@ -1099,9 +1115,9 @@
             pltpu.VMEM((16, LANES), F32),
             pltpu.VMEM((1, TILE), F32),
             pltpu.VMEM((2 * share, LANES), F32),
-            dma((10,)),
-            dma((3, 6)),
-            dma((3, 6)),
+            dma((11,)),
+            dma((3, 7)),
+            dma((3, 7)),
             dma((2,)),
             dma((2,)),
             dma((n_tiles,)),
@@ -1118,7 +1134,7 @@
             dma((n_copies,)),
         ],
         compiler_params=pltpu.CompilerParams(
-            collective_id=0, has_side_effects=True, vmem_limit_bytes=60 << 20
+            collective_id=0, has_side_effects=True, vmem_limit_bytes=62 << 20
         ),
     )(*args)
 

time: 135 us -> 130 us (0.963)
  Pallas kernels: 134 us -> 129 us
    pallas_call x1, Pallas kernels: 128 us -> 123 us  [run_main(): pl.pallas_call(functools.partial(main_kernel, (n_mp, n_dp, total_rows, hi...]
where the time goes in v5:
time: 130 us
  Pallas kernels  129 us (99%)
    pallas_call x1, Pallas kernels, run_main(): pl.pallas_call(functools.partial(main_kernel, (n_mp, n_dp, total_rows, hi...  123 us
    pallas_call x1, Pallas kernels, run_finish(): pl.pallas_call(functools.partial(finish_kernel, total_rows=total_rows, la...  5.66 us

profile of v5, /device:TPU:0, one launch (start us, length us, event | category | flops | bytes accessed | tf_op | source)
XLA Modules:
  0.0 129.9 jit_solution(13115862464111095495)
XLA Ops:
  0.7 123.5 %shard_map.315 = (bf16[8192,128]{1,0:T(8,128)(2,1)}, bf16[8192,128]{1,0:T(8,128)(2,1)}, bf16[1152,256]{1,0:T(8,128)(2,1)}, bf16[768,256]{1,0:T(8,128)(2,1)}, f32[8,512]{1,0:T(8,128)}) custom-call(bf16[8192,512]{1,0:T(8,128)(2,1)} %latent_in.1, bf16[8192,128]{1,0:T(8,128)(2,1)} %next_in.1, bf16[614,256]{1,0:T(8,128)(2,1)} %dyn_w1.1, bf16[614,256]{1,0:T(8,128)(2,1)} %rew_w1.1, ...), custom_call_target="tpu_custom_call" | custom-call | tf_op jit(solution)/shard_map/pallas_call | solution.py:1058
  124.1 5.7 %shard_map.316 = (bf16[8192,128]{1,0:T(8,128)(2,1)}, bf16[8192,128]{1,0:T(8,128)(2,1)}, f32[1,2]{1,0:T(1,128)}, f32[80,96]{1,0:T(8,128)}, f32[614,256]{1,0:T(8,1...) custom-call(bf16[8192,128]{1,0:T(8,128)(2,1)} %get-tuple-element.37., ...), custom_call_target="tpu_custom_call" | custom-call | tf_op jit(solution)/shard_map/pallas_call | solution.py:1013

commit v6 on v5

--- a/solution.py
+++ b/solution.py
@@ -15,9 +15,11 @@
 TILE = 512
 SUB = 128
 PART = 64
-LATE = 1
+LATE = 2
 PIECES = 2
-EVENTS = ((-1, 6, 10, 13, 99, 99), (0, 5, 9, 12, 15, 99), (0, 4, 9, 11, 13, 99))
+DYN_KINDS = (0, 1, 0)
+REW_KINDS = (0, 1, 0)
+EVENTS = ((-1, 4, 9, 13, 99), (0, 6, 10, 14, 99), (0, 7, 11, 99, 99))
 MESH = pl.DeviceIdType.MESH
 F32 = jnp.float32
 BF16 = jnp.bfloat16
@@ -217,6 +219,8 @@
         pl.semaphore_signal(
             barrier, inc=1, device_id={"mp": peer_of(flip)}, device_id_type=MESH
         )
+    aslant = {"mp": peer_of(2), "dp": column_peer(1)}
+    pl.semaphore_signal(barrier, inc=1, device_id=aslant, device_id_type=MESH)
     masks = sorted({mask for group in groups for mask in group_masks(group)})
     for mask in masks:
         pl.semaphore_signal(
@@ -291,7 +295,7 @@
     ]
     for copy in loads:
         copy.start()
-    pl.semaphore_wait(barrier, 3 + len(masks))
+    pl.semaphore_wait(barrier, 4 + len(masks))
     for index in w_needs[0] + w_needs[1]:
         weight_copy(index, 1).start()
         weight_copy(index, 0).start()
@@ -542,26 +546,6 @@
         local.start()
         remote.start()
 
-    gathered(w_needs[0][3:])
-    with_gain(w2_t, w2_g, 0)
-    loads[3].wait()
-    next_copy(1).wait_recv()
-
-    @pl.loop(0, n_tiles)
-    def _(tile):
-        cols = aligned(tile * TILE, TILE)
-        forward(0, aligned(own_rows + tile * TILE, TILE), True)
-        simnorm(1, tile, dpl, pair * chip_cols, tile * TILE)
-        local, remote = lat_copies(1, tile)
-        local.start()
-        remote.start()
-        dpl_copy(tile).wait_recv()
-        d_lat = dpl[:, cols]
-        g2t[...] += dot(d_lat, hid[...])
-        dh[...] = dot(d_lat, w2_g[...], 0, 0)
-        backward(0, d_dyn, tile * TILE)
-        g1[:, pl.ds(0, hid_width)] += dot(x_t[:, cols], d_dyn[cols, :])
-
     def add_into(target, others, n_rows):
         step_rows = next(size for size in (128, 96, 80, 64, 48, 32, 16) if n_rows % size == 0)
 
@@ -604,6 +588,28 @@
                 copies = [(source, target, {"mp": across})]
                 stages.append((copies, adds(rows, [where], length), None, pair))
                 spot += length
+                continue
+            if what == "cross":
+                both = False
+                length //= 2
+                keep_at = offset + place_in(groups[0], 0) * length
+                other_at = offset + place_in(groups[0], 1) * length
+                copies, wheres = [], []
+                for side, at, device in (
+                    (1 - pair, other_at, aslant),
+                    (1 - pair, keep_at, {"mp": across}),
+                    (pair, other_at, {"dp": column_peer(1)}),
+                ):
+                    where = pl.ds(spot, length)
+                    spot += length
+                    source, target = sides(aligned_to(at, length), where, side)
+                    copies.append((source, target, device))
+                    wheres.append(where)
+                keep = aligned_to(keep_at, length)
+                here = 2 * pair + place_in(groups[0], 0)
+                stages.append((copies, adds(keep, wheres, length), None, here))
+                gathers.append((groups[0], keep_at, length))
+                offset = keep_at
                 continue
             if length % (16 << len(what)) == 0:
                 parts = [what]
@@ -715,28 +721,55 @@
             g1[pl.ds(lat_width + n_task + 8 + line, 1), cols] = total / vecs[pl.ds(1, 1), cols]
 
     def order_of(kind):
-        if kind == 0:
-            return ["near", "across"] + groups
-        if kind == 1 or len(groups) < 2:
+        if kind == 0 or len(groups) < 2:
+            return ["near", "cross"] + groups[1:]
+        if kind == 1:
+            return ["near", groups[1], "cross"] + groups[2:]
+        if kind == 2:
             return ["near"] + groups[:1] + ["across"] + groups[1:]
-        return ["near", groups[1], "across", groups[0]] + groups[2:]
+        return ["near", "across"] + groups
 
     split = part_b.shape[2]
-    add_columns(0)
-    fill(part_a, 0, 0, lat_width, g2t, 0)
-    fill(part_b, 0, 0, split, g1, 0)
-    fill(part_c, 0, 0, in_rows - split, g1, split)
     dyn_places = (
         (part_a, got_a, in_rows, lat_width),
         (part_b, got_b, 0, split),
         (part_c, got_c, split, in_rows - split),
     )
     chunks = [
-        reduction(k, part, got, fin_dyn.at[pl.ds(first, count), :], order_of(k), False)
+        reduction(k, part, got, fin_dyn.at[pl.ds(first, count), :], order_of(DYN_KINDS[k]), False)
         for k, (part, got, first, count) in enumerate(dyn_places)
     ]
-    for chunk in chunks:
-        chunk[0](0)
+    gathered(w_needs[0][3:])
+    with_gain(w2_t, w2_g, 0)
+    loads[3].wait()
+    next_copy(1).wait_recv()
+
+    @pl.loop(0, n_tiles)
+    def _(tile):
+        cols = aligned(tile * TILE, TILE)
+        forward(0, aligned(own_rows + tile * TILE, TILE), True)
+        simnorm(1, tile, dpl, pair * chip_cols, tile * TILE)
+        local, remote = lat_copies(1, tile)
+        local.start()
+        remote.start()
+        dpl_copy(tile).wait_recv()
+        d_lat = dpl[:, cols]
+        g2t[...] += dot(d_lat, hid[...])
+
+        @pl.when(tile == n_tiles - 1)
+        def _():
+            fill(part_a, 0, 0, lat_width, g2t, 0)
+            chunks[0][0](0)
+
+        dh[...] = dot(d_lat, w2_g[...], 0, 0)
+        backward(0, d_dyn, tile * TILE)
+        g1[:, pl.ds(0, hid_width)] += dot(x_t[:, cols], d_dyn[cols, :])
+
+    fill(part_b, 0, 0, split, g1, 0)
+    chunks[1][0](0)
+    add_columns(0)
+    fill(part_c, 0, 0, in_rows - split, g1, split)
+    chunks[2][0](0)
     per_tile = 4
     inside = sorted(
         (place, chunk, index)
@@ -831,7 +864,7 @@
                 part_rew.at[k],
                 got_rew.at[k],
                 fin_rew.at[pl.ds(k * third, third), :],
-                order_of(k),
+                order_of(REW_KINDS[k]),
                 k == 2,
             )
         )
@@ -1052,7 +1085,7 @@
     shape = jax.ShapeDtypeStruct
     dma = pltpu.SemaphoreType.DMA
     n_bits = n_dp.bit_length() - 1
-    n_copies = 2 + 2 * sum(len(flips(group)) for group in column_groups(n_bits))
+    n_copies = 4 + 2 * sum(len(flips(group)) for group in column_groups(n_bits))
     third = (in_rows + LANES) // 3
     split = 3 * in_rows // 5
     return pl.pallas_call(

time: 130 us -> 127 us (0.977)
  Pallas kernels: 129 us -> 126 us
    pallas_call x1, Pallas kernels: 123 us -> 121 us  [run_main(): pl.pallas_call(functools.partial(main_kernel, (n_mp, n_dp, total_rows, hi...]
where the time goes in v6:
time: 127 us
  Pallas kernels  126 us (99%)
    pallas_call x1, Pallas kernels, run_main(): pl.pallas_call(functools.partial(main_kernel, (n_mp, n_dp, total_rows, hi...  121 us
    pallas_call x1, Pallas kernels, run_finish(): pl.pallas_call(functools.partial(finish_kernel, total_rows=total_rows, la...  5.66 us

profile of v6, /device:TPU:0, one launch (start us, length us, event | category | flops | bytes accessed | tf_op | source)
XLA Modules:
  0.0 127.0 jit_solution(15704723162200855590)
XLA Ops:
  0.7 120.5 %shard_map.315 = (bf16[8192,128]{1,0:T(8,128)(2,1)}, bf16[8192,128]{1,0:T(8,128)(2,1)}, bf16[1152,256]{1,0:T(8,128)(2,1)}, bf16[768,256]{1,0:T(8,128)(2,1)}, f32[8,512]{1,0:T(8,128)}) custom-call(bf16[8192,512]{1,0:T(8,128)(2,1)} %latent_in.1, bf16[8192,128]{1,0:T(8,128)(2,1)} %next_in.1, bf16[614,256]{1,0:T(8,128)(2,1)} %dyn_w1.1, bf16[614,256]{1,0:T(8,128)(2,1)} %rew_w1.1, ...), custom_call_target="tpu_custom_call" | custom-call | tf_op jit(solution)/shard_map/pallas_call | solution.py:1091
  121.2 5.7 %shard_map.316 = (bf16[8192,128]{1,0:T(8,128)(2,1)}, bf16[8192,128]{1,0:T(8,128)(2,1)}, f32[1,2]{1,0:T(1,128)}, f32[80,96]{1,0:T(8,128)}, f32[614,256]{1,0:T(8,1...) custom-call(bf16[8192,128]{1,0:T(8,128)(2,1)} %get-tuple-element.37., ...), custom_call_target="tpu_custom_call" | custom-call | tf_op jit(solution)/shard_map/pallas_call | solution.py:1046

commit v7 on v6

--- a/solution.py
+++ b/solution.py
@@ -143,7 +143,7 @@
     hid,
     d_pre,
     zt,
-    latt,
+    next_t,
     dlog,
     inv_ref,
     col_acc,
@@ -296,11 +296,11 @@
     for copy in loads:
         copy.start()
     pl.semaphore_wait(barrier, 4 + len(masks))
+    next_copy(0).start()
+    next_copy(1).start()
     for index in w_needs[0] + w_needs[1]:
         weight_copy(index, 1).start()
         weight_copy(index, 0).start()
-    next_copy(0).start()
-    next_copy(1).start()
 
     for ref in (g1, g2t, rg2t, col_acc, sum_acc, row_acc, b2_acc):
         ref[...] = jnp.zeros_like(ref)
@@ -455,9 +455,6 @@
     def simnorm(slot, tile, target, row, col):
         rows = aligned(tile * TILE, TILE)
         zt[...] = dot(w2_t[aligned(pair * chip_cols, chip_cols), :], hid[...], 1, 1)
-        for side in range(2):
-            latt[pl.ds(side * share, share), :] = next_lat[slot, side, rows, :].T.astype(F32)
-
         @pl.loop(0, chip_cols // PART)
         def _(step):
             part = aligned(step * PART, PART)
@@ -467,7 +464,8 @@
                 z = (zt[part, lanes] + bias).reshape(PART // GROUP, GROUP, LANES)
                 e = jnp.exp(z - jnp.max(z, axis=1, keepdims=True))
                 s = e * (1.0 / jnp.sum(e, axis=1, keepdims=True))
-                error = s - latt[part, lanes].reshape(z.shape)
+                wanted = next_t[slot, part, aligned(tile * TILE + lane * LANES, LANES)]
+                error = s - wanted.astype(F32).reshape(z.shape)
                 sum_acc[pl.ds(0, 8), :] += jnp.sum(error * error, axis=0)
                 d_lat = d_scale * error
                 d_z = s * (d_lat - jnp.sum(s * d_lat, axis=1, keepdims=True))
@@ -528,9 +526,17 @@
         local = pltpu.make_async_copy(lg_stage.at[mine, rows, :], out_rows, g_local.at[tile])
         return local, remotes
 
+    for slot in range(2):
+        loads[2 + slot].wait()
+        next_copy(slot).wait_recv()
+
+        @pl.loop(0, n_tiles)
+        def _(tile):
+            rows = aligned(tile * TILE, TILE)
+            for side in range(2):
+                next_t[slot, pl.ds(side * share, share), rows] = next_lat[slot, side, rows, :].T
+
     prepare(0)
-    loads[2].wait()
-    next_copy(0).wait_recv()
 
     @pl.loop(0, n_tiles)
     def _(tile):
@@ -741,8 +747,6 @@
     ]
     gathered(w_needs[0][3:])
     with_gain(w2_t, w2_g, 0)
-    loads[3].wait()
-    next_copy(1).wait_recv()
 
     @pl.loop(0, n_tiles)
     def _(tile):
@@ -1141,7 +1145,7 @@
             pltpu.VMEM((TILE, hid_width), BF16),
             pltpu.VMEM(((LATE + 1) * TILE, hid_width), BF16),
             pltpu.VMEM((2 * share, TILE), F32),
-            pltpu.VMEM((2 * share, TILE), F32),
+            pltpu.VMEM((2, 2 * share, own), BF16),
             pltpu.VMEM((LANES, TILE), BF16),
             pltpu.VMEM((TILE, LANES), F32),
             pltpu.VMEM((16, 2 * hid_width), F32),

time: 127 us -> 127 us (level)
  no operation moved by 1% of the time
where the time goes in v7:
time: 127 us
  Pallas kernels  126 us (99%)
    pallas_call x1, Pallas kernels, run_main(): pl.pallas_call(functools.partial(main_kernel, (n_mp, n_dp, total_rows, hi...  121 us
    pallas_call x1, Pallas kernels, run_finish(): pl.pallas_call(functools.partial(finish_kernel, total_rows=total_rows, la...  5.66 us

profile of v7, /device:TPU:0, one launch (start us, length us, event | category | flops | bytes accessed | tf_op | source)
XLA Modules:
  0.0 127.3 jit_solution(6945059800757426382)
XLA Ops:
  0.7 120.8 %shard_map.315 = (bf16[8192,128]{1,0:T(8,128)(2,1)}, bf16[8192,128]{1,0:T(8,128)(2,1)}, bf16[1152,256]{1,0:T(8,128)(2,1)}, bf16[768,256]{1,0:T(8,128)(2,1)}, f32[8,512]{1,0:T(8,128)}) custom-call(bf16[8192,512]{1,0:T(8,128)(2,1)} %latent_in.1, bf16[8192,128]{1,0:T(8,128)(2,1)} %next_in.1, bf16[614,256]{1,0:T(8,128)(2,1)} %dyn_w1.1, bf16[614,256]{1,0:T(8,128)(2,1)} %rew_w1.1, ...), custom_call_target="tpu_custom_call" | custom-call | tf_op jit(solution)/shard_map/pallas_call | solution.py:1095
  121.4 5.7 %shard_map.316 = (bf16[8192,128]{1,0:T(8,128)(2,1)}, bf16[8192,128]{1,0:T(8,128)(2,1)}, f32[1,2]{1,0:T(1,128)}, f32[80,96]{1,0:T(8,128)}, f32[614,256]{1,0:T(8,1...) custom-call(bf16[8192,128]{1,0:T(8,128)(2,1)} %get-tuple-element.37., ...), custom_call_target="tpu_custom_call" | custom-call | tf_op jit(solution)/shard_map/pallas_call | solution.py:1050
